TPU v7x, 256 devices: a whole 4x4x8 slice. The times are simulated.
256 devices in a mesh: slab: 64 (over y, z, core), plane: 4 (over x).
Axes of the slice: x: 4, y: 4, z: 8, core: 2. Of those that a mesh axis runs over, the one named last changes fastest.
Arguments:
- a_blocks: bfloat16 [4, 768, 7, 128, 128], P('plane', 'slab'), may hold values from -0.1875 to 0.1875
- a_cols: int32 [4, 768, 7], P('plane', 'slab'), may hold values from 0 to 767, as said below
- p_blocks: bfloat16 [4, 768, 4, 128, 128], P('plane', 'slab'), may hold values from -0.75 to 0.75
- p_cols: int32 [4, 768, 4], replicated, may hold values from 0 to 255, as said below
- coarse_slot: int32 [64, 4], replicated, may hold values from 0 to 3, each once within a row
Outputs:
- coarse_op: float32 [4, 64, 128, 2560], P('plane', 'slab')
Inputs may be any that keep to these rules, and one draw needn't show every extreme that they name: `a_cols`: row g = s*12 + r of column p names 7 distinct block rows of column p, among them g itself; they lie in s*12 to s*12 + 11, or, if r < 4, in the 4 rows just below s*12, or, if r >= 8, in the 4 rows from (s+1)*12 on. `p_cols`: row g = s*12 + r names 4 distinct coarse blocks of s*4 to s*4 + 3, or, if r < 4, also of the 4 blocks before, or, if r >= 8, of the 4 blocks after. `coarse_slot`: each row is a permutation of 0 to 3.
All inputs are finite; a program needn't handle non-finite values.
Results may differ from a plain program's by a relative error of at most 0.0029.
Values may be sent and summed in bfloat16 or wider, within the bound.
No kernel may reach another device: no remote copies, remote signals or barrier semaphores. Data moves between devices by JAX's collectives and lax.ppermute only.
A program may use at most 192 MiB of HBM per device.

v0:
```python
import jax
import jax.numpy as jnp
from jax import lax
from jax.sharding import PartitionSpec as P

GHOST = 4


def with_halo(shard, sides, width):
    for axis, dim in sides:
        count, length = (lax.axis_size(axis), shard.shape[dim])
        up = [(i, (i + 1) % count) for i in range(count - 1)]
        down = [(j, i) for i, j in up]
        last = lax.slice_in_dim(shard, length - width, length, axis=dim)
        leading = lax.slice_in_dim(shard, 0, width, axis=dim)
        before = lax.ppermute(last, axis, up)
        after = lax.ppermute(leading, axis, down)
        shard = jnp.concatenate([before, shard, after], axis=dim)
    return shard


def passed_along(shard, axis, by):
    count = lax.axis_size(axis)
    pairs = [(i, i + by) for i in range(count) if 0 <= i + by < count]
    return lax.ppermute(shard, axis, pairs)


def cut_along(shard, dim, count):
    lengths = shard.shape
    tiles = shard.reshape(*lengths[:dim], count, lengths[dim] // count, *lengths[dim + 1 :])
    return jnp.moveaxis(tiles, dim, 0)


def sent_and_summed(shard, axis, dim):
    count = lax.axis_size(axis)
    tiles = lax.all_to_all(cut_along(shard, dim, count), axis, 0, 0, tiled=True)
    return jnp.sum(tiles, axis=0)


def window_rows(blocks, cols, nearby, slab, coarse):
    count = blocks.shape[0]
    block = blocks.shape[2]
    relative = cols - (slab - 1) * coarse
    choose = (
        relative[:, :, None] == jnp.arange(3 * coarse, dtype=jnp.int32)[None, None, :]
    ).astype(jnp.int32)
    slot = jnp.sum(choose * nearby[None, None, :], axis=-1)
    place = relative // coarse * coarse + slot
    onehot = (place[:, :, None] == jnp.arange(3 * coarse, dtype=jnp.int32)[None, None, :]).astype(
        jnp.bfloat16
    )
    dense = jnp.einsum("nkw,nkab->nawb", onehot, blocks, preferred_element_type=jnp.float32)
    return dense.reshape(count, block, 3 * coarse * block).astype(jnp.bfloat16)


def on_device(a_blocks, a_cols, p_blocks, p_cols, coarse_slot):
    rows_here = a_blocks.shape[1]
    links = a_blocks.shape[2]
    block = a_blocks.shape[3]
    coarse = coarse_slot.shape[1]
    owned = coarse // lax.axis_size("plane")
    width = 3 * coarse * block
    slab = lax.axis_index("slab")
    column = lax.axis_index("plane")
    start = slab * rows_here
    ghosted = with_halo(p_blocks, (("slab", 1),), GHOST)[0]
    mine = lax.dynamic_slice_in_dim(p_cols, column, 1, 0)[0]
    mine = jnp.pad(mine, ((GHOST, GHOST), (0, 0)))
    near_cols = lax.dynamic_slice_in_dim(mine, start, rows_here + 2 * GHOST, 0)
    padded_slots = jnp.pad(coarse_slot, ((1, 1), (0, 0)))
    nearby = lax.dynamic_slice_in_dim(padded_slots, slab, 3, 0).reshape(-1)
    dense = window_rows(ghosted, near_cols, nearby, slab, coarse)
    local = a_cols[0] - (start - GHOST)
    total = jnp.zeros((rows_here, block, width), jnp.float32)
    for k in range(links):
        picked = jnp.take(dense, local[:, k], axis=0)
        total = total + jnp.einsum(
            "rab,rbw->raw", a_blocks[0, :, k], picked, preferred_element_type=jnp.float32
        )
    product = total.astype(jnp.bfloat16)
    own_rows = dense[GHOST : GHOST + rows_here].reshape(-1, width)
    partial_value = lax.dot_general(
        own_rows,
        product.reshape(-1, width),
        (((0,), (0,)), ((), ())),
        preferred_element_type=jnp.float32,
    )
    edge = coarse * block
    groups = partial_value.reshape(3, coarse * block, width)
    from_below = passed_along(groups[2], "slab", 1)
    from_above = passed_along(groups[0], "slab", -1)
    full = jnp.pad(groups[1], ((0, 0), (edge, edge)))
    full = full + jnp.pad(from_below, ((0, 0), (0, 2 * edge)))
    full = full + jnp.pad(from_above, ((0, 0), (2 * edge, 0)))
    full = full.reshape(coarse, block, 5 * coarse * block)
    result = sent_and_summed(full, "plane", 0)
    return result.reshape(1, owned, block, 5 * coarse * block)


def solution(mesh):
    return jax.shard_map(
        on_device,
        mesh=mesh,
        in_specs=(
            P("plane", "slab", None, None, None),
            P("plane", "slab", None),
            P("plane", "slab", None, None, None),
            P(),
            P(),
        ),
        out_specs=P("plane", "slab", None, None),
        check_vma=False,
    )
```

profile of v0, /device:TPU:113, one launch (start us, length us, event | category | flops | bytes accessed | tf_op | source)
XLA Modules:
  0.0 272.3 jit_solution(2656482572807901838)
XLA Ops:
  0.0 0.0 copy-start
  0.0 2.7 copy.47
  2.7 0.4 fusion.70
  3.0 5.3 %collective-permute-start = (bf16[1,4,4,128,128]{4,2,3,1,0:T(4,128)(2,1)S(1)}, bf16[1,4,4,128,128]{4,2,3,1,0:T(4,128)(2,1)S(1)}, u32[]{:S(2)}, u32[]{:S(2)}) collective-permute-start(bf16[1,4,4,128,128]{4,2,3,1,0:T(4,128)(2,1)S(1)} %get-tuple-element.23), channel_id=1, source_target_pairs={{0,4},{4,8},{8,12},{12,16},{16,20},{20,24},{24,28},{28,32},{32,36}... | collective-permute-start | bytes 1572872 | tf_op jit(solution)/shard_map/ppermute | solution.py:16
  8.4 1.9 collective-permute-start.1
  10.3 0.0 copy-done.5
  10.3 0.1 pad_dynamic-slice_fusion.1
  10.4 0.1 copy.50
  10.5 0.1 mul.23
  10.6 0.1 fusion.58
  10.7 0.1 select_reduce_fusion
  10.8 0.1 fusion.57
  10.9 0.1 copy.51
  11.1 3.4 %collective-permute-done = bf16[1,4,4,128,128]{4,2,3,1,0:T(4,128)(2,1)S(1)} collective-permute-done((bf16[1,4,4,128,128]{4,2,3,1,0:T(4,128)(2,1)S(1)}, bf16[1,4,4,128,128]{4,2,3,1,0:T(4,128)(2,1)S(1)}, u32[]{:S(2)}, u32[]{:S(2)}) %collective-permute-start) | collective-permute-done | bytes 524320 | tf_op jit(solution)/shard_map/ppermute | solution.py:16
  14.5 5.7 %collective-permute-done.1 = bf16[1,4,4,128,128]{4,2,3,1,0:T(4,128)(2,1)} collective-permute-done((bf16[1,4,4,128,128]{4,2,3,1,0:T(4,128)(2,1)S(1)}, bf16[1,4,4,128,128]{4,2,3,1,0:T(4,128)(2,1)}, u32[]{:S(2)}, u32[]{:S(2)}) %collective-permute-start.1) | collective-permute-done | bytes 524320 | tf_op jit(solution)/shard_map/ppermute | solution.py:17
  20.2 4.0 %convert_bitcast_fusion = bf16[20,128,12,128]{3,2,1,0:T(8,128)(2,1)S(1)} fusion(bf16[1,4,4,128,128]{4,2,3,1,0:T(4,128)(2,1)} %collective-permute-done.1, bf16[1,12,4,128,128]{4,2,3,1,0:T(4,128)(2,1)S(1)} %copy.47, bf16[1,4,4,128,128]{4,2,3,1,0:T(4,128)(2,1)S(1)} %collective-permute-done, s32[20,4]{1,0:T(8,128)S(1)} %copy.51), kind=kOutput, calls=%fused_computation.7 | convolution fusion | flops 43254720 | bytes 10486080 | tf_op jit(solution)/shard_map/nkw,nkab->nawb/dot_general | solution.py:52
  24.3 4.0 %copy-done.2 = bf16[20,128,12,128]{3,2,1,0:T(8,128)(2,1)} copy-done((bf16[20,128,12,128]{3,2,1,0:T(8,128)(2,1)}, bf16[20,128,12,128]{3,2,1,0:T(8,128)(2,1)S(1)}, u32[]{:S(2)}) %copy-start.2) | copy-done | bytes 7864344
  28.3 3.7 %slice.103 = bf16[12,128,12,128]{3,2,1,0:T(8,128)(2,1)} slice(bf16[20,128,12,128]{3,2,1,0:T(8,128)(2,1)S(1)} %convert_bitcast_fusion), slice={[4:16], [0:128], [0:12], [0:128]} | slice | bytes 9437184 | tf_op jit(solution)/shard_map/slice | solution.py:81
  31.9 14.1 %copy.54 = bf16[20,128,12,128]{1,3,2,0:T(8,128)(2,1)} copy(bf16[20,128,12,128]{3,2,1,0:T(8,128)(2,1)} %copy-done.2) | data formatting | bytes 15728640 | tf_op jit(solution)/shard_map/convert_element_type | solution.py:53
  46.0 8.6 %copy.52 = bf16[12,128,12,128]{1,3,2,0:T(8,128)(2,1)} copy(bf16[12,128,12,128]{3,2,1,0:T(8,128)(2,1)} %slice.103) | data formatting | bytes 9437184 | tf_op jit(solution)/shard_map/slice | solution.py:81
  54.6 6.7 %gather_fusion.6 = bf16[12,128,1536]{1,2,0:T(8,128)(2,1)} fusion(bf16[20,128,1536]{1,2,0:T(8,128)(2,1)} %bitcast.83, s32[1024]{0:T(1024)S(1)} %get-tuple-element.37), kind=kCustom, calls=%fused_computation.6.clone | custom fusion | bytes 9437232 | tf_op jit(solution)/shard_map/jit(_take)/gather | solution.py:76
  61.3 6.6 %gather_fusion.5 = bf16[12,128,1536]{1,2,0:T(8,128)(2,1)} fusion(bf16[20,128,1536]{1,2,0:T(8,128)(2,1)} %bitcast.84, s32[1024]{0:T(1024)S(1)} %get-tuple-element.38), kind=kCustom, calls=%fused_computation.5.clone | custom fusion | bytes 9437232 | tf_op jit(solution)/shard_map/jit(_take)/gather | solution.py:76
  67.9 6.7 %gather_fusion.4 = bf16[12,128,1536]{1,2,0:T(8,128)(2,1)} fusion(bf16[20,128,1536]{1,2,0:T(8,128)(2,1)} %bitcast.85, s32[1024]{0:T(1024)S(1)} %get-tuple-element.39), kind=kCustom, calls=%fused_computation.4.clone | custom fusion | bytes 9437232 | tf_op jit(solution)/shard_map/jit(_take)/gather | solution.py:76
  74.6 6.8 %gather_fusion.3 = bf16[12,128,1536]{1,2,0:T(8,128)(2,1)} fusion(bf16[20,128,1536]{1,2,0:T(8,128)(2,1)} %bitcast.86, s32[1024]{0:T(1024)S(1)} %get-tuple-element.40), kind=kCustom, calls=%fused_computation.3.clone | custom fusion | bytes 9437232 | tf_op jit(solution)/shard_map/jit(_take)/gather | solution.py:76
  81.3 6.7 %gather_fusion.2 = bf16[12,128,1536]{1,2,0:T(8,128)(2,1)} fusion(bf16[20,128,1536]{1,2,0:T(8,128)(2,1)} %bitcast.87, s32[1024]{0:T(1024)S(1)} %get-tuple-element.41), kind=kCustom, calls=%fused_computation.2.clone | custom fusion | bytes 9437232 | tf_op jit(solution)/shard_map/jit(_take)/gather | solution.py:76
  88.0 6.7 %gather_fusion.1 = bf16[12,128,1536]{1,2,0:T(8,128)(2,1)} fusion(bf16[20,128,1536]{1,2,0:T(8,128)(2,1)} %bitcast.88, s32[1024]{0:T(1024)S(1)} %get-tuple-element.42), kind=kCustom, calls=%fused_computation.1.clone | custom fusion | bytes 9437232 | tf_op jit(solution)/shard_map/jit(_take)/gather | solution.py:76
  94.7 6.8 %gather_fusion = bf16[12,128,1536]{1,2,0:T(8,128)(2,1)} fusion(bf16[20,128,1536]{1,2,0:T(8,128)(2,1)} %bitcast.89, s32[1024]{0:T(1024)S(1)} %pad_clamp_fusion.6), kind=kCustom, calls=%fused_computation.clone | custom fusion | bytes 9437232 | tf_op jit(solution)/shard_map/jit(_take)/gather | solution.py:76
  101.5 7.6 %fusion.13 = f32[12,1536,128]{2,1,0:T(8,128)} fusion(bf16[12,128,1536]{1,2,0:T(8,128)(2,1)} %gather_fusion, pred[12]{0:T(512)(128)(4,1)S(1)} %get-tuple-element.35, bf16[1,12,7,128,128]{4,3,2,1,0:T(8,128)(2,1)S(1)} %copy-done.3), kind=kOutput, calls=%fused_computation.23 | convolution fusion | flops 606339072 | bytes 14549504 | tf_op jit(solution)/shard_map/rab,rbw->raw/dot_general | solution.py:77
  109.1 0.0 slice-start.4
  109.1 4.5 %fusion.11 = f32[12,1536,128]{2,1,0:T(8,128)} fusion(bf16[12,128,1536]{1,2,0:T(8,128)(2,1)S(1)} %bitcast.100, pred[12]{0:T(512)(128)(4,1)S(1)} %get-tuple-element.33, bf16[1,12,7,128,128]{4,3,2,1,0:T(8,128)(2,1)S(1)} %copy-done.3), kind=kOutput, calls=%fused_computation.21 | convolution fusion | flops 606339072 | bytes 14549504 | tf_op jit(solution)/shard_map/rab,rbw->raw/dot_general | solution.py:77
  113.6 0.0 slice-start.2
  113.6 4.7 %fusion.9 = f32[12,1536,128]{2,1,0:T(8,128)} fusion(bf16[12,128,1536]{1,2,0:T(8,128)(2,1)S(1)} %bitcast.98, pred[12]{0:T(512)(128)(4,1)S(1)} %get-tuple-element.31, bf16[1,12,7,128,128]{4,3,2,1,0:T(8,128)(2,1)S(1)} %copy-done.3), kind=kOutput, calls=%fused_computation.19 | convolution fusion | flops 606339072 | bytes 14549504 | tf_op jit(solution)/shard_map/rab,rbw->raw/dot_general | solution.py:77
  118.3 0.0 slice-start
  118.4 4.5 %fusion.7 = f32[12,1536,128]{2,1,0:T(8,128)} fusion(bf16[12,128,1536]{1,2,0:T(8,128)(2,1)S(1)} %bitcast.96, pred[12]{0:T(512)(128)(4,1)S(1)} %get-tuple-element.29, bf16[1,12,7,128,128]{4,3,2,1,0:T(8,128)(2,1)S(1)} %copy-done.3), kind=kOutput, calls=%fused_computation.17 | convolution fusion | flops 606339072 | bytes 14549504 | tf_op jit(solution)/shard_map/rab,rbw->raw/dot_general | solution.py:77
  122.9 4.5 %fusion.5 = f32[12,1536,128]{2,1,0:T(8,128)} fusion(bf16[12,128,1536]{1,2,0:T(8,128)(2,1)S(1)} %bitcast.94, pred[12]{0:T(512)(128)(4,1)S(1)} %get-tuple-element.27, bf16[1,12,7,128,128]{4,3,2,1,0:T(8,128)(2,1)S(1)} %copy-done.3), kind=kOutput, calls=%fused_computation.15 | convolution fusion | flops 606339072 | bytes 14549504 | tf_op jit(solution)/shard_map/rab,rbw->raw/dot_general | solution.py:77
  127.4 0.0 slice-done
  127.4 4.4 %fusion.3 = f32[12,1536,128]{2,1,0:T(8,128)} fusion(bf16[12,128,1536]{1,2,0:T(8,128)(2,1)S(1)} %bitcast.92, pred[12]{0:T(512)(128)(4,1)S(1)} %get-tuple-element.25, bf16[1,12,7,128,128]{4,3,2,1,0:T(8,128)(2,1)S(1)} %copy-done.3), kind=kOutput, calls=%fused_computation.13 | convolution fusion | flops 606339072 | bytes 14549504 | tf_op jit(solution)/shard_map/rab,rbw->raw/dot_general | solution.py:77
  131.7 27.6 %convolution_bitcast_fusion = f32[1536,1536]{1,0:T(8,128)} fusion(bf16[12,128,1536]{1,2,0:T(8,128)(2,1)} %bitcast.101, f32[12,1536,128]{2,1,0:T(8,128)} %fusion.3, f32[12,1536,128]{2,1,0:T(8,128)} %fusion.5, f32[12,1536,128]{2,1,0:T(8,128)} %fusion.7, f32[12,1536,128]{2,1,0:T(8,128)} %fusion.9, f32[12,1536,128]{2,1,0:T(8,128)} %fusion.13, ...), kind=kOutput, calls=%fused_computation.9 | convolution fusion | flops 7870611456 | bytes 75891200 | tf_op jit(solution)/shard_map/dot_general | solution.py:82
  159.4 4.6 %fusion.69 = (f32[512,1536]{1,0:T(8,128)S(1)}, f32[512,1536]{1,0:T(8,128)S(1)}, f32[512,1536]{1,0:T(8,128)S(1)}) fusion(f32[1536,1536]{1,0:T(8,128)} %convolution_bitcast_fusion), kind=kLoop, calls=%fused_computation.107 | loop fusion | bytes 18874368 | tf_op jit(solution)/shard_map/slice | solution.py:92
  164.0 1.9 collective-permute-start.3
  165.9 4.9 %collective-permute-start.2 = (f32[512,1536]{1,0:T(8,128)S(1)}, f32[512,1536]{1,0:T(8,128)S(1)}, u32[]{:S(2)}, u32[]{:S(2)}) collective-permute-start(f32[512,1536]{1,0:T(8,128)S(1)} %get-tuple-element.22), channel_id=1, source_target_pairs={{0,4},{4,8},{8,12},{12,16},{16,20},{20,24},{24,28},{28,32},{32,36}... | collective-permute-start | bytes 9437192 | tf_op jit(solution)/shard_map/ppermute | solution.py:25
  170.8 33.0 %collective-permute-done.3 = f32[512,1536]{1,0:T(8,128)S(1)} collective-permute-done((f32[512,1536]{1,0:T(8,128)S(1)}, f32[512,1536]{1,0:T(8,128)S(1)}, u32[]{:S(2)}, u32[]{:S(2)}) %collective-permute-start.3) | collective-permute-done | bytes 3145760 | tf_op jit(solution)/shard_map/ppermute | solution.py:25
  203.8 1.2 collective-permute-done.2
  205.0 0.8 pad_add_fusion
  205.8 0.0 copy-start.1
  205.8 62.4 %all_to_all.5 = f32[4,1,128,2560]{3,2,1,0:T(8,128)} all-to-all(f32[4,1,128,2560]{3,2,1,0:T(8,128)S(1)} %bitcast.90), channel_id=1, replica_groups=mesh['slab'=64,'plane'=4] {'plane'}, dimensions={0} | all-to-all | bytes 10485760 | tf_op jit(solution)/shard_map/all_to_all | solution.py:36
  268.3 4.1 %reduce_sum.19 = f32[128,2560]{1,0:T(8,128)} reduce(f32[4,1,128,2560]{3,2,1,0:T(8,128)} %all_to_all.5, f32[]{:T(128)} %constant.51.clone.1), dimensions={0,1}, to_apply=%region_1.3 | reduce | flops 983040 | bytes 6553604 | tf_op jit(solution)/shard_map/reduce_sum | solution.py:37
  272.3 0.0 copy-done.1
  (35 shorter events, 0.1 us)
Async XLA Ops:
  0.0 10.6 %copy-start = (s32[4,768,4]{1,2,0:T(4,128)S(1)}, s32[4,768,4]{1,2,0:T(4,128)}, u32[]{:S(2)}) copy-start(s32[4,768,4]{1,2,0:T(4,128)} %param.10) | copy-start | bytes 147460
  0.0 10.3 %copy-start.5 = (s32[64,4]{0,1:T(4,128)S(1)}, s32[64,4]{0,1:T(4,128)}, u32[]{:S(2)}) copy-start(s32[64,4]{0,1:T(4,128)} %param.11) | copy-start | bytes 3076
  0.0 10.6 %copy-start.4 = (s32[1,12,7]{1,0,2:T(1,128)S(1)}, s32[1,12,7]{1,0,2:T(1,128)}, u32[]{:S(2)}) copy-start(s32[1,12,7]{1,0,2:T(1,128)} %param.8) | copy-start | bytes 1012
  3.0 11.4 %collective-permute-start = (bf16[1,4,4,128,128]{4,2,3,1,0:T(4,128)(2,1)S(1)}, bf16[1,4,4,128,128]{4,2,3,1,0:T(4,128)(2,1)S(1)}, u32[]{:S(2)}, u32[]{:S(2)}) collective-permute-start(bf16[1,4,4,128,128]{4,2,3,1,0:T(4,128)(2,1)S(1)} %get-tuple-element.23), channel_id=1, source_target_pairs={{0,4},{4,8},{8,12},{12,16},{16,20},{20,24},{24,28},{28,32},{32,36}... | collective-permute-start | bytes 1572872 | tf_op jit(solution)/shard_map/ppermute | solution.py:16
  8.4 11.8 %collective-permute-start.1 = (bf16[1,4,4,128,128]{4,2,3,1,0:T(4,128)(2,1)S(1)}, bf16[1,4,4,128,128]{4,2,3,1,0:T(4,128)(2,1)}, u32[]{:S(2)}, u32[]{:S(2)}) collective-permute-start(bf16[1,4,4,128,128]{4,2,3,1,0:T(4,128)(2,1)S(1)} %get-tuple-element.24), channel_id=1, source_target_pairs={{4,0},{8,4},{12,8},{16,12},{20,16},{24,20},{28,24},{32,28},{36,32}... | collective-permute-start | bytes 1572872 | tf_op jit(solution)/shard_map/ppermute | solution.py:17
  24.2 4.0 %copy-start.2 = (bf16[20,128,12,128]{3,2,1,0:T(8,128)(2,1)}, bf16[20,128,12,128]{3,2,1,0:T(8,128)(2,1)S(1)}, u32[]{:S(2)}) copy-start(bf16[20,128,12,128]{3,2,1,0:T(8,128)(2,1)S(1)} %convert_bitcast_fusion) | copy-start | bytes 23592964
  94.7 6.8 %copy-start.3 = (bf16[1,12,7,128,128]{4,3,2,1,0:T(8,128)(2,1)S(1)}, bf16[1,12,7,128,128]{4,3,2,1,0:T(8,128)(2,1)}, u32[]{:S(2)}) copy-start(bf16[1,12,7,128,128]{4,3,2,1,0:T(8,128)(2,1)} %param.7) | copy-start | bytes 8257540
  94.7 14.4 %slice-start.8 = ((s8[4718592]{0:T(1024)(128)(4,1)}), s8[524288]{0:T(1024)(128)(4,1)S(1)}, s32[]{:S(2)}) async-start(s8[4718592]{0:T(1024)(128)(4,1)} %bitcast.99), calls=%async_computation.9 | async-start | bytes 1048576
  101.5 7.6 %slice-start.9 = ((s8[4718592]{0:T(1024)(128)(4,1)}), s8[4194304]{0:T(1024)(128)(4,1)S(1)}, s32[]{:S(2)}) async-start(s8[4718592]{0:T(1024)(128)(4,1)} %bitcast.99), calls=%async_computation.10 | async-start | bytes 8388608
  101.5 12.1 %slice-start.6 = ((s8[4718592]{0:T(1024)(128)(4,1)}), s8[4194304]{0:T(1024)(128)(4,1)S(1)}, s32[]{:S(2)}) async-start(s8[4718592]{0:T(1024)(128)(4,1)} %bitcast.97), calls=%async_computation.7 | async-start | bytes 8388608
  109.1 4.5 %slice-start.7 = ((s8[4718592]{0:T(1024)(128)(4,1)}), s8[524288]{0:T(1024)(128)(4,1)S(1)}, s32[]{:S(2)}) async-start(s8[4718592]{0:T(1024)(128)(4,1)} %bitcast.97), calls=%async_computation.8 | async-start | bytes 1048576
  109.1 9.2 %slice-start.4 = ((s8[4718592]{0:T(1024)(128)(4,1)}), s8[4194304]{0:T(1024)(128)(4,1)S(1)}, s32[]{:S(2)}) async-start(s8[4718592]{0:T(1024)(128)(4,1)} %bitcast.95), calls=%async_computation.5 | async-start | bytes 8388608
  113.6 4.7 %slice-start.5 = ((s8[4718592]{0:T(1024)(128)(4,1)}), s8[524288]{0:T(1024)(128)(4,1)S(1)}, s32[]{:S(2)}) async-start(s8[4718592]{0:T(1024)(128)(4,1)} %bitcast.95), calls=%async_computation.6 | async-start | bytes 1048576
  113.6 9.2 %slice-start.2 = ((s8[4718592]{0:T(1024)(128)(4,1)}), s8[4194304]{0:T(1024)(128)(4,1)S(1)}, s32[]{:S(2)}) async-start(s8[4718592]{0:T(1024)(128)(4,1)} %bitcast.93), calls=%async_computation.3 | async-start | bytes 8388608
  118.3 4.5 %slice-start.3 = ((s8[4718592]{0:T(1024)(128)(4,1)}), s8[524288]{0:T(1024)(128)(4,1)S(1)}, s32[]{:S(2)}) async-start(s8[4718592]{0:T(1024)(128)(4,1)} %bitcast.93), calls=%async_computation.4 | async-start | bytes 1048576
  118.3 9.0 %slice-start = ((s8[4718592]{0:T(1024)(128)(4,1)}), s8[4194304]{0:T(1024)(128)(4,1)S(1)}, s32[]{:S(2)}) async-start(s8[4718592]{0:T(1024)(128)(4,1)} %bitcast.91), calls=%async_computation.1 | async-start | bytes 8388608
  122.9 4.5 %slice-start.1 = ((s8[4718592]{0:T(1024)(128)(4,1)}), s8[524288]{0:T(1024)(128)(4,1)S(1)}, s32[]{:S(2)}) async-start(s8[4718592]{0:T(1024)(128)(4,1)} %bitcast.91), calls=%async_computation.2 | async-start | bytes 1048576
  164.0 39.8 %collective-permute-start.3 = (f32[512,1536]{1,0:T(8,128)S(1)}, f32[512,1536]{1,0:T(8,128)S(1)}, u32[]{:S(2)}, u32[]{:S(2)}) collective-permute-start(f32[512,1536]{1,0:T(8,128)S(1)} %get-tuple-element.21), channel_id=1, source_target_pairs={{4,0},{8,4},{12,8},{16,12},{20,16},{24,20},{28,24},{32,28},{36,32}... | collective-permute-start | bytes 9437192 | tf_op jit(solution)/shard_map/ppermute | solution.py:25
  165.9 39.1 %collective-permute-start.2 = (f32[512,1536]{1,0:T(8,128)S(1)}, f32[512,1536]{1,0:T(8,128)S(1)}, u32[]{:S(2)}, u32[]{:S(2)}) collective-permute-start(f32[512,1536]{1,0:T(8,128)S(1)} %get-tuple-element.22), channel_id=1, source_target_pairs={{0,4},{4,8},{8,12},{12,16},{16,20},{20,24},{24,28},{28,32},{32,36}... | collective-permute-start | bytes 9437192 | tf_op jit(solution)/shard_map/ppermute | solution.py:25
  205.8 66.5 %copy-start.1 = (s32[4,768,4]{1,2,0:T(4,128)S(1)}, s32[4,768,4]{1,2,0:T(4,128)}, u32[]{:S(2)}) copy-start(s32[4,768,4]{1,2,0:T(4,128)} %param.10) | copy-start | bytes 147460
where the time goes:
time: 273 us; the launch traced here: 272 us
  local copies, waits for them, and re-layouts  85.3 us (31%)
  blocking collectives  62.4 us (23%)
  matrix products  61.8 us (23%)
  waiting for transfers between devices  43.3 us (16%)
  starting transfers between devices  14 us (5%)
  other arithmetic  5.22 us (2%)
    all_to_all x1, blocking collectives, sent_and_summed(): tiles = lax.all_to_all(cut_along(shard, dim, count), axis, 0, 0, tiled=True)  62.4 us
    gather x7, local copies, waits for them, and re-layouts, on_device(): picked = jnp.take(dense, local[:, k], axis=0)  46.9 us
    ppermute x2, waiting for transfers between devices, passed_along(): return lax.ppermute(shard, axis, pairs)  34.2 us
    dot_general x6, matrix products, on_device(): jnp.einsum('rab,rbw->raw', a_blocks[0, :, k], picked, preferred_element_t...  30.1 us
    dot_general x1, matrix products, on_device(): lax.dot_general(own_rows, product.reshape(-1, width), (((0,), (0,)), ((),...  27.6 us
    convert_element_type x1, local copies, waits for them, and re-layouts, window_rows(): return dense.reshape(count, block, 3 * coarse * block).astype(jnp.bfloat16)  14.1 us
    slice x2, local copies, waits for them, and re-layouts, on_device(): own_rows = dense[GHOST:GHOST + rows_here].reshape(-1, width)  12.3 us
    ppermute x2, starting transfers between devices, passed_along(): return lax.ppermute(shard, axis, pairs)  6.77 us
  transfers between devices with their start and end apart: 4, of which 4 were waited for; matrix products, arithmetic and copies ran while one was open for 0% of the time, Pallas kernels for 0%

commit v1 on v0

v1 whole, which is shorter than its diff:
```python
import jax
import jax.numpy as jnp
from jax import lax
from jax.experimental import pallas as pl
from jax.experimental.pallas import tpu as pltpu
from jax.sharding import PartitionSpec as P


GHOST = 4
F32 = jnp.float32
BF16 = jnp.bfloat16
VMEM_LIMIT = 28 * 1024 * 1024
HBM = pl.BlockSpec(memory_space=pltpu.HBM)
VMEM = pl.BlockSpec(memory_space=pltpu.VMEM)
SMEM = pl.BlockSpec(memory_space=pltpu.SMEM)


def dot(a, b):
    return lax.dot_general(a, b, (((1,), (0,)), ((), ())), preferred_element_type=F32)


def dot_t(a, b):
    return lax.dot_general(a, b, (((0,), (0,)), ((), ())), preferred_element_type=F32)


def start_a(acol, a_hbm, dst, rows, first, sem):
    b = a_hbm.shape[-1]
    count = dst.shape[1] // b
    for i, r in enumerate(rows):
        for k in range(a_hbm.shape[1]):
            c = jnp.clip(acol[r, k] - first, 0, count - 1)
            pltpu.make_async_copy(
                a_hbm.at[r, k], dst.at[pl.ds(i * b, b), pl.ds(pl.multiple_of(c * b, b), b)], sem
            ).start()


def place_of(rel, slots, m, r, low, high):
    coarse = slots.shape[1]
    c = jnp.clip(rel[m, r], low, high - 1)
    u = lax.div(c, coarse)
    return u * coarse + slots[u, c - u * coarse]


def start_w(rel, slots, p_hbm, w, rows, first_row, low, high, sem, first=0):
    b = p_hbm.shape[-1]
    for i, r in enumerate(rows):
        for m in range(p_hbm.shape[1]):
            q = place_of(rel, slots, m, r, low, high) - first
            pltpu.make_async_copy(
                p_hbm.at[i, m],
                w.at[pl.ds((r - first_row) * b, b), pl.ds(pl.multiple_of(q * b, b), b)],
                sem,
            ).start()


def wait_all(ref, sem):
    pltpu.make_async_copy(ref, ref, sem).wait()


def clear(ref):
    ref[...] = jnp.zeros(ref.shape, ref.dtype)


def halo_kernel(p_hbm, first, last, sems):
    g = GHOST
    rows = p_hbm.shape[0]
    moves = (
        pltpu.make_async_copy(p_hbm.at[rows - g : rows], last, sems.at[0]),
        pltpu.make_async_copy(p_hbm.at[0:g], first, sems.at[1]),
    )
    for move in moves:
        move.start()
    for move in moves:
        move.wait()


def first_kernel(acol, rel, slots, a_hbm, p_hbm, h0_hbm, l2_hbm, far, a_l, a_h, w, h0_v, l2_v, s_a, s_p, s_o):
    e = far.shape[0]
    g = GHOST
    clear(w.at[0:e, 0 : 2 * e])
    start_w(rel, slots, p_hbm.at[0:g], w, range(g, 2 * g), g, 0, 2 * g, s_p)
    clear(w.at[2 * e : 3 * e, e : 3 * e])
    start_w(rel, slots, p_hbm.at[2 * g : 3 * g], w, range(3 * g, 4 * g), g, g, 3 * g, s_p)
    start_w(rel, slots, p_hbm.at[g : 2 * g], w, range(2 * g, 3 * g), g, g, 2 * g, s_p)
    clear(a_l)
    start_a(acol, a_hbm, a_l, range(0, g), 0, s_a)
    clear(a_h)
    start_a(acol, a_hbm, a_h, range(2 * g, 3 * g), g, s_a)
    wait_all(p_hbm, s_p)
    wait_all(a_hbm.at[0 : 2 * g], s_a)
    low = w[0:e, 0:e]
    high = w[2 * e : 3 * e, 2 * e : 3 * e]
    h0_v[...] = dot(a_h[:, 0:e], low).astype(BF16)
    out_h = pltpu.make_async_copy(h0_v, h0_hbm, s_o.at[0])
    out_h.start()
    l2_v[...] = dot(a_l[:, 3 * e : 4 * e], high).astype(BF16)
    out_l = pltpu.make_async_copy(l2_v, l2_hbm, s_o.at[1])
    out_l.start()
    far[:, 0:e] = dot_t(high, h0_v[...]).astype(BF16)
    far[:, e : 2 * e] = dot_t(low, l2_v[...]).astype(BF16)
    out_h.wait()
    out_l.wait()


def second_kernel(
    acol, rel, slots, a_hbm, p_hbm, below, above, l_hbm, h_hbm, up, down,
    a_l, a_h, w, w_b, w_a, l_v, h_v, s_p, s_b, s_u, s_l, s_h, s_o,
):
    e = up.shape[0]
    g = GHOST
    one, two = slice(0, e), slice(e, 2 * e)
    clear(a_l)
    start_a(acol, a_hbm, a_l, range(0, g), 0, s_l)
    clear(w.at[0:e, 0 : 2 * e])
    start_w(rel, slots, p_hbm.at[0:g], w, range(g, 2 * g), g, 0, 2 * g, s_p)
    clear(w.at[2 * e : 3 * e, e : 3 * e])
    start_w(rel, slots, p_hbm.at[2 * g : 3 * g], w, range(3 * g, 4 * g), g, g, 3 * g, s_p)
    start_w(rel, slots, p_hbm.at[g : 2 * g], w, range(2 * g, 3 * g), g, g, 2 * g, s_p)
    clear(w_b)
    start_w(rel, slots, below, w_b, range(0, g), 0, 0, 2 * g, s_b)
    clear(a_h)
    start_a(acol, a_hbm, a_h, range(2 * g, 3 * g), g, s_h)
    clear(w_a)
    start_w(rel, slots, above, w_a, range(4 * g, 5 * g), 4 * g, g, 3 * g, s_u, g)
    wait_all(a_hbm.at[0:g], s_l)
    wait_all(p_hbm, s_p)
    low = w[0:e, 0:e]
    high = w[2 * e : 3 * e, 2 * e : 3 * e]
    wait_all(below, s_b)
    l_v[:, one] = (dot(a_l[:, 0:e], w_b[:, one]) + dot(a_l[:, e : 2 * e], low)).astype(BF16)
    down[:, one] = dot_t(low, l_v[:, one]).astype(BF16)
    l_v[:, two] = (dot(a_l[:, 0:e], w_b[:, two]) + dot(a_l[:, e : 4 * e], w[:, two])).astype(BF16)
    out_l = pltpu.make_async_copy(l_v, l_hbm, s_o.at[0])
    out_l.start()
    down[:, two] = dot_t(low, l_v[:, two]).astype(BF16)
    wait_all(above, s_u)
    wait_all(a_hbm.at[2 * g : 3 * g], s_h)
    h_v[:, two] = (dot(a_h[:, 2 * e : 3 * e], high) + dot(a_h[:, 3 * e : 4 * e], w_a[:, two])).astype(BF16)
    up[:, two] = dot_t(high, h_v[:, two]).astype(BF16)
    h_v[:, one] = (dot(a_h[:, 0 : 3 * e], w[:, two]) + dot(a_h[:, 3 * e : 4 * e], w_a[:, one])).astype(BF16)
    out_h = pltpu.make_async_copy(h_v, h_hbm, s_o.at[1])
    out_h.start()
    up[:, one] = dot_t(high, h_v[:, one]).astype(BF16)
    out_l.wait()
    out_h.wait()


def third_kernel(
    acol, rel, slots, a_hbm, p_hbm, l_hbm, h_hbm, l2_hbm, h0_hbm, middle, a_m, ap_l, ap_m, ap_h, w, s_p, s_m, s_a
):
    e = a_m.shape[0]
    g = GHOST
    clear(w.at[0:e, 0 : 2 * e])
    start_w(rel, slots, p_hbm.at[0:g], w, range(g, 2 * g), g, 0, 2 * g, s_p)
    clear(w.at[2 * e : 3 * e, e : 3 * e])
    start_w(rel, slots, p_hbm.at[2 * g : 3 * g], w, range(3 * g, 4 * g), g, g, 3 * g, s_p)
    start_w(rel, slots, p_hbm.at[g : 2 * g], w, range(2 * g, 3 * g), g, g, 2 * g, s_p)
    clear(a_m)
    start_a(acol, a_hbm, a_m, range(g, 2 * g), g, s_m)
    moves = [
        pltpu.make_async_copy(src, dst, s_a.at[i])
        for i, (src, dst) in enumerate(
            (
                (l_hbm, ap_l.at[:, 0 : 2 * e]),
                (l2_hbm, ap_l.at[:, 2 * e : 3 * e]),
                (h0_hbm, ap_h.at[:, 0:e]),
                (h_hbm, ap_h.at[:, e : 3 * e]),
            )
        )
    ]
    for move in moves:
        move.start()
    wait_all(p_hbm, s_p)
    wait_all(a_hbm.at[g : 2 * g], s_m)
    ap_m[:, 0:e] = dot(a_m[:, 0:e], w[0:e, 0:e]).astype(BF16)
    ap_m[:, e : 2 * e] = dot(a_m[...], w[:, e : 2 * e]).astype(BF16)
    ap_m[:, 2 * e : 3 * e] = dot(a_m[:, 2 * e : 3 * e], w[2 * e : 3 * e, 2 * e : 3 * e]).astype(BF16)
    for move in moves:
        move.wait()
    w_l = w[0:e, e : 2 * e]
    w_m = w[e : 2 * e, e : 2 * e]
    w_h = w[2 * e : 3 * e, e : 2 * e]
    for c in range(3):
        at = slice(c * e, (c + 1) * e)
        middle[:, at] = dot_t(w_l, ap_l[:, at]) + dot_t(w_m, ap_m[:, at]) + dot_t(w_h, ap_h[:, at])


def fourth_kernel(middle, below, above, near):
    e = near.shape[0]
    one, two, three = (slice(c * e, (c + 1) * e) for c in range(3))
    near[:, one] = (middle[:, one] + below[:, one].astype(F32)).astype(BF16)
    near[:, two] = (middle[:, two] + below[:, two].astype(F32) + above[:, one].astype(F32)).astype(BF16)
    near[:, three] = (middle[:, three] + above[:, two].astype(F32)).astype(BF16)


def run(body, ins, in_specs, outs, out_specs, scratch, flops):
    return pl.pallas_call(
        body,
        in_specs=in_specs,
        out_specs=out_specs,
        out_shape=outs,
        scratch_shapes=scratch,
        compiler_params=pltpu.CompilerParams(vmem_limit_bytes=VMEM_LIMIT),
        cost_estimate=pl.CostEstimate(flops=flops, transcendentals=0, bytes_accessed=8 * 1024 * 1024),
    )(*ins)


def passed_along(shard, by):
    count = lax.axis_size("slab")
    pairs = [(i, i + by) for i in range(count) if 0 <= i + by < count]
    return lax.ppermute(shard, "slab", pairs)


def window_cols(p_cols, coarse_slot, rows_here):
    coarse = coarse_slot.shape[1]
    slab = lax.axis_index("slab")
    column = lax.axis_index("plane")
    turned = jnp.transpose(p_cols, (0, 2, 1))
    mine = lax.dynamic_slice_in_dim(turned, column, 1, 0)[0]
    mine = jnp.pad(mine, ((0, 0), (GHOST, GHOST)))
    near = lax.dynamic_slice_in_dim(mine, slab * rows_here, rows_here + 2 * GHOST, 1)
    slots = jnp.pad(coarse_slot, ((1, 1), (0, 0)))
    return near - (slab - 1) * coarse, lax.dynamic_slice_in_dim(slots, slab, 3, 0)


def steps(a_blocks, a_cols, p_blocks, p_cols, coarse_slot):
    rows_here, b = a_blocks.shape[1], a_blocks.shape[3]
    coarse = coarse_slot.shape[1]
    e = coarse * b
    slab = lax.axis_index("slab")
    a, p = a_blocks[0], p_blocks[0]
    a = pltpu.with_memory_space_constraint(a, pltpu.HBM)
    p_here = pltpu.with_memory_space_constraint(p, pltpu.HBM)
    part = pltpu.VMEM((GHOST, *p.shape[1:]), BF16)
    first, last = run(halo_kernel, (p_here,), [HBM], (part, part), (VMEM, VMEM), [pltpu.SemaphoreType.DMA((2,))], 0)
    below = passed_along(last, 1)
    above = passed_along(first, -1)
    rel, slots = window_cols(p_cols, coarse_slot, rows_here)
    acol = a_cols[0] - (slab * rows_here - GHOST)
    unit = 2 * e * e * b

    def shape(rows, cols, dtype=BF16, space=pltpu.VMEM):
        return space((rows * e, cols * e), dtype)

    def far_shape(rows, cols):
        return shape(rows, cols, BF16, pltpu.HBM)

    a = pltpu.with_memory_space_constraint(a, pltpu.HBM)
    p_here = pltpu.with_memory_space_constraint(p, pltpu.HBM)

    def scratch(rows, cols):
        return pltpu.VMEM((rows * e, cols * e), BF16)

    dma = pltpu.SemaphoreType.DMA(())
    ap_h0, ap_l2, far = run(
        first_kernel,
        (acol, rel, slots, a, p_here),
        [SMEM, SMEM, SMEM, HBM, HBM],
        (far_shape(1, 1), far_shape(1, 1), shape(1, 2)),
        (HBM, HBM, VMEM),
        [scratch(1, 4), scratch(1, 4), scratch(3, 3), scratch(1, 1), scratch(1, 1)]
        + [dma, dma, pltpu.SemaphoreType.DMA((2,))],
        16 * unit,
    )
    far = lax.all_to_all(far.reshape(coarse, 1, b, 2 * e), "plane", 0, 0, tiled=True)
    below, above = (pltpu.with_memory_space_constraint(x, pltpu.VMEM) for x in (below, above))
    ap_l, ap_h, up, down = run(
        second_kernel,
        (acol, rel, slots, a, p_here, below, above),
        [SMEM, SMEM, SMEM, HBM, HBM, VMEM, VMEM],
        (far_shape(1, 2), far_shape(1, 2), shape(1, 2), shape(1, 2)),
        (HBM, HBM, VMEM, VMEM),
        [scratch(1, 4), scratch(1, 4), scratch(3, 3)]
        + [scratch(1, 2)] * 4
        + [dma] * 5
        + [pltpu.SemaphoreType.DMA((2,))],
        64 * unit,
    )
    from_below = passed_along(up, 1)
    from_above = passed_along(down, -1)
    kept = tuple(pltpu.with_memory_space_constraint(x, pltpu.HBM) for x in (ap_l, ap_h, ap_l2, ap_h0))
    middle = run(
        third_kernel,
        (acol, rel, slots, a, p_here) + kept,
        [SMEM, SMEM, SMEM] + [HBM] * 6,
        shape(1, 3, F32),
        VMEM,
        [scratch(1, 3)] * 4 + [scratch(3, 3), dma, dma, pltpu.SemaphoreType.DMA((4,))],
        56 * unit,
    )
    far = jnp.sum(far.astype(F32), axis=0)
    far_low = passed_along(far[:, :, :e], 1)
    far_high = passed_along(far[:, :, e:], -1)
    near = run(fourth_kernel, (middle, from_below, from_above), [VMEM] * 3, shape(1, 3), VMEM, [], e * 3 * e)
    near = near.reshape(coarse, 1, b, 3 * e)
    near = lax.all_to_all(near, "plane", 0, 0, tiled=True)
    near = jnp.sum(near.astype(F32), axis=0)
    return jnp.concatenate([far_low, near, far_high], axis=2)[None]


def solution(mesh):
    return jax.shard_map(
        steps,
        mesh=mesh,
        in_specs=(
            P("plane", "slab", None, None, None),
            P("plane", "slab", None),
            P("plane", "slab", None, None, None),
            P(),
            P(),
        ),
        out_specs=P("plane", "slab", None, None),
        check_vma=False,
    )
```

time: 273 us -> 83.3 us (0.31)
  the two profiles are of different devices: /device:TPU:113 before, /device:TPU:112 now
where the time goes in v1:
time: 83.3 us; the launch traced here: 82.7 us
  starting transfers between devices  27.4 us (33%)
  waiting for transfers between devices  26.8 us (32%)
  Pallas kernels  25 us (30%)
  other arithmetic  2.91 us (3%)
    pallas_call x5, Pallas kernels, run(): pl.pallas_call(body, in_specs=in_specs, out_specs=out_specs, out_shape=ou...  25 us
    ppermute x6, starting transfers between devices, passed_along(): return lax.ppermute(shard, 'slab', pairs)  19.6 us
    all_to_all x1, waiting for transfers between devices, steps(): near = lax.all_to_all(near, 'plane', 0, 0, tiled=True)  13.6 us
    all_to_all x1, waiting for transfers between devices, steps(): lax.all_to_all(far.reshape(coarse, 1, b, 2 * e), 'plane', 0, 0, tiled=True)  6.9 us
    ppermute x6, waiting for transfers between devices, passed_along(): return lax.ppermute(shard, 'slab', pairs)  6.33 us
    all_to_all x1, starting transfers between devices, steps(): lax.all_to_all(far.reshape(coarse, 1, b, 2 * e), 'plane', 0, 0, tiled=True)  4.3 us
    all_to_all x1, starting transfers between devices, steps(): near = lax.all_to_all(near, 'plane', 0, 0, tiled=True)  3.56 us
  transfers between devices with their start and end apart: 8, of which 4 were waited for; matrix products, arithmetic and copies ran while one was open for 2% of the time, Pallas kernels for 17%

profile of v1, /device:TPU:112, one launch (start us, length us, event | category | flops | bytes accessed | tf_op | source)
XLA Modules:
  0.0 82.7 jit_solution(12187469923325137098)
XLA Ops:
  0.0 0.0 copy-start
  0.0 0.0 copy-start.1
  0.0 0.0 copy-start.2
  0.0 1.2 %shard_map.56 = (bf16[4,4,128,128]{3,2,1,0:T(8,128)(2,1)S(1)}, bf16[4,4,128,128]{3,2,1,0:T(8,128)(2,1)S(1)}) custom-call(bf16[12,4,128,128]{3,2,1,0:T(8,128)(2,1)} %bitcast.18), custom_call_target="tpu_custom_call" | custom-call | bytes 8388608 | tf_op jit(solution)/shard_map/pallas_call | solution.py:197
  1.3 1.9 %collective-permute-start.1 = (bf16[4,4,128,128]{3,2,1,0:T(8,128)(2,1)S(1)}, bf16[4,4,128,128]{3,2,1,0:T(8,128)(2,1)S(1)}, u32[]{:S(2)}, u32[]{:S(2)}) collective-permute-start(bf16[4,4,128,128]{3,2,1,0:T(8,128)(2,1)S(1)} %get-tuple-element.15), channel_id=1, source_target_pairs={{0,4},{4,8},{8,12},{12,16},{16,20},{20,24},{24,28},{28,32},{32,36}... | collective-permute-start | bytes 1572872 | tf_op jit(solution)/shard_map/ppermute | solution.py:211
  3.2 3.6 %collective-permute-start.2 = (bf16[4,4,128,128]{3,2,1,0:T(8,128)(2,1)S(1)}, bf16[4,4,128,128]{3,2,1,0:T(8,128)(2,1)S(1)}, u32[]{:S(2)}, u32[]{:S(2)}) collective-permute-start(bf16[4,4,128,128]{3,2,1,0:T(8,128)(2,1)S(1)} %get-tuple-element.16), channel_id=1, source_target_pairs={{4,0},{8,4},{12,8},{16,12},{20,16},{24,20},{28,24},{32,28},{36,32}... | collective-permute-start | bytes 1572872 | tf_op jit(solution)/shard_map/ppermute | solution.py:211
  6.9 0.0 copy-done.1
  6.9 0.1 copy.13.acol
  7.0 0.0 copy-done.2
  7.0 0.1 copy.12
  7.1 0.0 copy-done
  7.1 0.1 fusion.1.rel
  7.2 4.6 %collective-permute-done.1.below = bf16[4,4,128,128]{3,2,1,0:T(8,128)(2,1)S(1)} collective-permute-done((bf16[4,4,128,128]{3,2,1,0:T(8,128)(2,1)S(1)}, bf16[4,4,128,128]{3,2,1,0:T(8,128)(2,1)S(1)}, u32[]{:S(2)}, u32[]{:S(2)}) %collective-permute-start.1) | collective-permute-done | bytes 524320 | tf_op jit(solution)/shard_map/ppermute | solution.py:211
  11.8 1.8 %collective-permute-done.2.above = bf16[4,4,128,128]{3,2,1,0:T(8,128)(2,1)S(1)} collective-permute-done((bf16[4,4,128,128]{3,2,1,0:T(8,128)(2,1)S(1)}, bf16[4,4,128,128]{3,2,1,0:T(8,128)(2,1)S(1)}, u32[]{:S(2)}, u32[]{:S(2)}) %collective-permute-start.2) | collective-permute-done | bytes 524320 | tf_op jit(solution)/shard_map/ppermute | solution.py:211
  13.5 9.4 %shard_map.57 = (bf16[512,1024]{1,0:T(8,128)(2,1)}, bf16[512,1024]{1,0:T(8,128)(2,1)}, bf16[512,1024]{1,0:T(8,128)(2,1)}, bf16[512,1024]{1,0:T(8,128)(2,1)S(1)}) custom-call(s32[12,7]{1,0:T(8,128)S(1)} %copy.13.acol, s32[4,20]{1,0:T(4,128)S(1)} %fusion.1.rel, s32[3,4]{1,0:T(4,128)S(1)} %pad_dynamic-slice_fusion.slots, bf16[12,7,128,128]{3,2,1,0:T(8,128)(2,1)} %bitcast.23, ...), custom_call_target="tpu_custom_call" | custom-call | flops 4294967296 | bytes 8388608 | tf_op jit(solution)/shard_map/pallas_call | solution.py:197
  22.9 6.5 %collective-permute-start.3 = (bf16[512,1024]{1,0:T(8,128)(2,1)}, bf16[512,1024]{1,0:T(8,128)(2,1)S(1)}, u32[]{:S(2)}, u32[]{:S(2)}) collective-permute-start(bf16[512,1024]{1,0:T(8,128)(2,1)} %get-tuple-element.21), channel_id=1, source_target_pairs={{0,4},{4,8},{8,12},{12,16},{16,20},{20,24},{24,28},{28,32},{32,36}... | collective-permute-start | bytes 3145736 | tf_op jit(solution)/shard_map/ppermute | solution.py:211
  29.4 1.9 %collective-permute-start.4 = (bf16[512,1024]{1,0:T(8,128)(2,1)S(1)}, bf16[512,1024]{1,0:T(8,128)(2,1)S(1)}, u32[]{:S(2)}, u32[]{:S(2)}) collective-permute-start(bf16[512,1024]{1,0:T(8,128)(2,1)S(1)} %get-tuple-element.22), channel_id=1, source_target_pairs={{4,0},{8,4},{12,8},{16,12},{20,16},{24,20},{28,24},{32,28},{36,32}... | collective-permute-start | bytes 3145736 | tf_op jit(solution)/shard_map/ppermute | solution.py:211
  31.4 5.3 %shard_map.55 = (bf16[512,512]{1,0:T(8,128)(2,1)}, bf16[512,512]{1,0:T(8,128)(2,1)}, bf16[512,1024]{1,0:T(8,128)(2,1)}) custom-call(s32[12,7]{1,0:T(8,128)S(1)} %copy.13.acol, s32[4,20]{1,0:T(4,128)S(1)} %fusion.1.rel, s32[3,4]{1,0:T(4,128)S(1)} %pad_dynamic-slice_fusion.slots, bf16[12,7,128,128]{3,2,1,0:T(8,128)(2,1)} %bitcast.24, ...), custom_call_target="tpu_custom_call" | custom-call | flops 1073741824 | bytes 8388608 | tf_op jit(solution)/shard_map/pallas_call | solution.py:197
  36.7 4.3 %all-to-all-start = ((bf16[4,1,128,1024]{3,2,1,0:T(8,128)(2,1)}), bf16[4,1,128,1024]{3,2,1,0:T(8,128)(2,1)}, u32[]{:S(2)}, u32[]{:S(2)}) async-start(bf16[4,1,128,1024]{3,2,1,0:T(8,128)(2,1)} %bitcast.6), calls=%async_computation | async-start | bytes 2097152 | tf_op jit(solution)/shard_map/all_to_all | solution.py:265
  41.0 7.6 %shard_map.58.middle = f32[512,1536]{1,0:T(8,128)S(1)} custom-call(s32[12,7]{1,0:T(8,128)S(1)} %copy.13.acol, s32[4,20]{1,0:T(4,128)S(1)} %fusion.1.rel, s32[3,4]{1,0:T(4,128)S(1)} %pad_dynamic-slice_fusion.slots, bf16[12,7,128,128]{3,2,1,0:T(8,128)(2,1)} %bitcast.25, bf16[12,4,128,128]{3,2,1,0:T(8,128)(2,1)} %bitcast.21, ...), custom_call_target="tpu_custom_call" | custom-call | flops 3758096384 | bytes 8388608 | tf_op jit(solution)/shard_map/pallas_call | solution.py:197
  48.6 0.0 collective-permute-done.3.below
  48.6 0.0 collective-permute-done.4.above
  48.6 1.5 %shard_map.59 = bf16[512,1536]{1,0:T(8,128)(2,1)} custom-call(f32[512,1536]{1,0:T(8,128)S(1)} %shard_map.58.middle, bf16[512,1024]{1,0:T(8,128)(2,1)S(1)} %collective-permute-done.3.below, bf16[512,1024]{1,0:T(8,128)(2,1)S(1)} %collective-permute-done.4.above), custom_call_target="tpu_custom_call" | custom-call | flops 786432 | bytes 8388608 | tf_op jit(solution)/shard_map/pallas_call | solution.py:197
  50.1 6.9 %all-to-all-done = bf16[4,1,128,1024]{3,2,1,0:T(8,128)(2,1)} async-done(((bf16[4,1,128,1024]{3,2,1,0:T(8,128)(2,1)}), bf16[4,1,128,1024]{3,2,1,0:T(8,128)(2,1)}, u32[]{:S(2)}, u32[]{:S(2)}) %all-to-all-start) | async-done | bytes 1048608 | tf_op jit(solution)/shard_map/all_to_all | solution.py:265
  57.0 3.6 %all-to-all-start.1 = ((bf16[4,1,128,1536]{3,2,1,0:T(8,128)(2,1)}), bf16[4,1,128,1536]{3,2,1,0:T(8,128)(2,1)S(1)}, u32[]{:S(2)}, u32[]{:S(2)}) async-start(bf16[4,1,128,1536]{3,2,1,0:T(8,128)(2,1)} %bitcast.9), calls=%async_computation.1 | async-start | bytes 3145728 | tf_op jit(solution)/shard_map/all_to_all | solution.py:296
  60.6 1.5 %convert_reduce_fusion.1 = f32[128,1024]{1,0:T(8,128)S(1)} fusion(bf16[4,1,128,1024]{3,2,1,0:T(8,128)(2,1)} %all-to-all-done), kind=kLoop, calls=%fused_computation.1 | loop fusion | flops 917504 | bytes 1572864 | tf_op jit(solution)/shard_map/reduce_sum | solution.py:291
  62.1 1.9 %collective-permute-start = (f32[1,128,512]{2,1,0:T(8,128)S(1)}, f32[1,128,512]{2,1,0:T(8,128)S(1)}, u32[]{:S(2)}, u32[]{:S(2)}) collective-permute-start(f32[1,128,512]{2,1,0:T(8,128)S(1)} %get-tuple-element.23), channel_id=1, source_target_pairs={{0,4},{4,8},{8,12},{12,16},{16,20},{20,24},{24,28},{28,32},{32,36}... | collective-permute-start | bytes 786440 | tf_op jit(solution)/shard_map/ppermute | solution.py:211
  64.0 3.6 %collective-permute-start.5 = (f32[1,128,512]{2,1,0:T(8,128)S(1)}, f32[1,128,512]{2,1,0:T(8,128)S(1)}, u32[]{:S(2)}, u32[]{:S(2)}) collective-permute-start(f32[1,128,512]{2,1,0:T(8,128)S(1)} %get-tuple-element.24), channel_id=1, source_target_pairs={{4,0},{8,4},{12,8},{16,12},{20,16},{24,20},{28,24},{32,28},{36,32}... | collective-permute-start | bytes 786440 | tf_op jit(solution)/shard_map/ppermute | solution.py:211
  67.7 13.6 %all-to-all-done.1 = bf16[4,1,128,1536]{3,2,1,0:T(8,128)(2,1)S(1)} async-done(((bf16[4,1,128,1536]{3,2,1,0:T(8,128)(2,1)}), bf16[4,1,128,1536]{3,2,1,0:T(8,128)(2,1)S(1)}, u32[]{:S(2)}, u32[]{:S(2)}) %all-to-all-start.1) | async-done | bytes 1572896 | tf_op jit(solution)/shard_map/all_to_all | solution.py:296
  81.3 0.2 convert_reduce_fusion
  81.5 0.0 collective-permute-done
  81.5 0.0 collective-permute-done.5
  81.5 1.1 %maximum_bitcast_fusion = f32[1,1,128,2560]{3,2,1,0:T(8,128)} fusion(f32[1,128,512]{2,1,0:T(8,128)S(1)} %collective-permute-done.5, f32[1,128,1536]{2,1,0:T(8,128)S(1)} %bitcast.22, f32[1,128,512]{2,1,0:T(8,128)S(1)} %collective-permute-done), kind=kLoop, calls=%fused_computation.2 | loop fusion | flops 655360 | bytes 2621440 | tf_op jit(solution)/shard_map/broadcast_in_dim | solution.py:298
  (4 shorter events, 0.1 us)
Async XLA Ops:
  0.0 7.1 %copy-start = (s32[4,768,4]{1,2,0:T(4,128)S(1)}, s32[4,768,4]{1,2,0:T(4,128)}, u32[]{:S(2)}) copy-start(s32[4,768,4]{1,2,0:T(4,128)} %param.8) | copy-start | bytes 147460
  0.0 6.9 %copy-start.1 = (s32[1,12,7]{1,0,2:T(1,128)S(1)}, s32[1,12,7]{1,0,2:T(1,128)}, u32[]{:S(2)}) copy-start(s32[1,12,7]{1,0,2:T(1,128)} %param.6) | copy-start | bytes 1012
  0.0 7.0 %copy-start.2 = (s32[64,4]{0,1:T(4,128)S(1)}, s32[64,4]{0,1:T(4,128)}, u32[]{:S(2)}) copy-start(s32[64,4]{0,1:T(4,128)} %param.9) | copy-start | bytes 3076
  1.3 10.5 %collective-permute-start.1 = (bf16[4,4,128,128]{3,2,1,0:T(8,128)(2,1)S(1)}, bf16[4,4,128,128]{3,2,1,0:T(8,128)(2,1)S(1)}, u32[]{:S(2)}, u32[]{:S(2)}) collective-permute-start(bf16[4,4,128,128]{3,2,1,0:T(8,128)(2,1)S(1)} %get-tuple-element.15), channel_id=1, source_target_pairs={{0,4},{4,8},{8,12},{12,16},{16,20},{20,24},{24,28},{28,32},{32,36}... | collective-permute-start | bytes 1572872 | tf_op jit(solution)/shard_map/ppermute | solution.py:211
  3.2 10.3 %collective-permute-start.2 = (bf16[4,4,128,128]{3,2,1,0:T(8,128)(2,1)S(1)}, bf16[4,4,128,128]{3,2,1,0:T(8,128)(2,1)S(1)}, u32[]{:S(2)}, u32[]{:S(2)}) collective-permute-start(bf16[4,4,128,128]{3,2,1,0:T(8,128)(2,1)S(1)} %get-tuple-element.16), channel_id=1, source_target_pairs={{4,0},{8,4},{12,8},{16,12},{20,16},{24,20},{28,24},{32,28},{36,32}... | collective-permute-start | bytes 1572872 | tf_op jit(solution)/shard_map/ppermute | solution.py:211
  22.9 25.7 %collective-permute-start.3 = (bf16[512,1024]{1,0:T(8,128)(2,1)}, bf16[512,1024]{1,0:T(8,128)(2,1)S(1)}, u32[]{:S(2)}, u32[]{:S(2)}) collective-permute-start(bf16[512,1024]{1,0:T(8,128)(2,1)} %get-tuple-element.21), channel_id=1, source_target_pairs={{0,4},{4,8},{8,12},{12,16},{16,20},{20,24},{24,28},{28,32},{32,36}... | collective-permute-start | bytes 3145736 | tf_op jit(solution)/shard_map/ppermute | solution.py:211
  29.4 19.2 %collective-permute-start.4 = (bf16[512,1024]{1,0:T(8,128)(2,1)S(1)}, bf16[512,1024]{1,0:T(8,128)(2,1)S(1)}, u32[]{:S(2)}, u32[]{:S(2)}) collective-permute-start(bf16[512,1024]{1,0:T(8,128)(2,1)S(1)} %get-tuple-element.22), channel_id=1, source_target_pairs={{4,0},{8,4},{12,8},{16,12},{20,16},{24,20},{28,24},{32,28},{36,32}... | collective-permute-start | bytes 3145736 | tf_op jit(solution)/shard_map/ppermute | solution.py:211
  36.7 20.4 %all-to-all-start = ((bf16[4,1,128,1024]{3,2,1,0:T(8,128)(2,1)}), bf16[4,1,128,1024]{3,2,1,0:T(8,128)(2,1)}, u32[]{:S(2)}, u32[]{:S(2)}) async-start(bf16[4,1,128,1024]{3,2,1,0:T(8,128)(2,1)} %bitcast.6), calls=%async_computation | async-start | bytes 2097152 | tf_op jit(solution)/shard_map/all_to_all | solution.py:265
  57.0 24.2 %all-to-all-start.1 = ((bf16[4,1,128,1536]{3,2,1,0:T(8,128)(2,1)}), bf16[4,1,128,1536]{3,2,1,0:T(8,128)(2,1)S(1)}, u32[]{:S(2)}, u32[]{:S(2)}) async-start(bf16[4,1,128,1536]{3,2,1,0:T(8,128)(2,1)} %bitcast.9), calls=%async_computation.1 | async-start | bytes 3145728 | tf_op jit(solution)/shard_map/all_to_all | solution.py:296
  62.1 19.4 %collective-permute-start = (f32[1,128,512]{2,1,0:T(8,128)S(1)}, f32[1,128,512]{2,1,0:T(8,128)S(1)}, u32[]{:S(2)}, u32[]{:S(2)}) collective-permute-start(f32[1,128,512]{2,1,0:T(8,128)S(1)} %get-tuple-element.23), channel_id=1, source_target_pairs={{0,4},{4,8},{8,12},{12,16},{16,20},{20,24},{24,28},{28,32},{32,36}... | collective-permute-start | bytes 786440 | tf_op jit(solution)/shard_map/ppermute | solution.py:211
  64.0 17.5 %collective-permute-start.5 = (f32[1,128,512]{2,1,0:T(8,128)S(1)}, f32[1,128,512]{2,1,0:T(8,128)S(1)}, u32[]{:S(2)}, u32[]{:S(2)}) collective-permute-start(f32[1,128,512]{2,1,0:T(8,128)S(1)} %get-tuple-element.24), channel_id=1, source_target_pairs={{4,0},{8,4},{12,8},{16,12},{20,16},{24,20},{28,24},{32,28},{36,32}... | collective-permute-start | bytes 786440 | tf_op jit(solution)/shard_map/ppermute | solution.py:211

commit v2 on v1

--- a/solution.py
+++ b/solution.py
@@ -9,7 +9,7 @@
 GHOST = 4
 F32 = jnp.float32
 BF16 = jnp.bfloat16
-VMEM_LIMIT = 28 * 1024 * 1024
+VMEM_LIMIT = 20 * 1024 * 1024
 HBM = pl.BlockSpec(memory_space=pltpu.HBM)
 VMEM = pl.BlockSpec(memory_space=pltpu.VMEM)
 SMEM = pl.BlockSpec(memory_space=pltpu.SMEM)
@@ -61,88 +61,104 @@
     ref[...] = jnp.zeros(ref.shape, ref.dtype)
 
 
-def halo_kernel(p_hbm, first, last, sems):
+def halo_kernel(p_hbm, first_hbm, last_hbm, first, last, s_i, s_o):
     g = GHOST
     rows = p_hbm.shape[0]
-    moves = (
-        pltpu.make_async_copy(p_hbm.at[rows - g : rows], last, sems.at[0]),
-        pltpu.make_async_copy(p_hbm.at[0:g], first, sems.at[1]),
-    )
-    for move in moves:
-        move.start()
-    for move in moves:
-        move.wait()
-
-
-def first_kernel(acol, rel, slots, a_hbm, p_hbm, h0_hbm, l2_hbm, far, a_l, a_h, w, h0_v, l2_v, s_a, s_p, s_o):
+    sides = ((p_hbm.at[rows - g : rows], last, last_hbm), (p_hbm.at[0:g], first, first_hbm))
+    moves = []
+    for i, (src, here, dst) in enumerate(sides):
+        for r in range(g):
+            at = i * g + r
+            into = pltpu.make_async_copy(src.at[r], here.at[r], s_i.at[at])
+            into.start()
+            moves.append((into, pltpu.make_async_copy(here.at[r], dst.at[r], s_o.at[at])))
+    for into, out in moves:
+        into.wait()
+        out.start()
+    for _, out in moves:
+        out.wait()
+
+
+def first_kernel(
+    acol, rel, slots, a_hbm, p_hbm, ghost_l, ghost_h, corner_l, corner_h, own_l, own_h, h0_hbm, l2_hbm, far_hbm,
+    a_l, a_h, w, h0_v, l2_v, far, s_p, s_m, s_h, s_l, s_o,
+):
     e = far.shape[0]
     g = GHOST
+    one, two = slice(0, e), slice(e, 2 * e)
+    outs = []
+
+    def send(src, dst):
+        outs.append(pltpu.make_async_copy(src, dst, s_o.at[len(outs)]))
+        outs[-1].start()
+
     clear(w.at[0:e, 0 : 2 * e])
     start_w(rel, slots, p_hbm.at[0:g], w, range(g, 2 * g), g, 0, 2 * g, s_p)
     clear(w.at[2 * e : 3 * e, e : 3 * e])
     start_w(rel, slots, p_hbm.at[2 * g : 3 * g], w, range(3 * g, 4 * g), g, g, 3 * g, s_p)
-    start_w(rel, slots, p_hbm.at[g : 2 * g], w, range(2 * g, 3 * g), g, g, 2 * g, s_p)
+    clear(a_h)
+    start_a(acol, a_hbm, a_h, range(2 * g, 3 * g), g, s_h)
     clear(a_l)
-    start_a(acol, a_hbm, a_l, range(0, g), 0, s_a)
-    clear(a_h)
-    start_a(acol, a_hbm, a_h, range(2 * g, 3 * g), g, s_a)
-    wait_all(p_hbm, s_p)
-    wait_all(a_hbm.at[0 : 2 * g], s_a)
+    start_a(acol, a_hbm, a_l, range(0, g), 0, s_l)
+    start_w(rel, slots, p_hbm.at[g : 2 * g], w, range(2 * g, 3 * g), g, g, 2 * g, s_m)
+    wait_all(p_hbm.at[0 : 2 * g], s_p)
+    wait_all(a_hbm.at[0:g], s_h)
     low = w[0:e, 0:e]
     high = w[2 * e : 3 * e, 2 * e : 3 * e]
     h0_v[...] = dot(a_h[:, 0:e], low).astype(BF16)
-    out_h = pltpu.make_async_copy(h0_v, h0_hbm, s_o.at[0])
-    out_h.start()
+    send(h0_v, h0_hbm)
+    far[:, one] = dot_t(high, h0_v[...]).astype(BF16)
+    send(far.at[:, one], far_hbm.at[:, one])
+    wait_all(a_hbm.at[0:g], s_l)
     l2_v[...] = dot(a_l[:, 3 * e : 4 * e], high).astype(BF16)
-    out_l = pltpu.make_async_copy(l2_v, l2_hbm, s_o.at[1])
-    out_l.start()
-    far[:, 0:e] = dot_t(high, h0_v[...]).astype(BF16)
-    far[:, e : 2 * e] = dot_t(low, l2_v[...]).astype(BF16)
-    out_h.wait()
-    out_l.wait()
+    send(l2_v, l2_hbm)
+    far[:, two] = dot_t(low, l2_v[...]).astype(BF16)
+    send(far.at[:, two], far_hbm.at[:, two])
+    corner_l[...] = low
+    corner_h[...] = high
+    ghost_l[...] = a_l[:, 0:e]
+    ghost_h[...] = a_h[:, 3 * e : 4 * e]
+    own_l[:, one] = dot(a_l[:, e : 2 * e], low)
+    own_h[:, two] = dot(a_h[:, 2 * e : 3 * e], high)
+    wait_all(p_hbm.at[0:g], s_m)
+    own_l[:, two] = dot(a_l[:, e : 4 * e], w[:, two])
+    own_h[:, one] = dot(a_h[:, 0 : 3 * e], w[:, two])
+    for out in outs:
+        out.wait()
 
 
 def second_kernel(
-    acol, rel, slots, a_hbm, p_hbm, below, above, l_hbm, h_hbm, up, down,
-    a_l, a_h, w, w_b, w_a, l_v, h_v, s_p, s_b, s_u, s_l, s_h, s_o,
+    rel, slots, ghost_l, ghost_h, low, high, own_l, own_h, below, above, l_hbm, h_hbm, up_hbm, down_hbm,
+    w_b, w_a, l_v, h_v, up, down, s_b, s_u, s_o,
 ):
     e = up.shape[0]
     g = GHOST
     one, two = slice(0, e), slice(e, 2 * e)
-    clear(a_l)
-    start_a(acol, a_hbm, a_l, range(0, g), 0, s_l)
-    clear(w.at[0:e, 0 : 2 * e])
-    start_w(rel, slots, p_hbm.at[0:g], w, range(g, 2 * g), g, 0, 2 * g, s_p)
-    clear(w.at[2 * e : 3 * e, e : 3 * e])
-    start_w(rel, slots, p_hbm.at[2 * g : 3 * g], w, range(3 * g, 4 * g), g, g, 3 * g, s_p)
-    start_w(rel, slots, p_hbm.at[g : 2 * g], w, range(2 * g, 3 * g), g, g, 2 * g, s_p)
+    outs = []
+
+    def send(src, dst):
+        outs.append(pltpu.make_async_copy(src, dst, s_o.at[len(outs)]))
+        outs[-1].start()
+
     clear(w_b)
     start_w(rel, slots, below, w_b, range(0, g), 0, 0, 2 * g, s_b)
-    clear(a_h)
-    start_a(acol, a_hbm, a_h, range(2 * g, 3 * g), g, s_h)
     clear(w_a)
     start_w(rel, slots, above, w_a, range(4 * g, 5 * g), 4 * g, g, 3 * g, s_u, g)
-    wait_all(a_hbm.at[0:g], s_l)
-    wait_all(p_hbm, s_p)
-    low = w[0:e, 0:e]
-    high = w[2 * e : 3 * e, 2 * e : 3 * e]
     wait_all(below, s_b)
-    l_v[:, one] = (dot(a_l[:, 0:e], w_b[:, one]) + dot(a_l[:, e : 2 * e], low)).astype(BF16)
-    down[:, one] = dot_t(low, l_v[:, one]).astype(BF16)
-    l_v[:, two] = (dot(a_l[:, 0:e], w_b[:, two]) + dot(a_l[:, e : 4 * e], w[:, two])).astype(BF16)
-    out_l = pltpu.make_async_copy(l_v, l_hbm, s_o.at[0])
-    out_l.start()
-    down[:, two] = dot_t(low, l_v[:, two]).astype(BF16)
+    l_v[...] = (own_l[...] + dot(ghost_l[...], w_b[...])).astype(BF16)
+    send(l_v, l_hbm)
+    down[...] = dot_t(low[...], l_v[...]).astype(BF16)
+    send(down, down_hbm)
     wait_all(above, s_u)
-    wait_all(a_hbm.at[2 * g : 3 * g], s_h)
-    h_v[:, two] = (dot(a_h[:, 2 * e : 3 * e], high) + dot(a_h[:, 3 * e : 4 * e], w_a[:, two])).astype(BF16)
-    up[:, two] = dot_t(high, h_v[:, two]).astype(BF16)
-    h_v[:, one] = (dot(a_h[:, 0 : 3 * e], w[:, two]) + dot(a_h[:, 3 * e : 4 * e], w_a[:, one])).astype(BF16)
-    out_h = pltpu.make_async_copy(h_v, h_hbm, s_o.at[1])
-    out_h.start()
-    up[:, one] = dot_t(high, h_v[:, one]).astype(BF16)
-    out_l.wait()
-    out_h.wait()
+    h_v[:, one] = (own_h[:, one] + dot(ghost_h[...], w_a[:, one])).astype(BF16)
+    up[:, one] = dot_t(high[...], h_v[:, one]).astype(BF16)
+    send(up.at[:, one], up_hbm.at[:, one])
+    h_v[:, two] = (own_h[:, two] + dot(ghost_h[...], w_a[:, two])).astype(BF16)
+    send(h_v, h_hbm)
+    up[:, two] = dot_t(high[...], h_v[:, two]).astype(BF16)
+    send(up.at[:, two], up_hbm.at[:, two])
+    for out in outs:
+        out.wait()
 
 
 def third_kernel(
@@ -185,12 +201,24 @@
         middle[:, at] = dot_t(w_l, ap_l[:, at]) + dot_t(w_m, ap_m[:, at]) + dot_t(w_h, ap_h[:, at])
 
 
-def fourth_kernel(middle, below, above, near):
+def fourth_kernel(middle, below, above, near_hbm, near, s_o):
     e = near.shape[0]
     one, two, three = (slice(c * e, (c + 1) * e) for c in range(3))
+    outs = [pltpu.make_async_copy(near.at[:, c], near_hbm.at[:, c], s_o.at[i]) for i, c in enumerate((one, two, three))]
     near[:, one] = (middle[:, one] + below[:, one].astype(F32)).astype(BF16)
+    outs[0].start()
     near[:, two] = (middle[:, two] + below[:, two].astype(F32) + above[:, one].astype(F32)).astype(BF16)
+    outs[1].start()
     near[:, three] = (middle[:, three] + above[:, two].astype(F32)).astype(BF16)
+    outs[2].start()
+    for out in outs:
+        out.wait()
+
+
+def summed_kernel(far, low, high):
+    e = low.shape[1]
+    low[...] = sum(far[q, :, 0:e].astype(F32) for q in range(far.shape[0]))
+    high[...] = sum(far[q, :, e : 2 * e].astype(F32) for q in range(far.shape[0]))
 
 
 def run(body, ins, in_specs, outs, out_specs, scratch, flops):
@@ -231,8 +259,16 @@
     a, p = a_blocks[0], p_blocks[0]
     a = pltpu.with_memory_space_constraint(a, pltpu.HBM)
     p_here = pltpu.with_memory_space_constraint(p, pltpu.HBM)
-    part = pltpu.VMEM((GHOST, *p.shape[1:]), BF16)
-    first, last = run(halo_kernel, (p_here,), [HBM], (part, part), (VMEM, VMEM), [pltpu.SemaphoreType.DMA((2,))], 0)
+    part = pltpu.HBM((GHOST, *p.shape[1:]), BF16)
+    first, last = run(
+        halo_kernel,
+        (p_here,),
+        [HBM],
+        (part, part),
+        (HBM, HBM),
+        [pltpu.VMEM(part.shape, BF16)] * 2 + [pltpu.SemaphoreType.DMA((2 * GHOST,))] * 2,
+        0,
+    )
     below = passed_along(last, 1)
     above = passed_along(first, -1)
     rel, slots = window_cols(p_cols, coarse_slot, rows_here)
@@ -252,29 +288,27 @@
         return pltpu.VMEM((rows * e, cols * e), BF16)
 
     dma = pltpu.SemaphoreType.DMA(())
-    ap_h0, ap_l2, far = run(
+    *kept, ap_h0, ap_l2, far = run(
         first_kernel,
         (acol, rel, slots, a, p_here),
         [SMEM, SMEM, SMEM, HBM, HBM],
-        (far_shape(1, 1), far_shape(1, 1), shape(1, 2)),
-        (HBM, HBM, VMEM),
-        [scratch(1, 4), scratch(1, 4), scratch(3, 3), scratch(1, 1), scratch(1, 1)]
-        + [dma, dma, pltpu.SemaphoreType.DMA((2,))],
-        16 * unit,
+        (shape(1, 1),) * 4 + (shape(1, 2, F32),) * 2 + (far_shape(1, 1), far_shape(1, 1), far_shape(1, 2)),
+        (VMEM,) * 6 + (HBM,) * 3,
+        [scratch(1, 4), scratch(1, 4), scratch(3, 3), scratch(1, 1), scratch(1, 1), scratch(1, 2)]
+        + [dma] * 4
+        + [pltpu.SemaphoreType.DMA((4,))],
+        48 * unit,
     )
     far = lax.all_to_all(far.reshape(coarse, 1, b, 2 * e), "plane", 0, 0, tiled=True)
     below, above = (pltpu.with_memory_space_constraint(x, pltpu.VMEM) for x in (below, above))
     ap_l, ap_h, up, down = run(
         second_kernel,
-        (acol, rel, slots, a, p_here, below, above),
-        [SMEM, SMEM, SMEM, HBM, HBM, VMEM, VMEM],
-        (far_shape(1, 2), far_shape(1, 2), shape(1, 2), shape(1, 2)),
-        (HBM, HBM, VMEM, VMEM),
-        [scratch(1, 4), scratch(1, 4), scratch(3, 3)]
-        + [scratch(1, 2)] * 4
-        + [dma] * 5
-        + [pltpu.SemaphoreType.DMA((2,))],
-        64 * unit,
+        (rel, slots, *kept, below, above),
+        [SMEM, SMEM] + [VMEM] * 8,
+        (far_shape(1, 2),) * 4,
+        (HBM,) * 4,
+        [scratch(1, 2)] * 6 + [dma, dma, pltpu.SemaphoreType.DMA((5,))],
+        32 * unit,
     )
     from_below = passed_along(up, 1)
     from_above = passed_along(down, -1)
@@ -288,14 +322,23 @@
         [scratch(1, 3)] * 4 + [scratch(3, 3), dma, dma, pltpu.SemaphoreType.DMA((4,))],
         56 * unit,
     )
-    far = jnp.sum(far.astype(F32), axis=0)
-    far_low = passed_along(far[:, :, :e], 1)
-    far_high = passed_along(far[:, :, e:], -1)
-    near = run(fourth_kernel, (middle, from_below, from_above), [VMEM] * 3, shape(1, 3), VMEM, [], e * 3 * e)
+    near = run(
+        fourth_kernel,
+        (middle, from_below, from_above),
+        [VMEM] * 3,
+        far_shape(1, 3),
+        HBM,
+        [scratch(1, 3), pltpu.SemaphoreType.DMA((3,))],
+        e * 3 * e,
+    )
     near = near.reshape(coarse, 1, b, 3 * e)
     near = lax.all_to_all(near, "plane", 0, 0, tiled=True)
+    one = pltpu.VMEM((b, e), F32)
+    low, high = run(summed_kernel, (far.reshape(coarse, b, 2 * e),), [VMEM], (one, one), (VMEM, VMEM), [], b * e * 8)
+    far_low = passed_along(low, 1)
+    far_high = passed_along(high, -1)
     near = jnp.sum(near.astype(F32), axis=0)
-    return jnp.concatenate([far_low, near, far_high], axis=2)[None]
+    return jnp.concatenate([far_low[None], near, far_high[None]], axis=2)[None]
 
 
 def solution(mesh):

time: 83.3 us -> 74.3 us (0.89)
  the two profiles are of different devices: /device:TPU:112 before, /device:TPU:96 now
where the time goes in v2:
time: 74.3 us; the launch traced here: 73.7 us
  starting transfers between devices  26.9 us (36%)
  Pallas kernels  23.3 us (31%)
  waiting for transfers between devices  21.6 us (29%)
  other arithmetic  1.45 us (2%)
    pallas_call x6, Pallas kernels, run(): pl.pallas_call(body, in_specs=in_specs, out_specs=out_specs, out_shape=ou...  23.3 us
    ppermute x6, starting transfers between devices, passed_along(): return lax.ppermute(shard, 'slab', pairs)  19.1 us
    all_to_all x1, waiting for transfers between devices, steps(): near = lax.all_to_all(near, 'plane', 0, 0, tiled=True)  14.8 us
    all_to_all x1, waiting for transfers between devices, steps(): lax.all_to_all(far.reshape(coarse, 1, b, 2 * e), 'plane', 0, 0, tiled=True)  6.15 us
    all_to_all x1, starting transfers between devices, steps(): lax.all_to_all(far.reshape(coarse, 1, b, 2 * e), 'plane', 0, 0, tiled=True)  4.32 us
    all_to_all x1, starting transfers between devices, steps(): near = lax.all_to_all(near, 'plane', 0, 0, tiled=True)  3.56 us
  transfers between devices with their start and end apart: 8, of which 3 were waited for; matrix products, arithmetic and copies ran while one was open for 1% of the time, Pallas kernels for 22%

profile of v2, /device:TPU:96, one launch (start us, length us, event | category | flops | bytes accessed | tf_op | source)
XLA Modules:
  0.0 73.7 jit_solution(14316500202510603355)
XLA Ops:
  0.0 0.0 copy-start
  0.0 0.0 copy-start.1
  0.0 0.0 copy-start.2
  0.0 2.1 %shard_map.57 = (bf16[4,4,128,128]{3,2,1,0:T(8,128)(2,1)}, bf16[4,4,128,128]{3,2,1,0:T(8,128)(2,1)}) custom-call(bf16[12,4,128,128]{3,2,1,0:T(8,128)(2,1)} %bitcast.23), custom_call_target="tpu_custom_call" | custom-call | bytes 8388608 | tf_op jit(solution)/shard_map/pallas_call | solution.py:225
  2.1 1.9 %collective-permute-start.1 = (bf16[4,4,128,128]{3,2,1,0:T(8,128)(2,1)}, bf16[4,4,128,128]{3,2,1,0:T(8,128)(2,1)S(1)}, u32[]{:S(2)}, u32[]{:S(2)}) collective-permute-start(bf16[4,4,128,128]{3,2,1,0:T(8,128)(2,1)} %get-tuple-element.30), channel_id=1, source_target_pairs={{0,4},{4,8},{8,12},{12,16},{16,20},{20,24},{24,28},{28,32},{32,36}... | collective-permute-start | bytes 1572872 | tf_op jit(solution)/shard_map/ppermute | solution.py:239
  4.1 3.6 %collective-permute-start.2 = (bf16[4,4,128,128]{3,2,1,0:T(8,128)(2,1)}, bf16[4,4,128,128]{3,2,1,0:T(8,128)(2,1)S(1)}, u32[]{:S(2)}, u32[]{:S(2)}) collective-permute-start(bf16[4,4,128,128]{3,2,1,0:T(8,128)(2,1)} %get-tuple-element.31), channel_id=1, source_target_pairs={{4,0},{8,4},{12,8},{16,12},{20,16},{24,20},{28,24},{32,28},{36,32}... | collective-permute-start | bytes 1572872 | tf_op jit(solution)/shard_map/ppermute | solution.py:239
  7.7 0.0 copy-done.1
  7.7 0.1 copy.12.acol
  7.8 0.0 copy-done.2
  7.8 0.1 copy.11
  7.9 0.0 copy-done
  8.0 0.1 fusion.1.rel
  8.1 7.0 %shard_map.55 = (bf16[512,512]{1,0:T(8,128)(2,1)S(1)}, bf16[512,512]{1,0:T(8,128)(2,1)S(1)}, bf16[512,512]{1,0:T(8,128)(2,1)S(1)}, bf16[512,512]{1,0:T(8,128)(2,...) custom-call(s32[12,7]{1,0:T(8,128)S(1)} %copy.12.acol, ...), custom_call_target="tpu_custom_call" | custom-call | flops 3221225472 | bytes 8388608 | tf_op jit(solution)/shard_map/pallas_call | solution.py:225
  15.1 0.0 collective-permute-done.1.below
  15.1 0.0 collective-permute-done.2.above
  15.1 5.2 %shard_map.58 = (bf16[512,1024]{1,0:T(8,128)(2,1)}, bf16[512,1024]{1,0:T(8,128)(2,1)}, bf16[512,1024]{1,0:T(8,128)(2,1)}, bf16[512,1024]{1,0:T(8,128)(2,1)}) custom-call(s32[4,20]{1,0:T(4,128)S(1)} %fusion.1.rel, s32[3,4]{1,0:T(4,128)S(1)} %pad_dynamic-slice_fusion.slots, bf16[512,512]{1,0:T(8,128)(2,1)S(1)} %get-tuple-element.24.ghost_l, ...), custom_call_target="tpu_custom_call" | custom-call | flops 2147483648 | bytes 8388608 | tf_op jit(solution)/shard_map/pallas_call | solution.py:225
  20.3 6.0 %collective-permute-start.3 = (bf16[512,1024]{1,0:T(8,128)(2,1)}, bf16[512,1024]{1,0:T(8,128)(2,1)S(1)}, u32[]{:S(2)}, u32[]{:S(2)}) collective-permute-start(bf16[512,1024]{1,0:T(8,128)(2,1)} %get-tuple-element.36), channel_id=1, source_target_pairs={{0,4},{4,8},{8,12},{12,16},{16,20},{20,24},{24,28},{28,32},{32,36}... | collective-permute-start | bytes 3145736 | tf_op jit(solution)/shard_map/ppermute | solution.py:239
  26.3 1.9 %collective-permute-start.4 = (bf16[512,1024]{1,0:T(8,128)(2,1)}, bf16[512,1024]{1,0:T(8,128)(2,1)S(1)}, u32[]{:S(2)}, u32[]{:S(2)}) collective-permute-start(bf16[512,1024]{1,0:T(8,128)(2,1)} %get-tuple-element.37), channel_id=1, source_target_pairs={{4,0},{8,4},{12,8},{16,12},{20,16},{24,20},{28,24},{32,28},{36,32}... | collective-permute-start | bytes 3145736 | tf_op jit(solution)/shard_map/ppermute | solution.py:239
  28.2 4.3 %all-to-all-start = ((bf16[4,1,128,1024]{3,2,1,0:T(8,128)(2,1)}), bf16[4,1,128,1024]{3,2,1,0:T(8,128)(2,1)S(1)}, u32[]{:S(2)}, u32[]{:S(2)}) async-start(bf16[4,1,128,1024]{3,2,1,0:T(8,128)(2,1)} %bitcast.26), calls=%async_computation | async-start | bytes 2097152 | tf_op jit(solution)/shard_map/all_to_all | solution.py:302
  32.5 7.6 %shard_map.59.middle = f32[512,1536]{1,0:T(8,128)S(1)} custom-call(s32[12,7]{1,0:T(8,128)S(1)} %copy.12.acol, s32[4,20]{1,0:T(4,128)S(1)} %fusion.1.rel, s32[3,4]{1,0:T(4,128)S(1)} %pad_dynamic-slice_fusion.slots, bf16[12,7,128,128]{3,2,1,0:T(8,128)(2,1)} %bitcast.30, bf16[12,4,128,128]{3,2,1,0:T(8,128)(2,1)} %bitcast.25, ...), custom_call_target="tpu_custom_call" | custom-call | flops 3758096384 | bytes 8388608 | tf_op jit(solution)/shard_map/pallas_call | solution.py:225
  40.2 0.0 collective-permute-done.3.below
  40.2 0.6 collective-permute-done.4.above
  40.8 1.3 %shard_map.60 = bf16[512,1536]{1,0:T(8,128)(2,1)} custom-call(f32[512,1536]{1,0:T(8,128)S(1)} %shard_map.59.middle, bf16[512,1024]{1,0:T(8,128)(2,1)S(1)} %collective-permute-done.3.below, bf16[512,1024]{1,0:T(8,128)(2,1)S(1)} %collective-permute-done.4.above), custom_call_target="tpu_custom_call" | custom-call | flops 786432 | bytes 8388608 | tf_op jit(solution)/shard_map/pallas_call | solution.py:225
  42.1 6.2 %all-to-all-done = bf16[4,1,128,1024]{3,2,1,0:T(8,128)(2,1)S(1)} async-done(((bf16[4,1,128,1024]{3,2,1,0:T(8,128)(2,1)}), bf16[4,1,128,1024]{3,2,1,0:T(8,128)(2,1)S(1)}, u32[]{:S(2)}, u32[]{:S(2)}) %all-to-all-start) | async-done | bytes 1048608 | tf_op jit(solution)/shard_map/all_to_all | solution.py:302
  48.3 3.6 %all-to-all-start.1 = ((bf16[4,1,128,1536]{3,2,1,0:T(8,128)(2,1)}), bf16[4,1,128,1536]{3,2,1,0:T(8,128)(2,1)S(1)}, u32[]{:S(2)}, u32[]{:S(2)}) async-start(bf16[4,1,128,1536]{3,2,1,0:T(8,128)(2,1)} %bitcast.21), calls=%async_computation.1 | async-start | bytes 3145728 | tf_op jit(solution)/shard_map/all_to_all | solution.py:335
  51.9 0.1 shard_map.56
  52.0 1.9 %collective-permute-start = (f32[128,512]{1,0:T(8,128)S(1)}, f32[128,512]{1,0:T(8,128)S(1)}, u32[]{:S(2)}, u32[]{:S(2)}) collective-permute-start(f32[128,512]{1,0:T(8,128)S(1)} %get-tuple-element.23), channel_id=1, source_target_pairs={{0,4},{4,8},{8,12},{12,16},{16,20},{20,24},{24,28},{28,32},{32,36}... | collective-permute-start | bytes 786440 | tf_op jit(solution)/shard_map/ppermute | solution.py:239
  53.9 3.6 %collective-permute-start.5 = (f32[128,512]{1,0:T(8,128)S(1)}, f32[128,512]{1,0:T(8,128)S(1)}, u32[]{:S(2)}, u32[]{:S(2)}) collective-permute-start(f32[128,512]{1,0:T(8,128)S(1)} %get-tuple-element.38), channel_id=1, source_target_pairs={{4,0},{8,4},{12,8},{16,12},{20,16},{24,20},{28,24},{32,28},{36,32}... | collective-permute-start | bytes 786440 | tf_op jit(solution)/shard_map/ppermute | solution.py:239
  57.6 14.8 %all-to-all-done.1 = bf16[4,1,128,1536]{3,2,1,0:T(8,128)(2,1)S(1)} async-done(((bf16[4,1,128,1536]{3,2,1,0:T(8,128)(2,1)}), bf16[4,1,128,1536]{3,2,1,0:T(8,128)(2,1)S(1)}, u32[]{:S(2)}, u32[]{:S(2)}) %all-to-all-start.1) | async-done | bytes 1572896 | tf_op jit(solution)/shard_map/all_to_all | solution.py:335
  72.3 0.2 convert_reduce_fusion
  72.6 0.0 collective-permute-done
  72.6 0.0 collective-permute-done.5
  72.6 1.1 %maximum_bitcast_fusion = f32[1,1,128,2560]{3,2,1,0:T(8,128)} fusion(f32[1,128,512]{2,1,0:T(8,128)S(1)} %bitcast.28, f32[1,128,1536]{2,1,0:T(8,128)S(1)} %bitcast.22, f32[1,128,512]{2,1,0:T(8,128)S(1)} %bitcast.27), kind=kLoop, calls=%fused_computation.1 | loop fusion | flops 655360 | bytes 2621440 | tf_op jit(solution)/shard_map/broadcast_in_dim | solution.py:341
  (3 shorter events, 0.0 us)
Async XLA Ops:
  0.0 7.9 %copy-start = (s32[4,768,4]{1,2,0:T(4,128)S(1)}, s32[4,768,4]{1,2,0:T(4,128)}, u32[]{:S(2)}) copy-start(s32[4,768,4]{1,2,0:T(4,128)} %param.8) | copy-start | bytes 147460
  0.0 7.7 %copy-start.1 = (s32[1,12,7]{1,0,2:T(1,128)S(1)}, s32[1,12,7]{1,0,2:T(1,128)}, u32[]{:S(2)}) copy-start(s32[1,12,7]{1,0,2:T(1,128)} %param.6) | copy-start | bytes 1012
  0.0 7.8 %copy-start.2 = (s32[64,4]{0,1:T(4,128)S(1)}, s32[64,4]{0,1:T(4,128)}, u32[]{:S(2)}) copy-start(s32[64,4]{0,1:T(4,128)} %param.9) | copy-start | bytes 3076
  2.1 12.9 %collective-permute-start.1 = (bf16[4,4,128,128]{3,2,1,0:T(8,128)(2,1)}, bf16[4,4,128,128]{3,2,1,0:T(8,128)(2,1)S(1)}, u32[]{:S(2)}, u32[]{:S(2)}) collective-permute-start(bf16[4,4,128,128]{3,2,1,0:T(8,128)(2,1)} %get-tuple-element.30), channel_id=1, source_target_pairs={{0,4},{4,8},{8,12},{12,16},{16,20},{20,24},{24,28},{28,32},{32,36}... | collective-permute-start | bytes 1572872 | tf_op jit(solution)/shard_map/ppermute | solution.py:239
  4.1 11.0 %collective-permute-start.2 = (bf16[4,4,128,128]{3,2,1,0:T(8,128)(2,1)}, bf16[4,4,128,128]{3,2,1,0:T(8,128)(2,1)S(1)}, u32[]{:S(2)}, u32[]{:S(2)}) collective-permute-start(bf16[4,4,128,128]{3,2,1,0:T(8,128)(2,1)} %get-tuple-element.31), channel_id=1, source_target_pairs={{4,0},{8,4},{12,8},{16,12},{20,16},{24,20},{28,24},{32,28},{36,32}... | collective-permute-start | bytes 1572872 | tf_op jit(solution)/shard_map/ppermute | solution.py:239
  20.3 19.9 %collective-permute-start.3 = (bf16[512,1024]{1,0:T(8,128)(2,1)}, bf16[512,1024]{1,0:T(8,128)(2,1)S(1)}, u32[]{:S(2)}, u32[]{:S(2)}) collective-permute-start(bf16[512,1024]{1,0:T(8,128)(2,1)} %get-tuple-element.36), channel_id=1, source_target_pairs={{0,4},{4,8},{8,12},{12,16},{16,20},{20,24},{24,28},{28,32},{32,36}... | collective-permute-start | bytes 3145736 | tf_op jit(solution)/shard_map/ppermute | solution.py:239
  26.3 14.5 %collective-permute-start.4 = (bf16[512,1024]{1,0:T(8,128)(2,1)}, bf16[512,1024]{1,0:T(8,128)(2,1)S(1)}, u32[]{:S(2)}, u32[]{:S(2)}) collective-permute-start(bf16[512,1024]{1,0:T(8,128)(2,1)} %get-tuple-element.37), channel_id=1, source_target_pairs={{4,0},{8,4},{12,8},{16,12},{20,16},{24,20},{28,24},{32,28},{36,32}... | collective-permute-start | bytes 3145736 | tf_op jit(solution)/shard_map/ppermute | solution.py:239
  28.2 20.1 %all-to-all-start = ((bf16[4,1,128,1024]{3,2,1,0:T(8,128)(2,1)}), bf16[4,1,128,1024]{3,2,1,0:T(8,128)(2,1)S(1)}, u32[]{:S(2)}, u32[]{:S(2)}) async-start(bf16[4,1,128,1024]{3,2,1,0:T(8,128)(2,1)} %bitcast.26), calls=%async_computation | async-start | bytes 2097152 | tf_op jit(solution)/shard_map/all_to_all | solution.py:302
  48.3 24.0 %all-to-all-start.1 = ((bf16[4,1,128,1536]{3,2,1,0:T(8,128)(2,1)}), bf16[4,1,128,1536]{3,2,1,0:T(8,128)(2,1)S(1)}, u32[]{:S(2)}, u32[]{:S(2)}) async-start(bf16[4,1,128,1536]{3,2,1,0:T(8,128)(2,1)} %bitcast.21), calls=%async_computation.1 | async-start | bytes 3145728 | tf_op jit(solution)/shard_map/all_to_all | solution.py:335
  52.0 20.6 %collective-permute-start = (f32[128,512]{1,0:T(8,128)S(1)}, f32[128,512]{1,0:T(8,128)S(1)}, u32[]{:S(2)}, u32[]{:S(2)}) collective-permute-start(f32[128,512]{1,0:T(8,128)S(1)} %get-tuple-element.23), channel_id=1, source_target_pairs={{0,4},{4,8},{8,12},{12,16},{16,20},{20,24},{24,28},{28,32},{32,36}... | collective-permute-start | bytes 786440 | tf_op jit(solution)/shard_map/ppermute | solution.py:239
  53.9 18.7 %collective-permute-start.5 = (f32[128,512]{1,0:T(8,128)S(1)}, f32[128,512]{1,0:T(8,128)S(1)}, u32[]{:S(2)}, u32[]{:S(2)}) collective-permute-start(f32[128,512]{1,0:T(8,128)S(1)} %get-tuple-element.38), channel_id=1, source_target_pairs={{4,0},{8,4},{12,8},{16,12},{20,16},{24,20},{28,24},{32,28},{36,32}... | collective-permute-start | bytes 786440 | tf_op jit(solution)/shard_map/ppermute | solution.py:239

commit v3 on v2

--- a/solution.py
+++ b/solution.py
@@ -61,15 +61,20 @@
     ref[...] = jnp.zeros(ref.shape, ref.dtype)
 
 
-def halo_kernel(p_hbm, first_hbm, last_hbm, first, last, s_i, s_o):
+def is_even():
+    return lax.rem(lax.axis_index("slab"), 2) == 0
+
+
+def halo_kernel(p_hbm, pair_hbm, cross_hbm, pair, cross, s_i, s_o):
     g = GHOST
-    rows = p_hbm.shape[0]
-    sides = ((p_hbm.at[rows - g : rows], last, last_hbm), (p_hbm.at[0:g], first, first_hbm))
+    last = p_hbm.shape[0] - g
+    even = is_even()
+    sides = ((jnp.where(even, 0, last), cross, cross_hbm), (jnp.where(even, last, 0), pair, pair_hbm))
     moves = []
-    for i, (src, here, dst) in enumerate(sides):
+    for i, (row, here, dst) in enumerate(sides):
         for r in range(g):
             at = i * g + r
-            into = pltpu.make_async_copy(src.at[r], here.at[r], s_i.at[at])
+            into = pltpu.make_async_copy(p_hbm.at[row + r], here.at[r], s_i.at[at])
             into.start()
             moves.append((into, pltpu.make_async_copy(here.at[r], dst.at[r], s_o.at[at])))
     for into, out in moves:
@@ -128,35 +133,59 @@
 
 
 def second_kernel(
-    rel, slots, ghost_l, ghost_h, low, high, own_l, own_h, below, above, l_hbm, h_hbm, up_hbm, down_hbm,
+    rel, slots, ghost_l, ghost_h, low, high, own_l, own_h, pair, cross, l_hbm, h_hbm, pair_hbm, cross_hbm,
     w_b, w_a, l_v, h_v, up, down, s_b, s_u, s_o,
 ):
     e = up.shape[0]
     g = GHOST
     one, two = slice(0, e), slice(e, 2 * e)
+    even = is_even()
     outs = []
+
+    def ghosts(below, above):
+        start_w(rel, slots, below, w_b, range(0, g), 0, 0, 2 * g, s_b)
+        start_w(rel, slots, above, w_a, range(4 * g, 5 * g), 4 * g, g, 3 * g, s_u, g)
 
     def send(src, dst):
         outs.append(pltpu.make_async_copy(src, dst, s_o.at[len(outs)]))
         outs[-1].start()
 
+    def send_to(src, if_even, if_odd):
+        sem = s_o.at[len(outs)]
+        outs.append(pltpu.make_async_copy(src, if_even, sem))
+
+        @pl.when(even)
+        def _():
+            pltpu.make_async_copy(src, if_even, sem).start()
+
+        @pl.when(jnp.logical_not(even))
+        def _():
+            pltpu.make_async_copy(src, if_odd, sem).start()
+
     clear(w_b)
-    start_w(rel, slots, below, w_b, range(0, g), 0, 0, 2 * g, s_b)
     clear(w_a)
-    start_w(rel, slots, above, w_a, range(4 * g, 5 * g), 4 * g, g, 3 * g, s_u, g)
-    wait_all(below, s_b)
+
+    @pl.when(even)
+    def _():
+        ghosts(cross, pair)
+
+    @pl.when(jnp.logical_not(even))
+    def _():
+        ghosts(pair, cross)
+
+    wait_all(pair, s_b)
     l_v[...] = (own_l[...] + dot(ghost_l[...], w_b[...])).astype(BF16)
     send(l_v, l_hbm)
     down[...] = dot_t(low[...], l_v[...]).astype(BF16)
-    send(down, down_hbm)
-    wait_all(above, s_u)
+    send_to(down, cross_hbm, pair_hbm)
+    wait_all(cross, s_u)
     h_v[:, one] = (own_h[:, one] + dot(ghost_h[...], w_a[:, one])).astype(BF16)
     up[:, one] = dot_t(high[...], h_v[:, one]).astype(BF16)
-    send(up.at[:, one], up_hbm.at[:, one])
+    send_to(up.at[:, one], pair_hbm.at[:, one], cross_hbm.at[:, one])
     h_v[:, two] = (own_h[:, two] + dot(ghost_h[...], w_a[:, two])).astype(BF16)
     send(h_v, h_hbm)
     up[:, two] = dot_t(high[...], h_v[:, two]).astype(BF16)
-    send(up.at[:, two], up_hbm.at[:, two])
+    send_to(up.at[:, two], pair_hbm.at[:, two], cross_hbm.at[:, two])
     for out in outs:
         out.wait()
 
@@ -201,18 +230,32 @@
         middle[:, at] = dot_t(w_l, ap_l[:, at]) + dot_t(w_m, ap_m[:, at]) + dot_t(w_h, ap_h[:, at])
 
 
-def fourth_kernel(middle, below, above, near_hbm, near, s_o):
+def fourth_kernel(middle, pair, cross, near_hbm, near, s_o):
     e = near.shape[0]
     one, two, three = (slice(c * e, (c + 1) * e) for c in range(3))
-    outs = [pltpu.make_async_copy(near.at[:, c], near_hbm.at[:, c], s_o.at[i]) for i, c in enumerate((one, two, three))]
-    near[:, one] = (middle[:, one] + below[:, one].astype(F32)).astype(BF16)
-    outs[0].start()
-    near[:, two] = (middle[:, two] + below[:, two].astype(F32) + above[:, one].astype(F32)).astype(BF16)
-    outs[1].start()
-    near[:, three] = (middle[:, three] + above[:, two].astype(F32)).astype(BF16)
-    outs[2].start()
-    for out in outs:
-        out.wait()
+    even = is_even()
+
+    def send(i, at):
+        return pltpu.make_async_copy(near.at[:, at], near_hbm.at[:, at], s_o.at[i])
+
+    def join(below, above):
+        near[:, one] = (middle[:, one] + below[:, one].astype(F32)).astype(BF16)
+        send(0, one).start()
+        near[:, two] = (middle[:, two] + below[:, two].astype(F32) + above[:, one].astype(F32)).astype(BF16)
+        send(1, two).start()
+        near[:, three] = (middle[:, three] + above[:, two].astype(F32)).astype(BF16)
+        send(2, three).start()
+
+    @pl.when(even)
+    def _():
+        join(cross, pair)
+
+    @pl.when(jnp.logical_not(even))
+    def _():
+        join(pair, cross)
+
+    for i, at in enumerate((one, two, three)):
+        send(i, at).wait()
 
 
 def summed_kernel(far, low, high):
@@ -233,6 +276,12 @@
     )(*ins)
 
 
+def swapped(shard, first):
+    count = lax.axis_size("slab")
+    pairs = [(i, i + 1) for i in range(first, count - 1, 2)]
+    return lax.ppermute(shard, "slab", pairs + [(j, i) for i, j in pairs])
+
+
 def passed_along(shard, by):
     count = lax.axis_size("slab")
     pairs = [(i, i + by) for i in range(count) if 0 <= i + by < count]
@@ -260,7 +309,7 @@
     a = pltpu.with_memory_space_constraint(a, pltpu.HBM)
     p_here = pltpu.with_memory_space_constraint(p, pltpu.HBM)
     part = pltpu.HBM((GHOST, *p.shape[1:]), BF16)
-    first, last = run(
+    pair, cross = run(
         halo_kernel,
         (p_here,),
         [HBM],
@@ -269,8 +318,8 @@
         [pltpu.VMEM(part.shape, BF16)] * 2 + [pltpu.SemaphoreType.DMA((2 * GHOST,))] * 2,
         0,
     )
-    below = passed_along(last, 1)
-    above = passed_along(first, -1)
+    cross = swapped(cross, 1)
+    pair = swapped(pair, 0)
     rel, slots = window_cols(p_cols, coarse_slot, rows_here)
     acol = a_cols[0] - (slab * rows_here - GHOST)
     unit = 2 * e * e * b
@@ -300,18 +349,18 @@
         48 * unit,
     )
     far = lax.all_to_all(far.reshape(coarse, 1, b, 2 * e), "plane", 0, 0, tiled=True)
-    below, above = (pltpu.with_memory_space_constraint(x, pltpu.VMEM) for x in (below, above))
-    ap_l, ap_h, up, down = run(
+    pair, cross = (pltpu.with_memory_space_constraint(x, pltpu.VMEM) for x in (pair, cross))
+    ap_l, ap_h, pair, cross = run(
         second_kernel,
-        (rel, slots, *kept, below, above),
+        (rel, slots, *kept, pair, cross),
         [SMEM, SMEM] + [VMEM] * 8,
         (far_shape(1, 2),) * 4,
         (HBM,) * 4,
         [scratch(1, 2)] * 6 + [dma, dma, pltpu.SemaphoreType.DMA((5,))],
         32 * unit,
     )
-    from_below = passed_along(up, 1)
-    from_above = passed_along(down, -1)
+    cross = swapped(cross, 1)
+    pair = swapped(pair, 0)
     kept = tuple(pltpu.with_memory_space_constraint(x, pltpu.HBM) for x in (ap_l, ap_h, ap_l2, ap_h0))
     middle = run(
         third_kernel,
@@ -324,7 +373,7 @@
     )
     near = run(
         fourth_kernel,
-        (middle, from_below, from_above),
+        (middle, pair, cross),
         [VMEM] * 3,
         far_shape(1, 3),
         HBM,

time: 74.3 us -> 69 us (0.929)
  the two profiles are of different devices: /device:TPU:96 before, /device:TPU:113 now
where the time goes in v3:
time: 69 us; the launch traced here: 68.5 us
  starting transfers between devices  23.5 us (34%)
  Pallas kernels  23.4 us (34%)
  waiting for transfers between devices  19.7 us (29%)
  other arithmetic  1.45 us (2%)
    pallas_call x6, Pallas kernels, run(): pl.pallas_call(body, in_specs=in_specs, out_specs=out_specs, out_shape=ou...  23.4 us
    all_to_all x1, waiting for transfers between devices, steps(): near = lax.all_to_all(near, 'plane', 0, 0, tiled=True)  14.7 us
    ppermute x4, starting transfers between devices, swapped(): return lax.ppermute(shard, 'slab', pairs + [(j, i) for i, j in pairs])  10 us
    ppermute x2, starting transfers between devices, passed_along(): return lax.ppermute(shard, 'slab', pairs)  5.9 us
    all_to_all x1, starting transfers between devices, steps(): lax.all_to_all(far.reshape(coarse, 1, b, 2 * e), 'plane', 0, 0, tiled=True)  4.03 us
    all_to_all x1, starting transfers between devices, steps(): near = lax.all_to_all(near, 'plane', 0, 0, tiled=True)  3.56 us
    all_to_all x1, waiting for transfers between devices, steps(): lax.all_to_all(far.reshape(coarse, 1, b, 2 * e), 'plane', 0, 0, tiled=True)  3.39 us
    ppermute x4, waiting for transfers between devices, swapped(): return lax.ppermute(shard, 'slab', pairs + [(j, i) for i, j in pairs])  1.61 us
  transfers between devices with their start and end apart: 8, of which 3 were waited for; matrix products, arithmetic and copies ran while one was open for 1% of the time, Pallas kernels for 23%

profile of v3, /device:TPU:113, one launch (start us, length us, event | category | flops | bytes accessed | tf_op | source)
XLA Modules:
  0.0 68.5 jit_solution(608088912855231024)
XLA Ops:
  0.0 0.0 copy-start
  0.0 0.0 copy-start.1
  0.0 0.0 copy-start.2
  0.0 2.1 %shard_map.57 = (bf16[4,4,128,128]{3,2,1,0:T(8,128)(2,1)}, bf16[4,4,128,128]{3,2,1,0:T(8,128)(2,1)}) custom-call(bf16[12,4,128,128]{3,2,1,0:T(8,128)(2,1)} %bitcast.23), custom_call_target="tpu_custom_call" | custom-call | bytes 8388608 | tf_op jit(solution)/shard_map/pallas_call | solution.py:268
  2.1 0.8 %collective-permute-start.1 = (bf16[4,4,128,128]{3,2,1,0:T(8,128)(2,1)}, bf16[4,4,128,128]{3,2,1,0:T(8,128)(2,1)S(1)}, u32[]{:S(2)}, u32[]{:S(2)}) collective-permute-start(bf16[4,4,128,128]{3,2,1,0:T(8,128)(2,1)} %get-tuple-element.30), channel_id=1, source_target_pairs={{0,4},{8,12},{16,20},{24,28},{32,36},{40,44},{48,52},{56,60},{64,6... | collective-permute-start | bytes 1572872 | tf_op jit(solution)/shard_map/ppermute | solution.py:282
  2.9 4.7 %collective-permute-start.2 = (bf16[4,4,128,128]{3,2,1,0:T(8,128)(2,1)}, bf16[4,4,128,128]{3,2,1,0:T(8,128)(2,1)S(1)}, u32[]{:S(2)}, u32[]{:S(2)}) collective-permute-start(bf16[4,4,128,128]{3,2,1,0:T(8,128)(2,1)} %get-tuple-element.31), channel_id=1, source_target_pairs={{4,8},{12,16},{20,24},{28,32},{36,40},{44,48},{52,56},{60,64},{68,... | collective-permute-start | bytes 1572872 | tf_op jit(solution)/shard_map/ppermute | solution.py:282
  7.6 0.0 copy-done.1
  7.6 0.1 copy.12.acol
  7.7 0.0 copy-done.2
  7.7 0.1 copy.11
  7.8 0.0 copy-done
  7.8 0.1 fusion.1.rel
  7.9 7.0 %shard_map.55 = (bf16[512,512]{1,0:T(8,128)(2,1)S(1)}, bf16[512,512]{1,0:T(8,128)(2,1)S(1)}, bf16[512,512]{1,0:T(8,128)(2,1)S(1)}, bf16[512,512]{1,0:T(8,128)(2,...) custom-call(s32[12,7]{1,0:T(8,128)S(1)} %copy.12.acol, ...), custom_call_target="tpu_custom_call" | custom-call | flops 3221225472 | bytes 8388608 | tf_op jit(solution)/shard_map/pallas_call | solution.py:268
  14.9 0.0 collective-permute-done.1.pair
  14.9 0.0 collective-permute-done.2.cross
  14.9 5.2 %shard_map.58 = (bf16[512,1024]{1,0:T(8,128)(2,1)}, bf16[512,1024]{1,0:T(8,128)(2,1)}, bf16[512,1024]{1,0:T(8,128)(2,1)}, bf16[512,1024]{1,0:T(8,128)(2,1)}) custom-call(s32[4,20]{1,0:T(4,128)S(1)} %fusion.1.rel, s32[3,4]{1,0:T(4,128)S(1)} %pad_dynamic-slice_fusion.slots, bf16[512,512]{1,0:T(8,128)(2,1)S(1)} %get-tuple-element.24.ghost_l, ...), custom_call_target="tpu_custom_call" | custom-call | flops 2147483648 | bytes 8388608 | tf_op jit(solution)/shard_map/pallas_call | solution.py:268
  20.1 0.1 collective-permute-start.3
  20.2 4.5 %collective-permute-start.4 = (bf16[512,1024]{1,0:T(8,128)(2,1)}, bf16[512,1024]{1,0:T(8,128)(2,1)S(1)}, u32[]{:S(2)}, u32[]{:S(2)}) collective-permute-start(bf16[512,1024]{1,0:T(8,128)(2,1)} %get-tuple-element.37), channel_id=1, source_target_pairs={{4,8},{12,16},{20,24},{28,32},{36,40},{44,48},{52,56},{60,64},{68,... | collective-permute-start | bytes 3145736 | tf_op jit(solution)/shard_map/ppermute | solution.py:282
  24.8 4.0 %all-to-all-start = ((bf16[4,1,128,1024]{3,2,1,0:T(8,128)(2,1)}), bf16[4,1,128,1024]{3,2,1,0:T(8,128)(2,1)S(1)}, u32[]{:S(2)}, u32[]{:S(2)}) async-start(bf16[4,1,128,1024]{3,2,1,0:T(8,128)(2,1)} %bitcast.26), calls=%async_computation | async-start | bytes 2097152 | tf_op jit(solution)/shard_map/all_to_all | solution.py:351
  28.8 7.6 %shard_map.59.middle = f32[512,1536]{1,0:T(8,128)S(1)} custom-call(s32[12,7]{1,0:T(8,128)S(1)} %copy.12.acol, s32[4,20]{1,0:T(4,128)S(1)} %fusion.1.rel, s32[3,4]{1,0:T(4,128)S(1)} %pad_dynamic-slice_fusion.slots, bf16[12,7,128,128]{3,2,1,0:T(8,128)(2,1)} %bitcast.30, bf16[12,4,128,128]{3,2,1,0:T(8,128)(2,1)} %bitcast.25, ...), custom_call_target="tpu_custom_call" | custom-call | flops 3758096384 | bytes 8388608 | tf_op jit(solution)/shard_map/pallas_call | solution.py:268
  36.5 0.0 collective-permute-done.3.pair
  36.5 1.6 %collective-permute-done.4.cross = bf16[512,1024]{1,0:T(8,128)(2,1)S(1)} collective-permute-done((bf16[512,1024]{1,0:T(8,128)(2,1)}, bf16[512,1024]{1,0:T(8,128)(2,1)S(1)}, u32[]{:S(2)}, u32[]{:S(2)}) %collective-permute-start.4) | collective-permute-done | bytes 1048608 | tf_op jit(solution)/shard_map/ppermute | solution.py:282
  38.1 1.3 %shard_map.60 = bf16[512,1536]{1,0:T(8,128)(2,1)} custom-call(f32[512,1536]{1,0:T(8,128)S(1)} %shard_map.59.middle, bf16[512,1024]{1,0:T(8,128)(2,1)S(1)} %collective-permute-done.3.pair, bf16[512,1024]{1,0:T(8,128)(2,1)S(1)} %collective-permute-done.4.cross), custom_call_target="tpu_custom_call" | custom-call | flops 786432 | bytes 8388608 | tf_op jit(solution)/shard_map/pallas_call | solution.py:268
  39.4 3.4 %all-to-all-done = bf16[4,1,128,1024]{3,2,1,0:T(8,128)(2,1)S(1)} async-done(((bf16[4,1,128,1024]{3,2,1,0:T(8,128)(2,1)}), bf16[4,1,128,1024]{3,2,1,0:T(8,128)(2,1)S(1)}, u32[]{:S(2)}, u32[]{:S(2)}) %all-to-all-start) | async-done | bytes 1048608 | tf_op jit(solution)/shard_map/all_to_all | solution.py:351
  42.8 3.6 %all-to-all-start.1 = ((bf16[4,1,128,1536]{3,2,1,0:T(8,128)(2,1)}), bf16[4,1,128,1536]{3,2,1,0:T(8,128)(2,1)S(1)}, u32[]{:S(2)}, u32[]{:S(2)}) async-start(bf16[4,1,128,1536]{3,2,1,0:T(8,128)(2,1)} %bitcast.21), calls=%async_computation.1 | async-start | bytes 3145728 | tf_op jit(solution)/shard_map/all_to_all | solution.py:384
  46.3 0.1 shard_map.56
  46.5 4.0 %collective-permute-start = (f32[128,512]{1,0:T(8,128)S(1)}, f32[128,512]{1,0:T(8,128)S(1)}, u32[]{:S(2)}, u32[]{:S(2)}) collective-permute-start(f32[128,512]{1,0:T(8,128)S(1)} %get-tuple-element.23), channel_id=1, source_target_pairs={{0,4},{4,8},{8,12},{12,16},{16,20},{20,24},{24,28},{28,32},{32,36}... | collective-permute-start | bytes 786440 | tf_op jit(solution)/shard_map/ppermute | solution.py:288
  50.5 1.9 %collective-permute-start.5 = (f32[128,512]{1,0:T(8,128)S(1)}, f32[128,512]{1,0:T(8,128)S(1)}, u32[]{:S(2)}, u32[]{:S(2)}) collective-permute-start(f32[128,512]{1,0:T(8,128)S(1)} %get-tuple-element.38), channel_id=1, source_target_pairs={{4,0},{8,4},{12,8},{16,12},{20,16},{24,20},{28,24},{32,28},{36,32}... | collective-permute-start | bytes 786440 | tf_op jit(solution)/shard_map/ppermute | solution.py:288
  52.4 14.7 %all-to-all-done.1 = bf16[4,1,128,1536]{3,2,1,0:T(8,128)(2,1)S(1)} async-done(((bf16[4,1,128,1536]{3,2,1,0:T(8,128)(2,1)}), bf16[4,1,128,1536]{3,2,1,0:T(8,128)(2,1)S(1)}, u32[]{:S(2)}, u32[]{:S(2)}) %all-to-all-start.1) | async-done | bytes 1572896 | tf_op jit(solution)/shard_map/all_to_all | solution.py:384
  67.1 0.2 convert_reduce_fusion
  67.3 0.0 collective-permute-done
  67.3 0.0 collective-permute-done.5
  67.3 1.1 %maximum_bitcast_fusion = f32[1,1,128,2560]{3,2,1,0:T(8,128)} fusion(f32[1,128,512]{2,1,0:T(8,128)S(1)} %bitcast.28, f32[1,128,1536]{2,1,0:T(8,128)S(1)} %bitcast.22, f32[1,128,512]{2,1,0:T(8,128)S(1)} %bitcast.27), kind=kLoop, calls=%fused_computation.1 | loop fusion | flops 655360 | bytes 2621440 | tf_op jit(solution)/shard_map/broadcast_in_dim | solution.py:390
  (3 shorter events, 0.0 us)
Async XLA Ops:
  0.0 7.8 %copy-start = (s32[4,768,4]{1,2,0:T(4,128)S(1)}, s32[4,768,4]{1,2,0:T(4,128)}, u32[]{:S(2)}) copy-start(s32[4,768,4]{1,2,0:T(4,128)} %param.8) | copy-start | bytes 147460
  0.0 7.6 %copy-start.1 = (s32[1,12,7]{1,0,2:T(1,128)S(1)}, s32[1,12,7]{1,0,2:T(1,128)}, u32[]{:S(2)}) copy-start(s32[1,12,7]{1,0,2:T(1,128)} %param.6) | copy-start | bytes 1012
  0.0 7.7 %copy-start.2 = (s32[64,4]{0,1:T(4,128)S(1)}, s32[64,4]{0,1:T(4,128)}, u32[]{:S(2)}) copy-start(s32[64,4]{0,1:T(4,128)} %param.9) | copy-start | bytes 3076
  2.1 12.8 %collective-permute-start.1 = (bf16[4,4,128,128]{3,2,1,0:T(8,128)(2,1)}, bf16[4,4,128,128]{3,2,1,0:T(8,128)(2,1)S(1)}, u32[]{:S(2)}, u32[]{:S(2)}) collective-permute-start(bf16[4,4,128,128]{3,2,1,0:T(8,128)(2,1)} %get-tuple-element.30), channel_id=1, source_target_pairs={{0,4},{8,12},{16,20},{24,28},{32,36},{40,44},{48,52},{56,60},{64,6... | collective-permute-start | bytes 1572872 | tf_op jit(solution)/shard_map/ppermute | solution.py:282
  2.9 12.0 %collective-permute-start.2 = (bf16[4,4,128,128]{3,2,1,0:T(8,128)(2,1)}, bf16[4,4,128,128]{3,2,1,0:T(8,128)(2,1)S(1)}, u32[]{:S(2)}, u32[]{:S(2)}) collective-permute-start(bf16[4,4,128,128]{3,2,1,0:T(8,128)(2,1)} %get-tuple-element.31), channel_id=1, source_target_pairs={{4,8},{12,16},{20,24},{28,32},{36,40},{44,48},{52,56},{60,64},{68,... | collective-permute-start | bytes 1572872 | tf_op jit(solution)/shard_map/ppermute | solution.py:282
  20.1 16.3 %collective-permute-start.3 = (bf16[512,1024]{1,0:T(8,128)(2,1)}, bf16[512,1024]{1,0:T(8,128)(2,1)S(1)}, u32[]{:S(2)}, u32[]{:S(2)}) collective-permute-start(bf16[512,1024]{1,0:T(8,128)(2,1)} %get-tuple-element.36), channel_id=1, source_target_pairs={{0,4},{8,12},{16,20},{24,28},{32,36},{40,44},{48,52},{56,60},{64,6... | collective-permute-start | bytes 3145736 | tf_op jit(solution)/shard_map/ppermute | solution.py:282
  20.2 17.8 %collective-permute-start.4 = (bf16[512,1024]{1,0:T(8,128)(2,1)}, bf16[512,1024]{1,0:T(8,128)(2,1)S(1)}, u32[]{:S(2)}, u32[]{:S(2)}) collective-permute-start(bf16[512,1024]{1,0:T(8,128)(2,1)} %get-tuple-element.37), channel_id=1, source_target_pairs={{4,8},{12,16},{20,24},{28,32},{36,40},{44,48},{52,56},{60,64},{68,... | collective-permute-start | bytes 3145736 | tf_op jit(solution)/shard_map/ppermute | solution.py:282
  24.8 18.0 %all-to-all-start = ((bf16[4,1,128,1024]{3,2,1,0:T(8,128)(2,1)}), bf16[4,1,128,1024]{3,2,1,0:T(8,128)(2,1)S(1)}, u32[]{:S(2)}, u32[]{:S(2)}) async-start(bf16[4,1,128,1024]{3,2,1,0:T(8,128)(2,1)} %bitcast.26), calls=%async_computation | async-start | bytes 2097152 | tf_op jit(solution)/shard_map/all_to_all | solution.py:351
  42.8 24.3 %all-to-all-start.1 = ((bf16[4,1,128,1536]{3,2,1,0:T(8,128)(2,1)}), bf16[4,1,128,1536]{3,2,1,0:T(8,128)(2,1)S(1)}, u32[]{:S(2)}, u32[]{:S(2)}) async-start(bf16[4,1,128,1536]{3,2,1,0:T(8,128)(2,1)} %bitcast.21), calls=%async_computation.1 | async-start | bytes 3145728 | tf_op jit(solution)/shard_map/all_to_all | solution.py:384
  46.5 20.8 %collective-permute-start = (f32[128,512]{1,0:T(8,128)S(1)}, f32[128,512]{1,0:T(8,128)S(1)}, u32[]{:S(2)}, u32[]{:S(2)}) collective-permute-start(f32[128,512]{1,0:T(8,128)S(1)} %get-tuple-element.23), channel_id=1, source_target_pairs={{0,4},{4,8},{8,12},{12,16},{16,20},{20,24},{24,28},{28,32},{32,36}... | collective-permute-start | bytes 786440 | tf_op jit(solution)/shard_map/ppermute | solution.py:288
  50.5 16.9 %collective-permute-start.5 = (f32[128,512]{1,0:T(8,128)S(1)}, f32[128,512]{1,0:T(8,128)S(1)}, u32[]{:S(2)}, u32[]{:S(2)}) collective-permute-start(f32[128,512]{1,0:T(8,128)S(1)} %get-tuple-element.38), channel_id=1, source_target_pairs={{4,0},{8,4},{12,8},{16,12},{20,16},{24,20},{28,24},{32,28},{36,32}... | collective-permute-start | bytes 786440 | tf_op jit(solution)/shard_map/ppermute | solution.py:288

commit v4 on v3

--- a/solution.py
+++ b/solution.py
@@ -65,23 +65,16 @@
     return lax.rem(lax.axis_index("slab"), 2) == 0
 
 
-def halo_kernel(p_hbm, pair_hbm, cross_hbm, pair, cross, s_i, s_o):
+def halo_kernel(p_hbm, pair, cross, sems):
     g = GHOST
     last = p_hbm.shape[0] - g
     even = is_even()
-    sides = ((jnp.where(even, 0, last), cross, cross_hbm), (jnp.where(even, last, 0), pair, pair_hbm))
-    moves = []
-    for i, (row, here, dst) in enumerate(sides):
-        for r in range(g):
-            at = i * g + r
-            into = pltpu.make_async_copy(p_hbm.at[row + r], here.at[r], s_i.at[at])
-            into.start()
-            moves.append((into, pltpu.make_async_copy(here.at[r], dst.at[r], s_o.at[at])))
-    for into, out in moves:
-        into.wait()
-        out.start()
-    for _, out in moves:
-        out.wait()
+    sides = ((jnp.where(even, 0, last), cross), (jnp.where(even, last, 0), pair))
+    moves = [pltpu.make_async_copy(p_hbm.at[pl.ds(row, g)], dst, sems.at[i]) for i, (row, dst) in enumerate(sides)]
+    for move in moves:
+        move.start()
+    for move in moves:
+        move.wait()
 
 
 def first_kernel(
@@ -142,9 +135,20 @@
     even = is_even()
     outs = []
 
-    def ghosts(below, above):
+    def ghost_below(below):
         start_w(rel, slots, below, w_b, range(0, g), 0, 0, 2 * g, s_b)
+
+    def ghost_above(above):
         start_w(rel, slots, above, w_a, range(4 * g, 5 * g), 4 * g, g, 3 * g, s_u, g)
+
+    def by_parity(start, if_even, if_odd):
+        @pl.when(even)
+        def _():
+            start(if_even)
+
+        @pl.when(jnp.logical_not(even))
+        def _():
+            start(if_odd)
 
     def send(src, dst):
         outs.append(pltpu.make_async_copy(src, dst, s_o.at[len(outs)]))
@@ -163,16 +167,9 @@
             pltpu.make_async_copy(src, if_odd, sem).start()
 
     clear(w_b)
+    by_parity(ghost_below, cross, pair)
     clear(w_a)
-
-    @pl.when(even)
-    def _():
-        ghosts(cross, pair)
-
-    @pl.when(jnp.logical_not(even))
-    def _():
-        ghosts(pair, cross)
-
+    by_parity(ghost_above, pair, cross)
     wait_all(pair, s_b)
     l_v[...] = (own_l[...] + dot(ghost_l[...], w_b[...])).astype(BF16)
     send(l_v, l_hbm)
@@ -184,8 +181,9 @@
     send_to(up.at[:, one], pair_hbm.at[:, one], cross_hbm.at[:, one])
     h_v[:, two] = (own_h[:, two] + dot(ghost_h[...], w_a[:, two])).astype(BF16)
     send(h_v, h_hbm)
-    up[:, two] = dot_t(high[...], h_v[:, two]).astype(BF16)
-    send_to(up.at[:, two], pair_hbm.at[:, two], cross_hbm.at[:, two])
+    for at in (slice(e, e + e // 2), slice(e + e // 2, 2 * e)):
+        up[:, at] = dot_t(high[...], h_v[:, at]).astype(BF16)
+        send_to(up.at[:, at], pair_hbm.at[:, at], cross_hbm.at[:, at])
     for out in outs:
         out.wait()
 
@@ -308,16 +306,8 @@
     a, p = a_blocks[0], p_blocks[0]
     a = pltpu.with_memory_space_constraint(a, pltpu.HBM)
     p_here = pltpu.with_memory_space_constraint(p, pltpu.HBM)
-    part = pltpu.HBM((GHOST, *p.shape[1:]), BF16)
-    pair, cross = run(
-        halo_kernel,
-        (p_here,),
-        [HBM],
-        (part, part),
-        (HBM, HBM),
-        [pltpu.VMEM(part.shape, BF16)] * 2 + [pltpu.SemaphoreType.DMA((2 * GHOST,))] * 2,
-        0,
-    )
+    part = pltpu.VMEM((GHOST, *p.shape[1:]), BF16)
+    pair, cross = run(halo_kernel, (p_here,), [HBM], (part, part), (VMEM, VMEM), [pltpu.SemaphoreType.DMA((2,))], 0)
     cross = swapped(cross, 1)
     pair = swapped(pair, 0)
     rel, slots = window_cols(p_cols, coarse_slot, rows_here)
@@ -356,7 +346,7 @@
         [SMEM, SMEM] + [VMEM] * 8,
         (far_shape(1, 2),) * 4,
         (HBM,) * 4,
-        [scratch(1, 2)] * 6 + [dma, dma, pltpu.SemaphoreType.DMA((5,))],
+        [scratch(1, 2)] * 6 + [dma, dma, pltpu.SemaphoreType.DMA((6,))],
         32 * unit,
     )
     cross = swapped(cross, 1)

time: 69 us -> 68.6 us (level)
  waiting for transfers between devices: 19.7 us -> 20.5 us
  Pallas kernels: 23.4 us -> 22.6 us
    pallas_call x6, Pallas kernels: 23.4 us -> 22.6 us  [run(): pl.pallas_call(body, in_specs=in_specs, out_specs=out_specs, out_shape=ou...]
  transfers between devices with their start and end apart: 8 -> 8, of which waited for: 3 -> 3; matrix products, arithmetic and copies ran while one was open for 1% -> 1% of each run, Pallas kernels for 23% -> 24%
where the time goes in v4:
time: 68.6 us; the launch traced here: 68.1 us
  starting transfers between devices  23.1 us (34%)
  Pallas kernels  22.6 us (33%)
  waiting for transfers between devices  20.5 us (30%)
  other arithmetic  1.45 us (2%)
    pallas_call x6, Pallas kernels, run(): pl.pallas_call(body, in_specs=in_specs, out_specs=out_specs, out_shape=ou...  22.6 us
    all_to_all x1, waiting for transfers between devices, steps(): near = lax.all_to_all(near, 'plane', 0, 0, tiled=True)  15.3 us
    ppermute x4, starting transfers between devices, swapped(): return lax.ppermute(shard, 'slab', pairs + [(j, i) for i, j in pairs])  9.83 us
    ppermute x2, starting transfers between devices, passed_along(): return lax.ppermute(shard, 'slab', pairs)  5.69 us
    all_to_all x1, starting transfers between devices, steps(): lax.all_to_all(far.reshape(coarse, 1, b, 2 * e), 'plane', 0, 0, tiled=True)  4.04 us
    all_to_all x1, starting transfers between devices, steps(): near = lax.all_to_all(near, 'plane', 0, 0, tiled=True)  3.56 us
    all_to_all x1, waiting for transfers between devices, steps(): lax.all_to_all(far.reshape(coarse, 1, b, 2 * e), 'plane', 0, 0, tiled=True)  3.4 us
    ppermute x4, waiting for transfers between devices, swapped(): return lax.ppermute(shard, 'slab', pairs + [(j, i) for i, j in pairs])  1.8 us
  transfers between devices with their start and end apart: 8, of which 3 were waited for; matrix products, arithmetic and copies ran while one was open for 1% of the time, Pallas kernels for 24%

profile of v4, /device:TPU:113, one launch (start us, length us, event | category | flops | bytes accessed | tf_op | source)
XLA Modules:
  0.0 68.1 jit_solution(4159120872818125393)
XLA Ops:
  0.0 0.0 copy-start
  0.0 0.0 copy-start.1
  0.0 0.0 copy-start.2
  0.0 1.2 %shard_map.57 = (bf16[4,4,128,128]{3,2,1,0:T(8,128)(2,1)S(1)}, bf16[4,4,128,128]{3,2,1,0:T(8,128)(2,1)S(1)}) custom-call(bf16[12,4,128,128]{3,2,1,0:T(8,128)(2,1)} %bitcast.23), custom_call_target="tpu_custom_call" | custom-call | bytes 8388608 | tf_op jit(solution)/shard_map/pallas_call | solution.py:266
  1.3 0.8 %collective-permute-start.1 = (bf16[4,4,128,128]{3,2,1,0:T(8,128)(2,1)S(1)}, bf16[4,4,128,128]{3,2,1,0:T(8,128)(2,1)S(1)}, u32[]{:S(2)}, u32[]{:S(2)}) collective-permute-start(bf16[4,4,128,128]{3,2,1,0:T(8,128)(2,1)S(1)} %get-tuple-element.30), channel_id=1, source_target_pairs={{0,4},{8,12},{16,20},{24,28},{32,36},{40,44},{48,52},{56,60},{64,6... | collective-permute-start | bytes 1572872 | tf_op jit(solution)/shard_map/ppermute | solution.py:280
  2.0 4.7 %collective-permute-start.2 = (bf16[4,4,128,128]{3,2,1,0:T(8,128)(2,1)S(1)}, bf16[4,4,128,128]{3,2,1,0:T(8,128)(2,1)S(1)}, u32[]{:S(2)}, u32[]{:S(2)}) collective-permute-start(bf16[4,4,128,128]{3,2,1,0:T(8,128)(2,1)S(1)} %get-tuple-element.31), channel_id=1, source_target_pairs={{4,8},{12,16},{20,24},{28,32},{36,40},{44,48},{52,56},{60,64},{68,... | collective-permute-start | bytes 1572872 | tf_op jit(solution)/shard_map/ppermute | solution.py:280
  6.7 0.0 copy-done.1
  6.7 0.1 copy.12.acol
  6.8 0.0 copy-done.2
  6.8 0.1 copy.11
  6.9 0.0 copy-done
  7.0 0.1 fusion.1.rel
  7.0 7.0 %shard_map.55 = (bf16[512,512]{1,0:T(8,128)(2,1)S(1)}, bf16[512,512]{1,0:T(8,128)(2,1)S(1)}, bf16[512,512]{1,0:T(8,128)(2,1)S(1)}, bf16[512,512]{1,0:T(8,128)(2,...) custom-call(s32[12,7]{1,0:T(8,128)S(1)} %copy.12.acol, ...), custom_call_target="tpu_custom_call" | custom-call | flops 3221225472 | bytes 8388608 | tf_op jit(solution)/shard_map/pallas_call | solution.py:266
  14.1 0.0 collective-permute-done.1.pair
  14.1 0.0 collective-permute-done.2.cross
  14.1 5.2 %shard_map.58 = (bf16[512,1024]{1,0:T(8,128)(2,1)}, bf16[512,1024]{1,0:T(8,128)(2,1)}, bf16[512,1024]{1,0:T(8,128)(2,1)}, bf16[512,1024]{1,0:T(8,128)(2,1)}) custom-call(s32[4,20]{1,0:T(4,128)S(1)} %fusion.1.rel, s32[3,4]{1,0:T(4,128)S(1)} %pad_dynamic-slice_fusion.slots, bf16[512,512]{1,0:T(8,128)(2,1)S(1)} %get-tuple-element.24.ghost_l, ...), custom_call_target="tpu_custom_call" | custom-call | flops 2147483648 | bytes 8388608 | tf_op jit(solution)/shard_map/pallas_call | solution.py:266
  19.3 0.1 collective-permute-start.3
  19.4 4.3 %collective-permute-start.4 = (bf16[512,1024]{1,0:T(8,128)(2,1)}, bf16[512,1024]{1,0:T(8,128)(2,1)S(1)}, u32[]{:S(2)}, u32[]{:S(2)}) collective-permute-start(bf16[512,1024]{1,0:T(8,128)(2,1)} %get-tuple-element.37), channel_id=1, source_target_pairs={{4,8},{12,16},{20,24},{28,32},{36,40},{44,48},{52,56},{60,64},{68,... | collective-permute-start | bytes 3145736 | tf_op jit(solution)/shard_map/ppermute | solution.py:280
  23.7 4.0 %all-to-all-start = ((bf16[4,1,128,1024]{3,2,1,0:T(8,128)(2,1)}), bf16[4,1,128,1024]{3,2,1,0:T(8,128)(2,1)S(1)}, u32[]{:S(2)}, u32[]{:S(2)}) async-start(bf16[4,1,128,1024]{3,2,1,0:T(8,128)(2,1)} %bitcast.26), calls=%async_computation | async-start | bytes 2097152 | tf_op jit(solution)/shard_map/all_to_all | solution.py:341
  27.8 7.6 %shard_map.59.middle = f32[512,1536]{1,0:T(8,128)S(1)} custom-call(s32[12,7]{1,0:T(8,128)S(1)} %copy.12.acol, s32[4,20]{1,0:T(4,128)S(1)} %fusion.1.rel, s32[3,4]{1,0:T(4,128)S(1)} %pad_dynamic-slice_fusion.slots, bf16[12,7,128,128]{3,2,1,0:T(8,128)(2,1)} %bitcast.30, bf16[12,4,128,128]{3,2,1,0:T(8,128)(2,1)} %bitcast.25, ...), custom_call_target="tpu_custom_call" | custom-call | flops 3758096384 | bytes 8388608 | tf_op jit(solution)/shard_map/pallas_call | solution.py:266
  35.4 0.0 collective-permute-done.3.pair
  35.5 1.8 %collective-permute-done.4.cross = bf16[512,1024]{1,0:T(8,128)(2,1)S(1)} collective-permute-done((bf16[512,1024]{1,0:T(8,128)(2,1)}, bf16[512,1024]{1,0:T(8,128)(2,1)S(1)}, u32[]{:S(2)}, u32[]{:S(2)}) %collective-permute-start.4) | collective-permute-done | bytes 1048608 | tf_op jit(solution)/shard_map/ppermute | solution.py:280
  37.3 1.3 %shard_map.60 = bf16[512,1536]{1,0:T(8,128)(2,1)} custom-call(f32[512,1536]{1,0:T(8,128)S(1)} %shard_map.59.middle, bf16[512,1024]{1,0:T(8,128)(2,1)S(1)} %collective-permute-done.3.pair, bf16[512,1024]{1,0:T(8,128)(2,1)S(1)} %collective-permute-done.4.cross), custom_call_target="tpu_custom_call" | custom-call | flops 786432 | bytes 8388608 | tf_op jit(solution)/shard_map/pallas_call | solution.py:266
  38.6 3.4 %all-to-all-done = bf16[4,1,128,1024]{3,2,1,0:T(8,128)(2,1)S(1)} async-done(((bf16[4,1,128,1024]{3,2,1,0:T(8,128)(2,1)}), bf16[4,1,128,1024]{3,2,1,0:T(8,128)(2,1)S(1)}, u32[]{:S(2)}, u32[]{:S(2)}) %all-to-all-start) | async-done | bytes 1048608 | tf_op jit(solution)/shard_map/all_to_all | solution.py:341
  42.0 3.6 %all-to-all-start.1 = ((bf16[4,1,128,1536]{3,2,1,0:T(8,128)(2,1)}), bf16[4,1,128,1536]{3,2,1,0:T(8,128)(2,1)S(1)}, u32[]{:S(2)}, u32[]{:S(2)}) async-start(bf16[4,1,128,1536]{3,2,1,0:T(8,128)(2,1)} %bitcast.21), calls=%async_computation.1 | async-start | bytes 3145728 | tf_op jit(solution)/shard_map/all_to_all | solution.py:374
  45.5 0.1 shard_map.56
  45.7 3.8 %collective-permute-start = (f32[128,512]{1,0:T(8,128)S(1)}, f32[128,512]{1,0:T(8,128)S(1)}, u32[]{:S(2)}, u32[]{:S(2)}) collective-permute-start(f32[128,512]{1,0:T(8,128)S(1)} %get-tuple-element.23), channel_id=1, source_target_pairs={{0,4},{4,8},{8,12},{12,16},{16,20},{20,24},{24,28},{28,32},{32,36}... | collective-permute-start | bytes 786440 | tf_op jit(solution)/shard_map/ppermute | solution.py:286
  49.4 1.9 %collective-permute-start.5 = (f32[128,512]{1,0:T(8,128)S(1)}, f32[128,512]{1,0:T(8,128)S(1)}, u32[]{:S(2)}, u32[]{:S(2)}) collective-permute-start(f32[128,512]{1,0:T(8,128)S(1)} %get-tuple-element.38), channel_id=1, source_target_pairs={{4,0},{8,4},{12,8},{16,12},{20,16},{24,20},{28,24},{32,28},{36,32}... | collective-permute-start | bytes 786440 | tf_op jit(solution)/shard_map/ppermute | solution.py:286
  51.4 15.3 %all-to-all-done.1 = bf16[4,1,128,1536]{3,2,1,0:T(8,128)(2,1)S(1)} async-done(((bf16[4,1,128,1536]{3,2,1,0:T(8,128)(2,1)}), bf16[4,1,128,1536]{3,2,1,0:T(8,128)(2,1)S(1)}, u32[]{:S(2)}, u32[]{:S(2)}) %all-to-all-start.1) | async-done | bytes 1572896 | tf_op jit(solution)/shard_map/all_to_all | solution.py:374
  66.7 0.2 convert_reduce_fusion
  66.9 0.0 collective-permute-done
  66.9 0.0 collective-permute-done.5
  66.9 1.1 %maximum_bitcast_fusion = f32[1,1,128,2560]{3,2,1,0:T(8,128)} fusion(f32[1,128,512]{2,1,0:T(8,128)S(1)} %bitcast.28, f32[1,128,1536]{2,1,0:T(8,128)S(1)} %bitcast.22, f32[1,128,512]{2,1,0:T(8,128)S(1)} %bitcast.27), kind=kLoop, calls=%fused_computation.1 | loop fusion | flops 655360 | bytes 2621440 | tf_op jit(solution)/shard_map/broadcast_in_dim | solution.py:380
  (3 shorter events, 0.0 us)
Async XLA Ops:
  0.0 6.9 %copy-start = (s32[4,768,4]{1,2,0:T(4,128)S(1)}, s32[4,768,4]{1,2,0:T(4,128)}, u32[]{:S(2)}) copy-start(s32[4,768,4]{1,2,0:T(4,128)} %param.8) | copy-start | bytes 147460
  0.0 6.7 %copy-start.1 = (s32[1,12,7]{1,0,2:T(1,128)S(1)}, s32[1,12,7]{1,0,2:T(1,128)}, u32[]{:S(2)}) copy-start(s32[1,12,7]{1,0,2:T(1,128)} %param.6) | copy-start | bytes 1012
  0.0 6.8 %copy-start.2 = (s32[64,4]{0,1:T(4,128)S(1)}, s32[64,4]{0,1:T(4,128)}, u32[]{:S(2)}) copy-start(s32[64,4]{0,1:T(4,128)} %param.9) | copy-start | bytes 3076
  1.3 12.8 %collective-permute-start.1 = (bf16[4,4,128,128]{3,2,1,0:T(8,128)(2,1)S(1)}, bf16[4,4,128,128]{3,2,1,0:T(8,128)(2,1)S(1)}, u32[]{:S(2)}, u32[]{:S(2)}) collective-permute-start(bf16[4,4,128,128]{3,2,1,0:T(8,128)(2,1)S(1)} %get-tuple-element.30), channel_id=1, source_target_pairs={{0,4},{8,12},{16,20},{24,28},{32,36},{40,44},{48,52},{56,60},{64,6... | collective-permute-start | bytes 1572872 | tf_op jit(solution)/shard_map/ppermute | solution.py:280
  2.0 12.0 %collective-permute-start.2 = (bf16[4,4,128,128]{3,2,1,0:T(8,128)(2,1)S(1)}, bf16[4,4,128,128]{3,2,1,0:T(8,128)(2,1)S(1)}, u32[]{:S(2)}, u32[]{:S(2)}) collective-permute-start(bf16[4,4,128,128]{3,2,1,0:T(8,128)(2,1)S(1)} %get-tuple-element.31), channel_id=1, source_target_pairs={{4,8},{12,16},{20,24},{28,32},{36,40},{44,48},{52,56},{60,64},{68,... | collective-permute-start | bytes 1572872 | tf_op jit(solution)/shard_map/ppermute | solution.py:280
  19.3 16.1 %collective-permute-start.3 = (bf16[512,1024]{1,0:T(8,128)(2,1)}, bf16[512,1024]{1,0:T(8,128)(2,1)S(1)}, u32[]{:S(2)}, u32[]{:S(2)}) collective-permute-start(bf16[512,1024]{1,0:T(8,128)(2,1)} %get-tuple-element.36), channel_id=1, source_target_pairs={{0,4},{8,12},{16,20},{24,28},{32,36},{40,44},{48,52},{56,60},{64,6... | collective-permute-start | bytes 3145736 | tf_op jit(solution)/shard_map/ppermute | solution.py:280
  19.4 17.8 %collective-permute-start.4 = (bf16[512,1024]{1,0:T(8,128)(2,1)}, bf16[512,1024]{1,0:T(8,128)(2,1)S(1)}, u32[]{:S(2)}, u32[]{:S(2)}) collective-permute-start(bf16[512,1024]{1,0:T(8,128)(2,1)} %get-tuple-element.37), channel_id=1, source_target_pairs={{4,8},{12,16},{20,24},{28,32},{36,40},{44,48},{52,56},{60,64},{68,... | collective-permute-start | bytes 3145736 | tf_op jit(solution)/shard_map/ppermute | solution.py:280
  23.7 18.2 %all-to-all-start = ((bf16[4,1,128,1024]{3,2,1,0:T(8,128)(2,1)}), bf16[4,1,128,1024]{3,2,1,0:T(8,128)(2,1)S(1)}, u32[]{:S(2)}, u32[]{:S(2)}) async-start(bf16[4,1,128,1024]{3,2,1,0:T(8,128)(2,1)} %bitcast.26), calls=%async_computation | async-start | bytes 2097152 | tf_op jit(solution)/shard_map/all_to_all | solution.py:341
  42.0 24.7 %all-to-all-start.1 = ((bf16[4,1,128,1536]{3,2,1,0:T(8,128)(2,1)}), bf16[4,1,128,1536]{3,2,1,0:T(8,128)(2,1)S(1)}, u32[]{:S(2)}, u32[]{:S(2)}) async-start(bf16[4,1,128,1536]{3,2,1,0:T(8,128)(2,1)} %bitcast.21), calls=%async_computation.1 | async-start | bytes 3145728 | tf_op jit(solution)/shard_map/all_to_all | solution.py:374
  45.7 21.2 %collective-permute-start = (f32[128,512]{1,0:T(8,128)S(1)}, f32[128,512]{1,0:T(8,128)S(1)}, u32[]{:S(2)}, u32[]{:S(2)}) collective-permute-start(f32[128,512]{1,0:T(8,128)S(1)} %get-tuple-element.23), channel_id=1, source_target_pairs={{0,4},{4,8},{8,12},{12,16},{16,20},{20,24},{24,28},{28,32},{32,36}... | collective-permute-start | bytes 786440 | tf_op jit(solution)/shard_map/ppermute | solution.py:286
  49.4 17.5 %collective-permute-start.5 = (f32[128,512]{1,0:T(8,128)S(1)}, f32[128,512]{1,0:T(8,128)S(1)}, u32[]{:S(2)}, u32[]{:S(2)}) collective-permute-start(f32[128,512]{1,0:T(8,128)S(1)} %get-tuple-element.38), channel_id=1, source_target_pairs={{4,0},{8,4},{12,8},{16,12},{20,16},{24,20},{28,24},{32,28},{36,32}... | collective-permute-start | bytes 786440 | tf_op jit(solution)/shard_map/ppermute | solution.py:286

commit v5 on v4

--- a/solution.py
+++ b/solution.py
@@ -7,6 +7,7 @@
 
 
 GHOST = 4
+OTHERS = (2, 1, 3)
 F32 = jnp.float32
 BF16 = jnp.bfloat16
 VMEM_LIMIT = 20 * 1024 * 1024
@@ -228,21 +229,26 @@
         middle[:, at] = dot_t(w_l, ap_l[:, at]) + dot_t(w_m, ap_m[:, at]) + dot_t(w_h, ap_h[:, at])
 
 
-def fourth_kernel(middle, pair, cross, near_hbm, near, s_o):
-    e = near.shape[0]
+def fourth_kernel(middle, pair, cross, own, *refs):
+    count = len(refs) // 2
+    outs, (*nears, s_o) = refs[:count], refs[count:]
+    b = own.shape[0]
+    e = pair.shape[0]
     one, two, three = (slice(c * e, (c + 1) * e) for c in range(3))
     even = is_even()
-
-    def send(i, at):
-        return pltpu.make_async_copy(near.at[:, at], near_hbm.at[:, at], s_o.at[i])
+    plane = lax.axis_index("plane")
 
     def join(below, above):
-        near[:, one] = (middle[:, one] + below[:, one].astype(F32)).astype(BF16)
-        send(0, one).start()
-        near[:, two] = (middle[:, two] + below[:, two].astype(F32) + above[:, one].astype(F32)).astype(BF16)
-        send(1, two).start()
-        near[:, three] = (middle[:, three] + above[:, two].astype(F32)).astype(BF16)
-        send(2, three).start()
+        for d in OTHERS + (0,):
+            rows = pl.ds(pl.multiple_of((plane ^ d) * b, b), b)
+            to = nears[OTHERS.index(d)] if d else own
+            to[:, one] = (middle[rows, one] + below[rows, one].astype(F32)).astype(to.dtype)
+            total = middle[rows, two] + below[rows, two].astype(F32) + above[rows, one].astype(F32)
+            to[:, two] = total.astype(to.dtype)
+            to[:, three] = (middle[rows, three] + above[rows, two].astype(F32)).astype(to.dtype)
+            if d:
+                k = OTHERS.index(d)
+                pltpu.make_async_copy(nears[k], outs[k], s_o.at[k]).start()
 
     @pl.when(even)
     def _():
@@ -252,8 +258,8 @@
     def _():
         join(pair, cross)
 
-    for i, at in enumerate((one, two, three)):
-        send(i, at).wait()
+    for k in range(count):
+        pltpu.make_async_copy(nears[k], outs[k], s_o.at[k]).wait()
 
 
 def summed_kernel(far, low, high):
@@ -361,22 +367,24 @@
         [scratch(1, 3)] * 4 + [scratch(3, 3), dma, dma, pltpu.SemaphoreType.DMA((4,))],
         56 * unit,
     )
-    near = run(
+    chunk = ((b, 3 * e), BF16)
+    own, *nears = run(
         fourth_kernel,
         (middle, pair, cross),
         [VMEM] * 3,
-        far_shape(1, 3),
-        HBM,
-        [scratch(1, 3), pltpu.SemaphoreType.DMA((3,))],
+        (pltpu.VMEM((b, 3 * e), F32),) + (pltpu.HBM(*chunk),) * len(OTHERS),
+        (VMEM,) + (HBM,) * len(OTHERS),
+        [pltpu.VMEM(*chunk)] * len(OTHERS) + [pltpu.SemaphoreType.DMA((len(OTHERS),))],
         e * 3 * e,
     )
-    near = near.reshape(coarse, 1, b, 3 * e)
-    near = lax.all_to_all(near, "plane", 0, 0, tiled=True)
+    got = []
+    for k, d in enumerate(OTHERS):
+        got.append(lax.ppermute(nears[k], "plane", [(q, q ^ d) for q in range(lax.axis_size("plane"))]))
     one = pltpu.VMEM((b, e), F32)
     low, high = run(summed_kernel, (far.reshape(coarse, b, 2 * e),), [VMEM], (one, one), (VMEM, VMEM), [], b * e * 8)
     far_low = passed_along(low, 1)
     far_high = passed_along(high, -1)
-    near = jnp.sum(near.astype(F32), axis=0)
+    near = (own + sum(x.astype(F32) for x in got))[None]
     return jnp.concatenate([far_low[None], near, far_high[None]], axis=2)[None]
 
 

time: 68.6 us -> 64.4 us (0.939)
  the two profiles are of different devices: /device:TPU:113 before, /device:TPU:29 now
where the time goes in v5:
time: 64.4 us; the launch traced here: 64 us
  starting transfers between devices  24.8 us (39%)
  Pallas kernels  22.4 us (35%)
  waiting for transfers between devices  14.1 us (22%)
  other arithmetic  1.39 us (2%)
  local copies, waits for them, and re-layouts  1.11 us (2%)
    pallas_call x6, Pallas kernels, run(): pl.pallas_call(body, in_specs=in_specs, out_specs=out_specs, out_shape=ou...  22.4 us
    ppermute x3, waiting for transfers between devices, steps(): lax.ppermute(nears[k], 'plane', [(q, q ^ d) for q in range(lax.axis_size(...  11.3 us
    ppermute x4, starting transfers between devices, swapped(): return lax.ppermute(shard, 'slab', pairs + [(j, i) for i, j in pairs])  10.8 us
    ppermute x2, starting transfers between devices, passed_along(): return lax.ppermute(shard, 'slab', pairs)  6.51 us
    all_to_all x1, starting transfers between devices, steps(): lax.all_to_all(far.reshape(coarse, 1, b, 2 * e), 'plane', 0, 0, tiled=True)  4.25 us
    ppermute x3, starting transfers between devices, steps(): lax.ppermute(nears[k], 'plane', [(q, q ^ d) for q in range(lax.axis_size(...  3.25 us
    ppermute x4, waiting for transfers between devices, swapped(): return lax.ppermute(shard, 'slab', pairs + [(j, i) for i, j in pairs])  2.79 us
  transfers between devices with their start and end apart: 10, of which 4 were waited for; matrix products, arithmetic and copies ran while one was open for 1% of the time, Pallas kernels for 25%

profile of v5, /device:TPU:29, one launch (start us, length us, event | category | flops | bytes accessed | tf_op | source)
XLA Modules:
  0.0 64.0 jit_solution(16767109846857290417)
XLA Ops:
  0.0 0.0 copy-start
  0.0 0.0 copy-start.3
  0.0 0.0 copy-start.4
  0.0 1.2 %shard_map.57 = (bf16[4,4,128,128]{3,2,1,0:T(8,128)(2,1)S(1)}, bf16[4,4,128,128]{3,2,1,0:T(8,128)(2,1)S(1)}) custom-call(bf16[12,4,128,128]{3,2,1,0:T(8,128)(2,1)} %bitcast.19), custom_call_target="tpu_custom_call" | custom-call | bytes 8388608 | tf_op jit(solution)/shard_map/pallas_call | solution.py:272
  1.3 0.8 %collective-permute-start.1 = (bf16[4,4,128,128]{3,2,1,0:T(8,128)(2,1)S(1)}, bf16[4,4,128,128]{3,2,1,0:T(8,128)(2,1)S(1)}, u32[]{:S(2)}, u32[]{:S(2)}) collective-permute-start(bf16[4,4,128,128]{3,2,1,0:T(8,128)(2,1)S(1)} %get-tuple-element.34), channel_id=1, source_target_pairs={{0,4},{8,12},{16,20},{24,28},{32,36},{40,44},{48,52},{56,60},{64,6... | collective-permute-start | bytes 1572872 | tf_op jit(solution)/shard_map/ppermute | solution.py:286
  2.0 3.4 %collective-permute-start.2 = (bf16[4,4,128,128]{3,2,1,0:T(8,128)(2,1)S(1)}, bf16[4,4,128,128]{3,2,1,0:T(8,128)(2,1)S(1)}, u32[]{:S(2)}, u32[]{:S(2)}) collective-permute-start(bf16[4,4,128,128]{3,2,1,0:T(8,128)(2,1)S(1)} %get-tuple-element.35), channel_id=1, source_target_pairs={{4,8},{12,16},{20,24},{28,32},{36,40},{44,48},{52,56},{60,64},{68,... | collective-permute-start | bytes 1572872 | tf_op jit(solution)/shard_map/ppermute | solution.py:286
  5.5 0.0 copy-done.3
  5.5 0.1 copy.12.acol
  5.6 0.0 copy-done.4
  5.6 0.1 copy.11
  5.7 0.0 copy-done
  5.7 0.1 fusion.1.rel
  5.8 7.0 %shard_map.55 = (bf16[512,512]{1,0:T(8,128)(2,1)S(1)}, bf16[512,512]{1,0:T(8,128)(2,1)S(1)}, bf16[512,512]{1,0:T(8,128)(2,1)S(1)}, bf16[512,512]{1,0:T(8,128)(2,...) custom-call(s32[12,7]{1,0:T(8,128)S(1)} %copy.12.acol, ...), custom_call_target="tpu_custom_call" | custom-call | flops 3221225472 | bytes 8388608 | tf_op jit(solution)/shard_map/pallas_call | solution.py:272
  12.8 0.0 collective-permute-done.1.pair
  12.9 0.0 collective-permute-done.2.cross
  12.9 5.2 %shard_map.58 = (bf16[512,1024]{1,0:T(8,128)(2,1)}, bf16[512,1024]{1,0:T(8,128)(2,1)}, bf16[512,1024]{1,0:T(8,128)(2,1)}, bf16[512,1024]{1,0:T(8,128)(2,1)}) custom-call(s32[4,20]{1,0:T(4,128)S(1)} %fusion.1.rel, s32[3,4]{1,0:T(4,128)S(1)} %pad_dynamic-slice_fusion.slots, bf16[512,512]{1,0:T(8,128)(2,1)S(1)} %get-tuple-element.28.ghost_l, ...), custom_call_target="tpu_custom_call" | custom-call | flops 2147483648 | bytes 8388608 | tf_op jit(solution)/shard_map/pallas_call | solution.py:272
  18.1 4.7 %collective-permute-start.3 = (bf16[512,1024]{1,0:T(8,128)(2,1)}, bf16[512,1024]{1,0:T(8,128)(2,1)S(1)}, u32[]{:S(2)}, u32[]{:S(2)}) collective-permute-start(bf16[512,1024]{1,0:T(8,128)(2,1)} %get-tuple-element.40), channel_id=1, source_target_pairs={{0,4},{8,12},{16,20},{24,28},{32,36},{40,44},{48,52},{56,60},{64,6... | collective-permute-start | bytes 3145736 | tf_op jit(solution)/shard_map/ppermute | solution.py:286
  22.8 1.9 %collective-permute-start.4 = (bf16[512,1024]{1,0:T(8,128)(2,1)}, bf16[512,1024]{1,0:T(8,128)(2,1)S(1)}, u32[]{:S(2)}, u32[]{:S(2)}) collective-permute-start(bf16[512,1024]{1,0:T(8,128)(2,1)} %get-tuple-element.41), channel_id=1, source_target_pairs={{4,8},{12,16},{20,24},{28,32},{36,40},{44,48},{52,56},{60,64},{68,... | collective-permute-start | bytes 3145736 | tf_op jit(solution)/shard_map/ppermute | solution.py:286
  24.7 4.2 %all-to-all-start = ((bf16[4,1,128,1024]{3,2,1,0:T(8,128)(2,1)}), bf16[4,1,128,1024]{3,2,1,0:T(8,128)(2,1)S(1)}, u32[]{:S(2)}, u32[]{:S(2)}) async-start(bf16[4,1,128,1024]{3,2,1,0:T(8,128)(2,1)} %bitcast.22), calls=%async_computation | async-start | bytes 2097152 | tf_op jit(solution)/shard_map/all_to_all | solution.py:347
  29.0 7.6 %shard_map.59.middle = f32[512,1536]{1,0:T(8,128)S(1)} custom-call(s32[12,7]{1,0:T(8,128)S(1)} %copy.12.acol, s32[4,20]{1,0:T(4,128)S(1)} %fusion.1.rel, s32[3,4]{1,0:T(4,128)S(1)} %pad_dynamic-slice_fusion.slots, bf16[12,7,128,128]{3,2,1,0:T(8,128)(2,1)} %bitcast.26, bf16[12,4,128,128]{3,2,1,0:T(8,128)(2,1)} %bitcast.21, ...), custom_call_target="tpu_custom_call" | custom-call | flops 3758096384 | bytes 8388608 | tf_op jit(solution)/shard_map/pallas_call | solution.py:272
  36.6 0.0 collective-permute-done.3.pair
  36.6 2.8 %collective-permute-done.4.cross = bf16[512,1024]{1,0:T(8,128)(2,1)S(1)} collective-permute-done((bf16[512,1024]{1,0:T(8,128)(2,1)}, bf16[512,1024]{1,0:T(8,128)(2,1)S(1)}, u32[]{:S(2)}, u32[]{:S(2)}) %collective-permute-start.4) | collective-permute-done | bytes 1048608 | tf_op jit(solution)/shard_map/ppermute | solution.py:286
  39.4 1.2 %shard_map.60 = (f32[128,1536]{1,0:T(8,128)S(1)}, bf16[128,1536]{1,0:T(8,128)(2,1)}, bf16[128,1536]{1,0:T(8,128)(2,1)}, bf16[128,1536]{1,0:T(8,128)(2,1)}) custom-call(f32[512,1536]{1,0:T(8,128)S(1)} %shard_map.59.middle, bf16[512,1024]{1,0:T(8,128)(2,1)S(1)} %collective-permute-done.3.pair, bf16[512,1024]{1,0:T(8,128)(2,1)S(1)} %collective-permute-done.4.cross), custom_call_target="tpu_custom_call" | custom-call | flops 786432 | bytes 8388608 | tf_op jit(solution)/shard_map/pallas_call | solution.py:272
  40.6 0.0 copy-start.1
  40.6 0.9 %copy-done.1 = f32[128,1536]{1,0:T(8,128)} copy-done((f32[128,1536]{1,0:T(8,128)}, f32[128,1536]{1,0:T(8,128)S(1)}, u32[]{:S(2)}) %copy-start.1) | copy-done | bytes 786456
  41.5 0.0 copy-start.2
  41.5 0.2 collective-permute-start.5
  41.7 1.8 %collective-permute-start.6 = (bf16[128,1536]{1,0:T(8,128)(2,1)}, bf16[128,1536]{1,0:T(8,128)(2,1)S(1)}, u32[]{:S(2)}, u32[]{:S(2)}) collective-permute-start(bf16[128,1536]{1,0:T(8,128)(2,1)} %get-tuple-element.44), channel_id=1, source_target_pairs={{0,1},{1,0},{2,3},{3,2},{4,5},{5,4},{6,7},{7,6},{8,9},{9,8},{10,11... | collective-permute-start | bytes 1179656 | tf_op jit(solution)/shard_map/ppermute | solution.py:382
  43.5 1.2 %collective-permute-start.7 = (bf16[128,1536]{1,0:T(8,128)(2,1)}, bf16[128,1536]{1,0:T(8,128)(2,1)S(1)}, u32[]{:S(2)}, u32[]{:S(2)}) collective-permute-start(bf16[128,1536]{1,0:T(8,128)(2,1)} %get-tuple-element.45), channel_id=1, source_target_pairs={{0,3},{1,2},{2,1},{3,0},{4,7},{5,6},{6,5},{7,4},{8,11},{9,10},{10,... | collective-permute-start | bytes 1179656 | tf_op jit(solution)/shard_map/ppermute | solution.py:382
  44.7 0.0 all-to-all-done
  44.7 0.1 shard_map.56
  44.8 2.5 %collective-permute-start = (f32[128,512]{1,0:T(8,128)S(1)}, f32[128,512]{1,0:T(8,128)S(1)}, u32[]{:S(2)}, u32[]{:S(2)}) collective-permute-start(f32[128,512]{1,0:T(8,128)S(1)} %get-tuple-element.27), channel_id=1, source_target_pairs={{0,4},{4,8},{8,12},{12,16},{16,20},{20,24},{24,28},{28,32},{32,36}... | collective-permute-start | bytes 786440 | tf_op jit(solution)/shard_map/ppermute | solution.py:292
  47.3 4.0 %collective-permute-start.8 = (f32[128,512]{1,0:T(8,128)S(1)}, f32[128,512]{1,0:T(8,128)S(1)}, u32[]{:S(2)}, u32[]{:S(2)}) collective-permute-start(f32[128,512]{1,0:T(8,128)S(1)} %get-tuple-element.46), channel_id=1, source_target_pairs={{4,0},{8,4},{12,8},{16,12},{20,16},{24,20},{28,24},{32,28},{36,32}... | collective-permute-start | bytes 786440 | tf_op jit(solution)/shard_map/ppermute | solution.py:292
  51.4 0.7 %collective-permute-done.5 = bf16[128,1536]{1,0:T(8,128)(2,1)S(1)} collective-permute-done((bf16[128,1536]{1,0:T(8,128)(2,1)}, bf16[128,1536]{1,0:T(8,128)(2,1)S(1)}, u32[]{:S(2)}, u32[]{:S(2)}) %collective-permute-start.5) | collective-permute-done | bytes 393248 | tf_op jit(solution)/shard_map/ppermute | solution.py:382
  52.1 7.5 %collective-permute-done.6 = bf16[128,1536]{1,0:T(8,128)(2,1)S(1)} collective-permute-done((bf16[128,1536]{1,0:T(8,128)(2,1)}, bf16[128,1536]{1,0:T(8,128)(2,1)S(1)}, u32[]{:S(2)}, u32[]{:S(2)}) %collective-permute-start.6) | collective-permute-done | bytes 393248 | tf_op jit(solution)/shard_map/ppermute | solution.py:382
  59.5 3.1 %collective-permute-done.7 = bf16[128,1536]{1,0:T(8,128)(2,1)S(1)} collective-permute-done((bf16[128,1536]{1,0:T(8,128)(2,1)}, bf16[128,1536]{1,0:T(8,128)(2,1)S(1)}, u32[]{:S(2)}, u32[]{:S(2)}) %collective-permute-start.7) | collective-permute-done | bytes 393248 | tf_op jit(solution)/shard_map/ppermute | solution.py:382
  62.6 0.0 copy-done.2
  62.6 0.2 add_bitcast_fusion
  62.8 0.0 collective-permute-done
  62.8 0.0 collective-permute-done.8
  62.8 1.1 %maximum_bitcast_fusion = f32[1,1,128,2560]{3,2,1,0:T(8,128)} fusion(f32[1,128,512]{2,1,0:T(8,128)S(1)} %bitcast.24, f32[1,128,1536]{2,1,0:T(8,128)S(1)} %add_bitcast_fusion, f32[1,128,512]{2,1,0:T(8,128)S(1)} %bitcast.23), kind=kLoop, calls=%fused_computation | loop fusion | flops 655360 | bytes 2621440 | tf_op jit(solution)/shard_map/broadcast_in_dim | solution.py:388
  (3 shorter events, 0.0 us)
Async XLA Ops:
  0.0 5.7 %copy-start = (s32[4,768,4]{1,2,0:T(4,128)S(1)}, s32[4,768,4]{1,2,0:T(4,128)}, u32[]{:S(2)}) copy-start(s32[4,768,4]{1,2,0:T(4,128)} %param.8) | copy-start | bytes 147460
  0.0 5.5 %copy-start.3 = (s32[1,12,7]{1,0,2:T(1,128)S(1)}, s32[1,12,7]{1,0,2:T(1,128)}, u32[]{:S(2)}) copy-start(s32[1,12,7]{1,0,2:T(1,128)} %param.6) | copy-start | bytes 1012
  0.0 5.6 %copy-start.4 = (s32[64,4]{0,1:T(4,128)S(1)}, s32[64,4]{0,1:T(4,128)}, u32[]{:S(2)}) copy-start(s32[64,4]{0,1:T(4,128)} %param.9) | copy-start | bytes 3076
  1.3 11.6 %collective-permute-start.1 = (bf16[4,4,128,128]{3,2,1,0:T(8,128)(2,1)S(1)}, bf16[4,4,128,128]{3,2,1,0:T(8,128)(2,1)S(1)}, u32[]{:S(2)}, u32[]{:S(2)}) collective-permute-start(bf16[4,4,128,128]{3,2,1,0:T(8,128)(2,1)S(1)} %get-tuple-element.34), channel_id=1, source_target_pairs={{0,4},{8,12},{16,20},{24,28},{32,36},{40,44},{48,52},{56,60},{64,6... | collective-permute-start | bytes 1572872 | tf_op jit(solution)/shard_map/ppermute | solution.py:286
  2.0 10.8 %collective-permute-start.2 = (bf16[4,4,128,128]{3,2,1,0:T(8,128)(2,1)S(1)}, bf16[4,4,128,128]{3,2,1,0:T(8,128)(2,1)S(1)}, u32[]{:S(2)}, u32[]{:S(2)}) collective-permute-start(bf16[4,4,128,128]{3,2,1,0:T(8,128)(2,1)S(1)} %get-tuple-element.35), channel_id=1, source_target_pairs={{4,8},{12,16},{20,24},{28,32},{36,40},{44,48},{52,56},{60,64},{68,... | collective-permute-start | bytes 1572872 | tf_op jit(solution)/shard_map/ppermute | solution.py:286
  18.1 18.5 %collective-permute-start.3 = (bf16[512,1024]{1,0:T(8,128)(2,1)}, bf16[512,1024]{1,0:T(8,128)(2,1)S(1)}, u32[]{:S(2)}, u32[]{:S(2)}) collective-permute-start(bf16[512,1024]{1,0:T(8,128)(2,1)} %get-tuple-element.40), channel_id=1, source_target_pairs={{0,4},{8,12},{16,20},{24,28},{32,36},{40,44},{48,52},{56,60},{64,6... | collective-permute-start | bytes 3145736 | tf_op jit(solution)/shard_map/ppermute | solution.py:286
  22.8 16.6 %collective-permute-start.4 = (bf16[512,1024]{1,0:T(8,128)(2,1)}, bf16[512,1024]{1,0:T(8,128)(2,1)S(1)}, u32[]{:S(2)}, u32[]{:S(2)}) collective-permute-start(bf16[512,1024]{1,0:T(8,128)(2,1)} %get-tuple-element.41), channel_id=1, source_target_pairs={{4,8},{12,16},{20,24},{28,32},{36,40},{44,48},{52,56},{60,64},{68,... | collective-permute-start | bytes 3145736 | tf_op jit(solution)/shard_map/ppermute | solution.py:286
  24.7 20.0 %all-to-all-start = ((bf16[4,1,128,1024]{3,2,1,0:T(8,128)(2,1)}), bf16[4,1,128,1024]{3,2,1,0:T(8,128)(2,1)S(1)}, u32[]{:S(2)}, u32[]{:S(2)}) async-start(bf16[4,1,128,1024]{3,2,1,0:T(8,128)(2,1)} %bitcast.22), calls=%async_computation | async-start | bytes 2097152 | tf_op jit(solution)/shard_map/all_to_all | solution.py:347
  40.6 0.9 %copy-start.1 = (f32[128,1536]{1,0:T(8,128)}, f32[128,1536]{1,0:T(8,128)S(1)}, u32[]{:S(2)}) copy-start(f32[128,1536]{1,0:T(8,128)S(1)} %get-tuple-element.42) | copy-start | bytes 2359300
  41.5 21.2 %copy-start.2 = (f32[128,1536]{1,0:T(8,128)S(1)}, f32[128,1536]{1,0:T(8,128)}, u32[]{:S(2)}) copy-start(f32[128,1536]{1,0:T(8,128)} %copy-done.1) | copy-start | bytes 2359300
  41.5 10.6 %collective-permute-start.5 = (bf16[128,1536]{1,0:T(8,128)(2,1)}, bf16[128,1536]{1,0:T(8,128)(2,1)S(1)}, u32[]{:S(2)}, u32[]{:S(2)}) collective-permute-start(bf16[128,1536]{1,0:T(8,128)(2,1)} %get-tuple-element.43), channel_id=1, source_target_pairs={{0,2},{1,3},{2,0},{3,1},{4,6},{5,7},{6,4},{7,5},{8,10},{9,11},{10,... | collective-permute-start | bytes 1179656 | tf_op jit(solution)/shard_map/ppermute | solution.py:382
  41.7 17.9 %collective-permute-start.6 = (bf16[128,1536]{1,0:T(8,128)(2,1)}, bf16[128,1536]{1,0:T(8,128)(2,1)S(1)}, u32[]{:S(2)}, u32[]{:S(2)}) collective-permute-start(bf16[128,1536]{1,0:T(8,128)(2,1)} %get-tuple-element.44), channel_id=1, source_target_pairs={{0,1},{1,0},{2,3},{3,2},{4,5},{5,4},{6,7},{7,6},{8,9},{9,8},{10,11... | collective-permute-start | bytes 1179656 | tf_op jit(solution)/shard_map/ppermute | solution.py:382
  43.5 19.1 %collective-permute-start.7 = (bf16[128,1536]{1,0:T(8,128)(2,1)}, bf16[128,1536]{1,0:T(8,128)(2,1)S(1)}, u32[]{:S(2)}, u32[]{:S(2)}) collective-permute-start(bf16[128,1536]{1,0:T(8,128)(2,1)} %get-tuple-element.45), channel_id=1, source_target_pairs={{0,3},{1,2},{2,1},{3,0},{4,7},{5,6},{6,5},{7,4},{8,11},{9,10},{10,... | collective-permute-start | bytes 1179656 | tf_op jit(solution)/shard_map/ppermute | solution.py:382
  44.8 18.0 %collective-permute-start = (f32[128,512]{1,0:T(8,128)S(1)}, f32[128,512]{1,0:T(8,128)S(1)}, u32[]{:S(2)}, u32[]{:S(2)}) collective-permute-start(f32[128,512]{1,0:T(8,128)S(1)} %get-tuple-element.27), channel_id=1, source_target_pairs={{0,4},{4,8},{8,12},{12,16},{16,20},{20,24},{24,28},{28,32},{32,36}... | collective-permute-start | bytes 786440 | tf_op jit(solution)/shard_map/ppermute | solution.py:292
  47.3 15.5 %collective-permute-start.8 = (f32[128,512]{1,0:T(8,128)S(1)}, f32[128,512]{1,0:T(8,128)S(1)}, u32[]{:S(2)}, u32[]{:S(2)}) collective-permute-start(f32[128,512]{1,0:T(8,128)S(1)} %get-tuple-element.46), channel_id=1, source_target_pairs={{4,0},{8,4},{12,8},{16,12},{20,16},{24,20},{28,24},{32,28},{36,32}... | collective-permute-start | bytes 786440 | tf_op jit(solution)/shard_map/ppermute | solution.py:292

commit v6 on v5

--- a/solution.py
+++ b/solution.py
@@ -79,10 +79,12 @@
 
 
 def first_kernel(
-    acol, rel, slots, a_hbm, p_hbm, ghost_l, ghost_h, corner_l, corner_h, own_l, own_h, h0_hbm, l2_hbm, far_hbm,
-    a_l, a_h, w, h0_v, l2_v, far, s_p, s_m, s_h, s_l, s_o,
+    acol, rel, slots, a_hbm, p_hbm, ghost_l, ghost_h, corner_l, corner_h, own_l, own_h, h0_hbm, l2_hbm, *rest,
 ):
+    fars, (a_l, a_h, w, h0_v, l2_v, far, s_p, s_m, s_h, s_l, s_o) = rest[:-11], rest[-11:]
     e = far.shape[0]
+    b = fars[0].shape[0]
+    plane = lax.axis_index("plane")
     g = GHOST
     one, two = slice(0, e), slice(e, 2 * e)
     outs = []
@@ -90,6 +92,10 @@
     def send(src, dst):
         outs.append(pltpu.make_async_copy(src, dst, s_o.at[len(outs)]))
         outs[-1].start()
+
+    def send_far(at):
+        for d, dst in zip((0,) + OTHERS, fars):
+            send(far.at[pl.ds(pl.multiple_of((plane ^ d) * b, b), b), at], dst.at[:, at])
 
     clear(w.at[0:e, 0 : 2 * e])
     start_w(rel, slots, p_hbm.at[0:g], w, range(g, 2 * g), g, 0, 2 * g, s_p)
@@ -107,12 +113,12 @@
     h0_v[...] = dot(a_h[:, 0:e], low).astype(BF16)
     send(h0_v, h0_hbm)
     far[:, one] = dot_t(high, h0_v[...]).astype(BF16)
-    send(far.at[:, one], far_hbm.at[:, one])
+    send_far(one)
     wait_all(a_hbm.at[0:g], s_l)
     l2_v[...] = dot(a_l[:, 3 * e : 4 * e], high).astype(BF16)
     send(l2_v, l2_hbm)
     far[:, two] = dot_t(low, l2_v[...]).astype(BF16)
-    send(far.at[:, two], far_hbm.at[:, two])
+    send_far(two)
     corner_l[...] = low
     corner_h[...] = high
     ghost_l[...] = a_l[:, 0:e]
@@ -262,10 +268,11 @@
         pltpu.make_async_copy(nears[k], outs[k], s_o.at[k]).wait()
 
 
-def summed_kernel(far, low, high):
+def summed_kernel(*refs):
+    *fars, low, high = refs
     e = low.shape[1]
-    low[...] = sum(far[q, :, 0:e].astype(F32) for q in range(far.shape[0]))
-    high[...] = sum(far[q, :, e : 2 * e].astype(F32) for q in range(far.shape[0]))
+    low[...] = sum(far[:, 0:e].astype(F32) for far in fars)
+    high[...] = sum(far[:, e : 2 * e].astype(F32) for far in fars)
 
 
 def run(body, ins, in_specs, outs, out_specs, scratch, flops):
@@ -284,6 +291,10 @@
     count = lax.axis_size("slab")
     pairs = [(i, i + 1) for i in range(first, count - 1, 2)]
     return lax.ppermute(shard, "slab", pairs + [(j, i) for i, j in pairs])
+
+
+def over_planes(shard, d):
+    return lax.ppermute(shard, "plane", [(q, q ^ d) for q in range(lax.axis_size("plane"))])
 
 
 def passed_along(shard, by):
@@ -333,22 +344,23 @@
         return pltpu.VMEM((rows * e, cols * e), BF16)
 
     dma = pltpu.SemaphoreType.DMA(())
-    *kept, ap_h0, ap_l2, far = run(
+    ghost_l, ghost_h, corner_l, corner_h, own_l, own_h, ap_h0, ap_l2, *fars = run(
         first_kernel,
         (acol, rel, slots, a, p_here),
         [SMEM, SMEM, SMEM, HBM, HBM],
-        (shape(1, 1),) * 4 + (shape(1, 2, F32),) * 2 + (far_shape(1, 1), far_shape(1, 1), far_shape(1, 2)),
-        (VMEM,) * 6 + (HBM,) * 3,
+        (shape(1, 1),) * 4 + (shape(1, 2, F32),) * 2 + (far_shape(1, 1), far_shape(1, 1)) + (pltpu.HBM((b, 2 * e), BF16),) * (1 + len(OTHERS)),
+        (VMEM,) * 6 + (HBM,) * (3 + len(OTHERS)),
         [scratch(1, 4), scratch(1, 4), scratch(3, 3), scratch(1, 1), scratch(1, 1), scratch(1, 2)]
         + [dma] * 4
-        + [pltpu.SemaphoreType.DMA((4,))],
+        + [pltpu.SemaphoreType.DMA((2 + 2 * (1 + len(OTHERS)),))],
         48 * unit,
     )
-    far = lax.all_to_all(far.reshape(coarse, 1, b, 2 * e), "plane", 0, 0, tiled=True)
+    for k, d in enumerate(OTHERS):
+        fars[1 + k] = over_planes(fars[1 + k], d)
     pair, cross = (pltpu.with_memory_space_constraint(x, pltpu.VMEM) for x in (pair, cross))
     ap_l, ap_h, pair, cross = run(
         second_kernel,
-        (rel, slots, *kept, pair, cross),
+        (rel, slots, ghost_l, ghost_h, corner_l, corner_h, own_l, own_h, pair, cross),
         [SMEM, SMEM] + [VMEM] * 8,
         (far_shape(1, 2),) * 4,
         (HBM,) * 4,
@@ -379,9 +391,9 @@
     )
     got = []
     for k, d in enumerate(OTHERS):
-        got.append(lax.ppermute(nears[k], "plane", [(q, q ^ d) for q in range(lax.axis_size("plane"))]))
+        got.append(over_planes(nears[k], d))
     one = pltpu.VMEM((b, e), F32)
-    low, high = run(summed_kernel, (far.reshape(coarse, b, 2 * e),), [VMEM], (one, one), (VMEM, VMEM), [], b * e * 8)
+    low, high = run(summed_kernel, tuple(fars), [VMEM] * len(fars), (one, one), (VMEM, VMEM), [], b * e * 8)
     far_low = passed_along(low, 1)
     far_high = passed_along(high, -1)
     near = (own + sum(x.astype(F32) for x in got))[None]

time: 64.4 us -> 80.6 us (1.25)
  the two profiles are of different devices: /device:TPU:29 before, /device:TPU:113 now
where the time goes in v6:
time: 80.6 us; the launch traced here: 79.2 us
  waiting for transfers between devices  29.7 us (37%)
  starting transfers between devices  25.2 us (31%)
  Pallas kernels  22.4 us (28%)
  other arithmetic  1.39 us (2%)
    pallas_call x6, Pallas kernels, run(): pl.pallas_call(body, in_specs=in_specs, out_specs=out_specs, out_shape=ou...  22.4 us
    ppermute x6, waiting for transfers between devices, over_planes(): lax.ppermute(shard, 'plane', [(q, q ^ d) for q in range(lax.axis_size('pl...  20.4 us
    ppermute x4, starting transfers between devices, swapped(): return lax.ppermute(shard, 'slab', pairs + [(j, i) for i, j in pairs])  9.79 us
    ppermute x6, starting transfers between devices, over_planes(): lax.ppermute(shard, 'plane', [(q, q ^ d) for q in range(lax.axis_size('pl...  9.36 us
    ppermute x2, waiting for transfers between devices, passed_along(): return lax.ppermute(shard, 'slab', pairs)  6.77 us
    ppermute x2, starting transfers between devices, passed_along(): return lax.ppermute(shard, 'slab', pairs)  6.04 us
    ppermute x4, waiting for transfers between devices, swapped(): return lax.ppermute(shard, 'slab', pairs + [(j, i) for i, j in pairs])  2.55 us
  transfers between devices with their start and end apart: 12, of which 4 were waited for; matrix products, arithmetic and copies ran while one was open for 1% of the time, Pallas kernels for 20%

profile of v6, /device:TPU:113, one launch (start us, length us, event | category | flops | bytes accessed | tf_op | source)
XLA Modules:
  0.0 79.2 jit_solution(2708117436471015693)
XLA Ops:
  0.0 0.0 copy-start
  0.0 0.0 copy-start.2
  0.0 1.2 %shard_map.57 = (bf16[4,4,128,128]{3,2,1,0:T(8,128)(2,1)S(1)}, bf16[4,4,128,128]{3,2,1,0:T(8,128)(2,1)S(1)}) custom-call(bf16[12,4,128,128]{3,2,1,0:T(8,128)(2,1)} %bitcast.14), custom_call_target="tpu_custom_call" | custom-call | bytes 8388608 | tf_op jit(solution)/shard_map/pallas_call | solution.py:279
  1.3 0.8 collective-permute-start.4
  2.0 4.7 %collective-permute-start.5 = (bf16[4,4,128,128]{3,2,1,0:T(8,128)(2,1)S(1)}, bf16[4,4,128,128]{3,2,1,0:T(8,128)(2,1)S(1)}, u32[]{:S(2)}, u32[]{:S(2)}) collective-permute-start(bf16[4,4,128,128]{3,2,1,0:T(8,128)(2,1)S(1)} %get-tuple-element.41), channel_id=1, source_target_pairs={{4,8},{12,16},{20,24},{28,32},{36,40},{44,48},{52,56},{60,64},{68,... | collective-permute-start | bytes 1572872 | tf_op jit(solution)/shard_map/ppermute | solution.py:293
  6.7 0.0 copy-done.2
  6.7 0.1 copy.8.acol
  6.8 0.0 copy-done.3
  6.8 0.1 copy.7
  6.9 0.0 copy-done
  7.0 0.1 fusion.1.rel
  7.0 7.1 %shard_map.55 = (bf16[512,512]{1,0:T(8,128)(2,1)S(1)}, bf16[512,512]{1,0:T(8,128)(2,1)S(1)}, bf16[512,512]{1,0:T(8,128)(2,1)S(1)}, bf16[512,512]{1,0:T(8,128)(2,...) custom-call(s32[12,7]{1,0:T(8,128)S(1)} %copy.8.acol, ...), custom_call_target="tpu_custom_call" | custom-call | flops 3221225472 | bytes 8388608 | tf_op jit(solution)/shard_map/pallas_call | solution.py:279
  14.1 0.0 collective-permute-done.4.pair
  14.1 0.0 collective-permute-done.5.cross
  14.1 0.0 copy-start.6
  14.2 5.2 %shard_map.58 = (bf16[512,1024]{1,0:T(8,128)(2,1)}, bf16[512,1024]{1,0:T(8,128)(2,1)}, bf16[512,1024]{1,0:T(8,128)(2,1)}, bf16[512,1024]{1,0:T(8,128)(2,1)}) custom-call(s32[4,20]{1,0:T(4,128)S(1)} %fusion.1.rel, s32[3,4]{1,0:T(4,128)S(1)} %pad_dynamic-slice_fusion.slots, bf16[512,512]{1,0:T(8,128)(2,1)S(1)} %get-tuple-element.34.ghost_l, ...), custom_call_target="tpu_custom_call" | custom-call | flops 2147483648 | bytes 8388608 | tf_op jit(solution)/shard_map/pallas_call | solution.py:279
  19.4 0.1 collective-permute-start.6
  19.5 4.3 %collective-permute-start.7 = (bf16[512,1024]{1,0:T(8,128)(2,1)}, bf16[512,1024]{1,0:T(8,128)(2,1)S(1)}, u32[]{:S(2)}, u32[]{:S(2)}) collective-permute-start(bf16[512,1024]{1,0:T(8,128)(2,1)} %get-tuple-element.47), channel_id=1, source_target_pairs={{4,8},{12,16},{20,24},{28,32},{36,40},{44,48},{52,56},{60,64},{68,... | collective-permute-start | bytes 3145736 | tf_op jit(solution)/shard_map/ppermute | solution.py:293
  23.8 0.0 copy-done.6
  23.8 3.0 %collective-permute-start = (bf16[128,1024]{1,0:T(8,128)(2,1)S(1)}, bf16[128,1024]{1,0:T(8,128)(2,1)S(1)}, u32[]{:S(2)}, u32[]{:S(2)}) collective-permute-start(bf16[128,1024]{1,0:T(8,128)(2,1)S(1)} %copy-done.6), channel_id=1, source_target_pairs={{0,2},{1,3},{2,0},{3,1},{4,6},{5,7},{6,4},{7,5},{8,10},{9,11},{10,... | collective-permute-start | bytes 786440 | tf_op jit(solution)/shard_map/ppermute | solution.py:297
  26.8 7.6 %shard_map.59.middle = f32[512,1536]{1,0:T(8,128)S(1)} custom-call(s32[12,7]{1,0:T(8,128)S(1)} %copy.8.acol, s32[4,20]{1,0:T(4,128)S(1)} %fusion.1.rel, s32[3,4]{1,0:T(4,128)S(1)} %pad_dynamic-slice_fusion.slots, bf16[12,7,128,128]{3,2,1,0:T(8,128)(2,1)} %bitcast.20, bf16[12,4,128,128]{3,2,1,0:T(8,128)(2,1)} %bitcast.16, ...), custom_call_target="tpu_custom_call" | custom-call | flops 3758096384 | bytes 8388608 | tf_op jit(solution)/shard_map/pallas_call | solution.py:279
  34.4 0.0 copy-start.5
  34.4 0.0 copy-start.4
  34.5 0.0 copy-start.1
  34.5 0.0 collective-permute-done.6.pair
  34.5 2.5 %collective-permute-done.7.cross = bf16[512,1024]{1,0:T(8,128)(2,1)S(1)} collective-permute-done((bf16[512,1024]{1,0:T(8,128)(2,1)}, bf16[512,1024]{1,0:T(8,128)(2,1)S(1)}, u32[]{:S(2)}, u32[]{:S(2)}) %collective-permute-start.7) | collective-permute-done | bytes 1048608 | tf_op jit(solution)/shard_map/ppermute | solution.py:293
  37.0 1.1 %shard_map.60 = (f32[128,1536]{1,0:T(8,128)S(1)}, bf16[128,1536]{1,0:T(8,128)(2,1)}, bf16[128,1536]{1,0:T(8,128)(2,1)}, bf16[128,1536]{1,0:T(8,128)(2,1)}) custom-call(f32[512,1536]{1,0:T(8,128)S(1)} %shard_map.59.middle, bf16[512,1024]{1,0:T(8,128)(2,1)S(1)} %collective-permute-done.6.pair, bf16[512,1024]{1,0:T(8,128)(2,1)S(1)} %collective-permute-done.7.cross), custom_call_target="tpu_custom_call" | custom-call | flops 786432 | bytes 8388608 | tf_op jit(solution)/shard_map/pallas_call | solution.py:279
  38.1 2.8 %collective-permute-start.8 = (bf16[128,1536]{1,0:T(8,128)(2,1)}, bf16[128,1536]{1,0:T(8,128)(2,1)S(1)}, u32[]{:S(2)}, u32[]{:S(2)}) collective-permute-start(bf16[128,1536]{1,0:T(8,128)(2,1)} %get-tuple-element.49), channel_id=1, source_target_pairs={{0,2},{1,3},{2,0},{3,1},{4,6},{5,7},{6,4},{7,5},{8,10},{9,11},{10,... | collective-permute-start | bytes 1179656 | tf_op jit(solution)/shard_map/ppermute | solution.py:297
  41.0 0.3 collective-permute-start.9
  41.3 0.6 collective-permute-start.10
  41.8 0.0 copy-done.5
  41.8 0.9 %collective-permute-start.1 = (bf16[128,1024]{1,0:T(8,128)(2,1)S(1)}, bf16[128,1024]{1,0:T(8,128)(2,1)S(1)}, u32[]{:S(2)}, u32[]{:S(2)}) collective-permute-start(bf16[128,1024]{1,0:T(8,128)(2,1)S(1)} %copy-done.5), channel_id=1, source_target_pairs={{0,1},{1,0},{2,3},{3,2},{4,5},{5,4},{6,7},{7,6},{8,9},{9,8},{10,11... | collective-permute-start | bytes 786440 | tf_op jit(solution)/shard_map/ppermute | solution.py:297
  42.7 0.0 collective-permute-done.refs_1_
  42.7 0.0 copy-done.4
  42.7 1.8 %collective-permute-start.2 = (bf16[128,1024]{1,0:T(8,128)(2,1)S(1)}, bf16[128,1024]{1,0:T(8,128)(2,1)S(1)}, u32[]{:S(2)}, u32[]{:S(2)}) collective-permute-start(bf16[128,1024]{1,0:T(8,128)(2,1)S(1)} %copy-done.4), channel_id=1, source_target_pairs={{0,3},{1,2},{2,1},{3,0},{4,7},{5,6},{6,5},{7,4},{8,11},{9,10},{10,... | collective-permute-start | bytes 786440 | tf_op jit(solution)/shard_map/ppermute | solution.py:297
  44.5 20.3 %collective-permute-done.1.refs_2_ = bf16[128,1024]{1,0:T(8,128)(2,1)S(1)} collective-permute-done((bf16[128,1024]{1,0:T(8,128)(2,1)S(1)}, bf16[128,1024]{1,0:T(8,128)(2,1)S(1)}, u32[]{:S(2)}, u32[]{:S(2)}) %collective-permute-start.1) | collective-permute-done | bytes 262176 | tf_op jit(solution)/shard_map/ppermute | solution.py:297
  64.9 0.0 collective-permute-done.2.refs_3_
  64.9 0.0 copy-done.1
  64.9 0.1 shard_map.56
  65.0 4.1 %collective-permute-start.3 = (f32[128,512]{1,0:T(8,128)S(1)}, f32[128,512]{1,0:T(8,128)S(1)}, u32[]{:S(2)}, u32[]{:S(2)}) collective-permute-start(f32[128,512]{1,0:T(8,128)S(1)} %get-tuple-element.33), channel_id=1, source_target_pairs={{0,4},{4,8},{8,12},{12,16},{16,20},{20,24},{24,28},{28,32},{32,36}... | collective-permute-start | bytes 786440 | tf_op jit(solution)/shard_map/ppermute | solution.py:303
  69.1 1.9 %collective-permute-start.11 = (f32[128,512]{1,0:T(8,128)S(1)}, f32[128,512]{1,0:T(8,128)S(1)}, u32[]{:S(2)}, u32[]{:S(2)}) collective-permute-start(f32[128,512]{1,0:T(8,128)S(1)} %get-tuple-element.52), channel_id=1, source_target_pairs={{4,0},{8,4},{12,8},{16,12},{20,16},{24,20},{28,24},{32,28},{36,32}... | collective-permute-start | bytes 786440 | tf_op jit(solution)/shard_map/ppermute | solution.py:303
  71.1 0.0 collective-permute-done.8
  71.1 0.0 collective-permute-done.9
  71.1 0.0 collective-permute-done.10
  71.1 0.2 add_bitcast_fusion
  71.3 1.2 %collective-permute-done.3 = f32[128,512]{1,0:T(8,128)S(1)} collective-permute-done((f32[128,512]{1,0:T(8,128)S(1)}, f32[128,512]{1,0:T(8,128)S(1)}, u32[]{:S(2)}, u32[]{:S(2)}) %collective-permute-start.3) | collective-permute-done | bytes 262176 | tf_op jit(solution)/shard_map/ppermute | solution.py:303
  72.4 5.6 %collective-permute-done.11 = f32[128,512]{1,0:T(8,128)S(1)} collective-permute-done((f32[128,512]{1,0:T(8,128)S(1)}, f32[128,512]{1,0:T(8,128)S(1)}, u32[]{:S(2)}, u32[]{:S(2)}) %collective-permute-start.11) | collective-permute-done | bytes 262176 | tf_op jit(solution)/shard_map/ppermute | solution.py:303
  78.0 1.1 %maximum_bitcast_fusion = f32[1,1,128,2560]{3,2,1,0:T(8,128)} fusion(f32[1,128,512]{2,1,0:T(8,128)S(1)} %bitcast.18, f32[1,128,1536]{2,1,0:T(8,128)S(1)} %add_bitcast_fusion, f32[1,128,512]{2,1,0:T(8,128)S(1)} %bitcast.17), kind=kLoop, calls=%fused_computation | loop fusion | flops 655360 | bytes 2621440 | tf_op jit(solution)/shard_map/broadcast_in_dim | solution.py:400
  (4 shorter events, 0.0 us)
Async XLA Ops:
  0.0 6.9 %copy-start = (s32[4,768,4]{1,2,0:T(4,128)S(1)}, s32[4,768,4]{1,2,0:T(4,128)}, u32[]{:S(2)}) copy-start(s32[4,768,4]{1,2,0:T(4,128)} %param.8) | copy-start | bytes 147460
  0.0 6.7 %copy-start.2 = (s32[1,12,7]{1,0,2:T(1,128)S(1)}, s32[1,12,7]{1,0,2:T(1,128)}, u32[]{:S(2)}) copy-start(s32[1,12,7]{1,0,2:T(1,128)} %param.6) | copy-start | bytes 1012
  0.0 6.8 %copy-start.3 = (s32[64,4]{0,1:T(4,128)S(1)}, s32[64,4]{0,1:T(4,128)}, u32[]{:S(2)}) copy-start(s32[64,4]{0,1:T(4,128)} %param.9) | copy-start | bytes 3076
  1.3 12.9 %collective-permute-start.4 = (bf16[4,4,128,128]{3,2,1,0:T(8,128)(2,1)S(1)}, bf16[4,4,128,128]{3,2,1,0:T(8,128)(2,1)S(1)}, u32[]{:S(2)}, u32[]{:S(2)}) collective-permute-start(bf16[4,4,128,128]{3,2,1,0:T(8,128)(2,1)S(1)} %get-tuple-element.40), channel_id=1, source_target_pairs={{0,4},{8,12},{16,20},{24,28},{32,36},{40,44},{48,52},{56,60},{64,6... | collective-permute-start | bytes 1572872 | tf_op jit(solution)/shard_map/ppermute | solution.py:293
  2.0 12.1 %collective-permute-start.5 = (bf16[4,4,128,128]{3,2,1,0:T(8,128)(2,1)S(1)}, bf16[4,4,128,128]{3,2,1,0:T(8,128)(2,1)S(1)}, u32[]{:S(2)}, u32[]{:S(2)}) collective-permute-start(bf16[4,4,128,128]{3,2,1,0:T(8,128)(2,1)S(1)} %get-tuple-element.41), channel_id=1, source_target_pairs={{4,8},{12,16},{20,24},{28,32},{36,40},{44,48},{52,56},{60,64},{68,... | collective-permute-start | bytes 1572872 | tf_op jit(solution)/shard_map/ppermute | solution.py:293
  14.1 9.6 %copy-start.6 = (bf16[128,1024]{1,0:T(8,128)(2,1)S(1)}, bf16[128,1024]{1,0:T(8,128)(2,1)}, u32[]{:S(2)}) copy-start(bf16[128,1024]{1,0:T(8,128)(2,1)} %get-tuple-element.30) | copy-start | bytes 786436
  19.4 15.1 %collective-permute-start.6 = (bf16[512,1024]{1,0:T(8,128)(2,1)}, bf16[512,1024]{1,0:T(8,128)(2,1)S(1)}, u32[]{:S(2)}, u32[]{:S(2)}) collective-permute-start(bf16[512,1024]{1,0:T(8,128)(2,1)} %get-tuple-element.46), channel_id=1, source_target_pairs={{0,4},{8,12},{16,20},{24,28},{32,36},{40,44},{48,52},{56,60},{64,6... | collective-permute-start | bytes 3145736 | tf_op jit(solution)/shard_map/ppermute | solution.py:293
  19.5 17.5 %collective-permute-start.7 = (bf16[512,1024]{1,0:T(8,128)(2,1)}, bf16[512,1024]{1,0:T(8,128)(2,1)S(1)}, u32[]{:S(2)}, u32[]{:S(2)}) collective-permute-start(bf16[512,1024]{1,0:T(8,128)(2,1)} %get-tuple-element.47), channel_id=1, source_target_pairs={{4,8},{12,16},{20,24},{28,32},{36,40},{44,48},{52,56},{60,64},{68,... | collective-permute-start | bytes 3145736 | tf_op jit(solution)/shard_map/ppermute | solution.py:293
  23.8 18.9 %collective-permute-start = (bf16[128,1024]{1,0:T(8,128)(2,1)S(1)}, bf16[128,1024]{1,0:T(8,128)(2,1)S(1)}, u32[]{:S(2)}, u32[]{:S(2)}) collective-permute-start(bf16[128,1024]{1,0:T(8,128)(2,1)S(1)} %copy-done.6), channel_id=1, source_target_pairs={{0,2},{1,3},{2,0},{3,1},{4,6},{5,7},{6,4},{7,5},{8,10},{9,11},{10,... | collective-permute-start | bytes 786440 | tf_op jit(solution)/shard_map/ppermute | solution.py:297
  34.4 7.4 %copy-start.5 = (bf16[128,1024]{1,0:T(8,128)(2,1)S(1)}, bf16[128,1024]{1,0:T(8,128)(2,1)}, u32[]{:S(2)}) copy-start(bf16[128,1024]{1,0:T(8,128)(2,1)} %get-tuple-element.31) | copy-start | bytes 786436
  34.4 8.3 %copy-start.4 = (bf16[128,1024]{1,0:T(8,128)(2,1)S(1)}, bf16[128,1024]{1,0:T(8,128)(2,1)}, u32[]{:S(2)}) copy-start(bf16[128,1024]{1,0:T(8,128)(2,1)} %get-tuple-element.32) | copy-start | bytes 786436
  34.5 30.4 %copy-start.1 = (bf16[128,1024]{1,0:T(8,128)(2,1)S(1)}, bf16[128,1024]{1,0:T(8,128)(2,1)}, u32[]{:S(2)}) copy-start(bf16[128,1024]{1,0:T(8,128)(2,1)} %get-tuple-element.29.refs_0_) | copy-start | bytes 786436
  38.1 32.9 %collective-permute-start.8 = (bf16[128,1536]{1,0:T(8,128)(2,1)}, bf16[128,1536]{1,0:T(8,128)(2,1)S(1)}, u32[]{:S(2)}, u32[]{:S(2)}) collective-permute-start(bf16[128,1536]{1,0:T(8,128)(2,1)} %get-tuple-element.49), channel_id=1, source_target_pairs={{0,2},{1,3},{2,0},{3,1},{4,6},{5,7},{6,4},{7,5},{8,10},{9,11},{10,... | collective-permute-start | bytes 1179656 | tf_op jit(solution)/shard_map/ppermute | solution.py:297
  41.0 30.1 %collective-permute-start.9 = (bf16[128,1536]{1,0:T(8,128)(2,1)}, bf16[128,1536]{1,0:T(8,128)(2,1)S(1)}, u32[]{:S(2)}, u32[]{:S(2)}) collective-permute-start(bf16[128,1536]{1,0:T(8,128)(2,1)} %get-tuple-element.50), channel_id=1, source_target_pairs={{0,1},{1,0},{2,3},{3,2},{4,5},{5,4},{6,7},{7,6},{8,9},{9,8},{10,11... | collective-permute-start | bytes 1179656 | tf_op jit(solution)/shard_map/ppermute | solution.py:297
  41.3 29.8 %collective-permute-start.10 = (bf16[128,1536]{1,0:T(8,128)(2,1)}, bf16[128,1536]{1,0:T(8,128)(2,1)S(1)}, u32[]{:S(2)}, u32[]{:S(2)}) collective-permute-start(bf16[128,1536]{1,0:T(8,128)(2,1)} %get-tuple-element.51), channel_id=1, source_target_pairs={{0,3},{1,2},{2,1},{3,0},{4,7},{5,6},{6,5},{7,4},{8,11},{9,10},{10,... | collective-permute-start | bytes 1179656 | tf_op jit(solution)/shard_map/ppermute | solution.py:297
  41.8 23.0 %collective-permute-start.1 = (bf16[128,1024]{1,0:T(8,128)(2,1)S(1)}, bf16[128,1024]{1,0:T(8,128)(2,1)S(1)}, u32[]{:S(2)}, u32[]{:S(2)}) collective-permute-start(bf16[128,1024]{1,0:T(8,128)(2,1)S(1)} %copy-done.5), channel_id=1, source_target_pairs={{0,1},{1,0},{2,3},{3,2},{4,5},{5,4},{6,7},{7,6},{8,9},{9,8},{10,11... | collective-permute-start | bytes 786440 | tf_op jit(solution)/shard_map/ppermute | solution.py:297
  42.7 22.2 %collective-permute-start.2 = (bf16[128,1024]{1,0:T(8,128)(2,1)S(1)}, bf16[128,1024]{1,0:T(8,128)(2,1)S(1)}, u32[]{:S(2)}, u32[]{:S(2)}) collective-permute-start(bf16[128,1024]{1,0:T(8,128)(2,1)S(1)} %copy-done.4), channel_id=1, source_target_pairs={{0,3},{1,2},{2,1},{3,0},{4,7},{5,6},{6,5},{7,4},{8,11},{9,10},{10,... | collective-permute-start | bytes 786440 | tf_op jit(solution)/shard_map/ppermute | solution.py:297
  65.0 7.4 %collective-permute-start.3 = (f32[128,512]{1,0:T(8,128)S(1)}, f32[128,512]{1,0:T(8,128)S(1)}, u32[]{:S(2)}, u32[]{:S(2)}) collective-permute-start(f32[128,512]{1,0:T(8,128)S(1)} %get-tuple-element.33), channel_id=1, source_target_pairs={{0,4},{4,8},{8,12},{12,16},{16,20},{20,24},{24,28},{28,32},{32,36}... | collective-permute-start | bytes 786440 | tf_op jit(solution)/shard_map/ppermute | solution.py:303
  69.1 8.9 %collective-permute-start.11 = (f32[128,512]{1,0:T(8,128)S(1)}, f32[128,512]{1,0:T(8,128)S(1)}, u32[]{:S(2)}, u32[]{:S(2)}) collective-permute-start(f32[128,512]{1,0:T(8,128)S(1)} %get-tuple-element.52), channel_id=1, source_target_pairs={{4,0},{8,4},{12,8},{16,12},{20,16},{24,20},{28,24},{32,28},{36,32}... | collective-permute-start | bytes 786440 | tf_op jit(solution)/shard_map/ppermute | solution.py:303
